TPU v7x, 32 devices: a whole 2x2x4 slice. The times are simulated.
32 devices in a mesh: readout: 8 (over y, x, core), frame: 4 (over z).
Axes of the slice: x: 2, y: 2, z: 4, core: 2. Of those that a mesh axis runs over, the one named last changes fastest.
Arguments:
- equilibrium: float32 [2, 8, 16, 128, 128], P(None, 'frame', 'readout'), may hold values from -6 to 6
- cotangent: float32 [2, 8, 16, 128, 128], P(None, 'frame', 'readout'), may hold values from -8 to 8
- sensitivity: float32 [2, 8, 16, 128, 128], P(None, None, 'readout'), may hold values from -1.5 to 1.5
- sampling: int32 [8, 8, 128, 128], P('frame'), may hold values 0 or 1
- weight_in: bfloat16 [24, 2, 3, 3, 3], replicated, may hold values from -0.875 to 0.875
- bias_in: float32 [24], replicated, may hold values from -4 to 4
- weight_mid: bfloat16 [24, 24, 3, 3, 3], replicated, may hold values from -0.25 to 0.25
- bias_mid: float32 [24], replicated, may hold values from -4 to 4
- weight_out: bfloat16 [2, 24, 3, 3, 3], replicated, may hold values from -0.25 to 0.25
Outputs:
- adjoint: float32 [2, 8, 16, 128, 128], P(None, 'frame', 'readout')
Inputs may be any that keep to these rules, and one draw needn't show every extreme that they name: `sampling`: 1 where the k-space sample is acquired for that frame and coil, else 0.
All inputs are finite; a program needn't handle non-finite values. No bound on the sum of `sampling` on one device may be relied on, other than what follows from the above.
Results may differ from a plain program's by a relative error of at most 0.0024.
Values may be sent and summed in bfloat16 or wider, within the bound.
No kernel may reach another device: no remote copies, remote signals or barrier semaphores. Data moves between devices by JAX's collectives and lax.ppermute only.
A program may use at most 128 MiB of HBM per device.

v0:
```python
import math

import jax
import jax.numpy as jnp
from jax import lax
from jax.sharding import PartitionSpec as P

ITERS = 2
DEPTH = 5


ETA = 0.5
RIDGE = 0.0001


def padded_2(cells, sides, width):
    for axis, dim in sides:
        count = lax.axis_size(axis)
        ends = count - 1
        head = lax.slice_in_dim(cells, 0, width, axis=dim)
        tail = lax.slice_in_dim(cells, cells.shape[dim] - width, cells.shape[dim], axis=dim)
        cells = jnp.concatenate(
            [
                lax.ppermute(tail, axis, [(i, (i + 1) % count) for i in range(ends)]),
                cells,
                lax.ppermute(head, axis, [((i + 1) % count, i) for i in range(ends)]),
            ],
            axis=dim,
        )
    return cells


def from_behind(block, axis, distance):
    devices = range(lax.axis_size(axis))
    route = [(i - distance, i) for i in devices if i - distance in devices]
    return lax.ppermute(block, axis, route)


def correlate(padded, kernel):
    return lax.conv_general_dilated(
        padded,
        kernel,
        (1, 1, 1),
        "VALID",
        dimension_numbers=("CTXYN", "OITXY", "CTXYN"),
        preferred_element_type=jnp.float32,
    )


def pad_plane(field):
    return jnp.pad(field, ((0, 0), (0, 0), (0, 0), (1, 1), (0, 0)))


def flip_kernel(weight):
    return jnp.transpose(jnp.flip(weight, (2, 3, 4)), (1, 0, 2, 3, 4))


def silu_slope(value):
    sigma = jax.nn.sigmoid(value)
    return sigma * (1.0 + value * (1.0 - sigma))


def dft_tables(length):
    index = jnp.arange(length, dtype=jnp.int32)
    product = index[:, None] * index[None, :] % length
    angle = 2.0 * math.pi / length * product.astype(jnp.float32)
    scale = 1.0 / math.sqrt(length)
    return (jnp.cos(angle) * scale, jnp.sin(angle) * scale)


def left_blocks(tables, sign):
    cosine, sine = tables
    top = jnp.stack([cosine, sign * sine], axis=1)
    bottom = jnp.stack([-sign * sine, cosine], axis=1)
    return jnp.stack([top, bottom], axis=0)


def right_blocks(tables, sign):
    cosine, sine = tables
    from_real = jnp.stack([cosine, -sign * sine], axis=1)
    from_imag = jnp.stack([sign * sine, cosine], axis=1)
    return jnp.stack([from_real, from_imag], axis=0)


def transform(stacked, block_y, block_z):
    middle = jnp.einsum("pkqy,qcfxyz->pcfxkz", block_y, stacked, precision=lax.Precision.HIGHEST)
    return jnp.einsum("qcfxyz,qzpk->pcfxyk", middle, block_z, precision=lax.Precision.HIGHEST)


def small_solve(matrix, target):
    order = target.shape[0]
    lines = [matrix[index] for index in range(order)]
    values = [target[index] for index in range(order)]
    for column in range(order):
        for line in range(column + 1, order):
            factor = lines[line][column] / lines[column][column]
            lines[line] = lines[line] - factor * lines[column]
            values[line] = values[line] - factor * values[column]
    solution = [None] * order
    for line in reversed(range(order)):
        running = values[line]
        for column in range(line + 1, order):
            running = running - lines[line][column] * solution[column]
        solution[line] = running / lines[line][line]
    return jnp.stack(solution)


def per_device(
    equilibrium,
    cotangent,
    sensitivity,
    sampling,
    weight_in,
    bias_in,
    weight_mid,
    bias_mid,
    weight_out,
):
    start_image = equilibrium.astype(jnp.bfloat16)
    padded = padded_2(start_image, (("readout", 2), ("frame", 1)), 1)
    pre_one = correlate(pad_plane(padded), weight_in) + bias_in[:, None, None, None, None]
    hidden = jax.nn.silu(pre_one).astype(jnp.bfloat16)
    slope_one = silu_slope(pre_one).astype(jnp.bfloat16)
    padded = padded_2(hidden, (("readout", 2), ("frame", 1)), 1)
    pre_two = correlate(pad_plane(padded), weight_mid) + bias_mid[:, None, None, None, None]
    slope_two = silu_slope(pre_two).astype(jnp.bfloat16)
    back_out = flip_kernel(weight_out)
    back_mid = flip_kernel(weight_mid)
    back_in = flip_kernel(weight_in)
    tables_y = dft_tables(sensitivity.shape[3])
    tables_z = dft_tables(sensitivity.shape[4])
    forward_y = left_blocks(tables_y, 1.0)
    forward_z = right_blocks(tables_z, 1.0)
    inverse_y = left_blocks(tables_y, -1.0)
    inverse_z = right_blocks(tables_z, -1.0)
    sens_real = sensitivity[0][:, None]
    sens_imag = sensitivity[1][:, None]
    mask_block = jnp.transpose(sampling, (1, 0, 2, 3))[:, :, None].astype(jnp.float32)
    current = cotangent
    mapped_list = []
    residuals = []
    gram = {}
    for step in range(ITERS):
        field_real = current[0][None]
        field_imag = current[1][None]
        coil_real = sens_real * field_real - sens_imag * field_imag
        coil_imag = sens_real * field_imag + sens_imag * field_real
        kspace = transform(jnp.stack([coil_real, coil_imag]), forward_y, forward_z)
        images = transform(kspace * mask_block[None], inverse_y, inverse_z)
        back_real = images[0]
        back_imag = images[1]
        total_real = jnp.sum(sens_real * back_real + sens_imag * back_imag, axis=0)
        total_imag = jnp.sum(sens_real * back_imag - sens_imag * back_real, axis=0)
        rounded = current.astype(jnp.bfloat16)
        padded_in = padded_2(rounded, (("readout", 2), ("frame", 1)), 1)
        grad_two = (slope_two * correlate(pad_plane(padded_in), back_out)).astype(jnp.bfloat16)
        padded_mid = padded_2(grad_two, (("readout", 2), ("frame", 1)), 1)
        grad_one = (slope_one * correlate(pad_plane(padded_mid), back_mid)).astype(jnp.bfloat16)
        spread = jnp.pad(grad_one, ((0, 0), (2, 2), (2, 2), (1, 1), (0, 0)))
        full = correlate(spread, back_in)
        frames = full.shape[1] - 2
        width = full.shape[2] - 2
        from_next = from_behind(full[:, :, :1], "readout", -1)
        from_prev = from_behind(full[:, :, -1:], "readout", 1)
        middle = full[:, :, 1:-1]
        middle = middle + jnp.pad(from_next, ((0, 0), (0, 0), (width - 1, 0), (0, 0), (0, 0)))
        middle = middle + jnp.pad(from_prev, ((0, 0), (0, 0), (0, width - 1), (0, 0), (0, 0)))
        next_frames = from_behind(middle[:, :1], "frame", -1)
        prev_frames = from_behind(middle[:, -1:], "frame", 1)
        result = middle[:, 1:-1]
        result = result + jnp.pad(next_frames, ((0, 0), (frames - 1, 0), (0, 0), (0, 0), (0, 0)))
        result = result + jnp.pad(prev_frames, ((0, 0), (0, frames - 1), (0, 0), (0, 0), (0, 0)))
        mapped = cotangent + current - ETA * jnp.stack([total_real, total_imag]) - result
        residual = mapped - current
        mapped_list.append(mapped)
        residuals.append(residual)
        first = max(0, step + 1 - DEPTH)
        window = list(range(first, step + 1))
        partial_value = jnp.stack([jnp.sum(residual * residuals[older]) for older in window])
        summed = lax.psum(partial_value, ("readout", "frame"))
        for position in range(len(window)):
            gram[step, window[position]] = summed[position]
        count = len(window)
        if count == 1:
            current = mapped
        else:
            matrix = jnp.stack(
                [
                    jnp.stack([gram[max(left, right), min(left, right)] for right in window])
                    for left in window
                ]
            )
            ridge = RIDGE * jnp.trace(matrix) / count
            matrix = matrix + ridge * jnp.eye(count, dtype=matrix.dtype)
            solution = small_solve(matrix, jnp.ones((count,), matrix.dtype))
            alpha = solution / jnp.sum(solution)
            current = alpha[0] * mapped_list[window[0]]
            position = 1
            current = current + alpha[position] * mapped_list[window[position]]
    return current


def solution(mesh):
    placed = (
        P(None, "frame", "readout", None, None),
        P(None, "frame", "readout", None, None),
        P(None, None, "readout", None, None),
        P("frame", None, None, None),
        P(),
        P(),
        P(),
        P(),
        P(),
    )
    return jax.shard_map(
        per_device,
        mesh=mesh,
        in_specs=placed,
        out_specs=P(None, "frame", "readout", None, None),
        check_vma=False,
    )
```

profile of v0, /device:TPU:0, one launch (start us, length us, event | category | flops | bytes accessed | tf_op | source)
XLA Modules:
  0.0 614.0 jit_solution(6043110645983785388)
XLA Ops:
  18.2 4.7 collective-permute-done.3
  22.9 6.7 %multiply_convert_fusion.1 = (bf16[24,2,2,128,128]{4,0,3,2,1:T(8,128)(2,1)S(1)}, f32[24,2,2,128,128]{4,0,3,2,1:T(8,128)}) fusion(f32[24]{0:T(128)} %param.14, bf16[24,2,3,3,3]{0,1,4,3,2:T(2,128)(2,1)} %param.13, bf16[2,1,4,128,128]{4,0,3,2,1:T(2,128)(2,1)S(1)} %collective-permute-done.3, bf16[2,2,1,128,128]{4,0,3,2,1:T(2,128)(2,1)S(1)} %collective-permute-done.1, ...), kind=kOutput, calls=%fused_computation.42 | convolution fusion | flops 183664640 | bytes 10488448 | tf_op jit(solution)/shard_map/conv_general_dilated | solution.py:40
  30.1 4.1 collective-permute-start.4
  49.1 34.8 %collective-permute-start.8 = (bf16[2,2,1,128,128]{4,0,3,2,1:T(2,128)(2,1)S(1)}, bf16[2,2,1,128,128]{4,0,3,2,1:T(2,128)(2,1)S(1)}, u32[]{:S(2)}, u32[]{:S(2)}) collective-permute-start(bf16[2,2,1,128,128]{4,0,3,2,1:T(2,128)(2,1)S(1)} %get-tuple-element.55), channel_id=1, source_target_pairs={{0,4},{4,8},{8,12},{12,16},{16,20},{20,24},{24,28},{1,5},{5,9},{9,... | collective-permute-start | bytes 393224 | tf_op jit(solution)/shard_map/ppermute | solution.py:24
  88.3 4.3 collective-permute-start.10
  94.2 11.9 %multiply_convert_fusion = bf16[24,2,2,128,128]{4,0,3,2,1:T(8,128)(2,1)S(1)} fusion(f32[24]{0:T(128)S(1)} %copy-done.42, bf16[24,24,3,3,3]{1,0,4,3,2:T(8,128)(2,1)S(1)} %copy-done, bf16[24,1,4,128,128]{4,0,3,2,1:T(8,128)(2,1)S(1)} %collective-permute-done.7, bf16[24,2,1,128,128]{4,0,3,2,1:T(8,128)(2,1)S(1)} %collective-permute-done.5, ...), kind=kOutput, calls=%fused_computation.41 | convolution fusion | flops 2104885248 | bytes 15759840 | tf_op jit(solution)/shard_map/conv_general_dilated | solution.py:40
  106.1 4.3 fusion.32
  111.0 30.5 %collective-permute-start.12 = (bf16[24,2,1,128,128]{4,0,3,2,1:T(8,128)(2,1)S(1)}, bf16[24,2,1,128,128]{4,0,3,2,1:T(8,128)(2,1)S(1)}, u32[]{:S(2)}, u32[]{:S(2)}) collective-permute-start(bf16[24,2,1,128,128]{4,0,3,2,1:T(8,128)(2,1)S(1)} %get-tuple-element.25), channel_id=1, source_target_pairs={{0,4},{4,8},{8,12},{12,16},{16,20},{20,24},{24,28},{1,5},{5,9},{9,... | collective-permute-start | bytes 4718600 | tf_op jit(solution)/shard_map/ppermute | solution.py:24
  144.5 31.9 %collective-permute-done.13 = bf16[24,2,1,128,128]{4,0,3,2,1:T(8,128)(2,1)S(1)} collective-permute-done((bf16[24,2,1,128,128]{4,0,3,2,1:T(8,128)(2,1)S(1)}, bf16[24,2,1,128,128]{4,0,3,2,1:T(8,128)(2,1)S(1)}, u32[]{:S(2)}, u32[]{:S(2)}) %collective-permute-start.13) | collective-permute-done | bytes 1572896 | tf_op jit(solution)/shard_map/ppermute | solution.py:26
  181.7 5.0 collective-permute-start.14
  205.3 6.1 fusion.47
  211.5 16.1 %collective-permute-done.14 = bf16[24,1,4,128,128]{4,0,3,2,1:T(8,128)(2,1)} collective-permute-done((bf16[24,1,4,128,128]{4,0,3,2,1:T(8,128)(2,1)}, bf16[24,1,4,128,128]{4,0,3,2,1:T(8,128)(2,1)}, u32[]{:S(2)}, u32[]{:S(2)}) %collective-permute-start.14) | collective-permute-done | bytes 3145760 | tf_op jit(solution)/shard_map/ppermute | solution.py:24
  227.6 6.4 %collective-permute-done.15 = bf16[24,1,4,128,128]{4,0,3,2,1:T(8,128)(2,1)} collective-permute-done((bf16[24,1,4,128,128]{4,0,3,2,1:T(8,128)(2,1)}, bf16[24,1,4,128,128]{4,0,3,2,1:T(8,128)(2,1)}, u32[]{:S(2)}, u32[]{:S(2)}) %collective-permute-start.15) | collective-permute-done | bytes 3145760 | tf_op jit(solution)/shard_map/ppermute | solution.py:26
  234.0 14.6 %fusion.10 = f32[24,2,2,128,128]{4,0,3,2,1:T(8,128)} fusion(bf16[24,24,3,3,3]{1,0,4,3,2:T(8,128)(2,1)S(1)} %copy-done, bf16[24,1,4,128,128]{4,0,3,2,1:T(8,128)(2,1)} %collective-permute-done.15, bf16[24,2,1,128,128]{4,0,3,2,1:T(8,128)(2,1)S(1)} %copy-done.34, bf16[24,2,2,128,128]{4,0,3,2,1:T(8,128)(2,1)S(1)} %copy-done.12, ...), kind=kOutput, calls=%fused_computation.10 | convolution fusion | flops 2090729472 | bytes 18905472 | tf_op jit(solution)/shard_map/conv_general_dilated | solution.py:40
  248.6 25.2 %fusion.56 = f32[2,4,4,128,128]{4,0,3,2,1:T(2,128)S(1)} fusion(bf16[24,2,3,3,3]{0,1,4,3,2:T(2,128)(2,1)S(1)} %copy-done.41, f32[24,2,2,128,128]{4,0,3,2,1:T(8,128)} %fusion.10, f32[24,2,2,128,128]{4,0,3,2,1:T(8,128)S(1)} %bitcast.176, f32[24]{0:T(128)S(1)} %copy-done.43), kind=kOutput, calls=%fused_computation.70 | convolution fusion | flops 187858944 | bytes 14682752 | tf_op jit(solution)/shard_map/conv_general_dilated | solution.py:40
  275.5 28.6 %collective-permute-start.17 = (f32[2,4,1,128,128]{4,3,2,1,0:T(8,128)S(1)}, f32[2,4,1,128,128]{4,3,2,1,0:T(8,128)S(1)}, u32[]{:S(2)}, u32[]{:S(2)}) collective-permute-start(f32[2,4,1,128,128]{4,3,2,1,0:T(8,128)S(1)} %copy.108), channel_id=1, source_target_pairs={{0,4},{4,8},{8,12},{12,16},{16,20},{20,24},{24,28},{1,5},{5,9},{9,... | collective-permute-start | bytes 1572872 | tf_op jit(solution)/shard_map/ppermute | solution.py:36
  304.2 4.7 fusion.52
  317.4 5.3 collective-permute-start.19
  327.8 20.5 %collective-permute-start.20 = (bf16[2,2,1,128,128]{4,3,2,1,0:T(8,128)(2,1)S(1)}, bf16[2,2,1,128,128]{4,3,2,1,0:T(8,128)(2,1)S(1)}, u32[]{:S(2)}, u32[]{:S(2)}) collective-permute-start(bf16[2,2,1,128,128]{4,3,2,1,0:T(8,128)(2,1)S(1)} %get-tuple-element.53), channel_id=1, source_target_pairs={{0,4},{4,8},{8,12},{12,16},{16,20},{20,24},{24,28},{1,5},{5,9},{9,... | collective-permute-start | bytes 393224 | tf_op jit(solution)/shard_map/ppermute | solution.py:24
  349.6 5.4 collective-permute-done.21
  355.2 4.4 collective-permute-start.22
  363.7 4.7 collective-permute-done.23
  368.5 4.4 fusion.33
  400.4 6.1 fusion.42
  406.5 24.6 %collective-permute-done.26 = bf16[24,1,4,128,128]{4,0,3,2,1:T(8,128)(2,1)} collective-permute-done((bf16[24,1,4,128,128]{4,0,3,2,1:T(8,128)(2,1)}, bf16[24,1,4,128,128]{4,0,3,2,1:T(8,128)(2,1)}, u32[]{:S(2)}, u32[]{:S(2)}) %collective-permute-start.26) | collective-permute-done | bytes 3145760 | tf_op jit(solution)/shard_map/ppermute | solution.py:24
  431.1 6.3 %collective-permute-done.27 = bf16[24,1,4,128,128]{4,0,3,2,1:T(8,128)(2,1)} collective-permute-done((bf16[24,1,4,128,128]{4,0,3,2,1:T(8,128)(2,1)}, bf16[24,1,4,128,128]{4,0,3,2,1:T(8,128)(2,1)}, u32[]{:S(2)}, u32[]{:S(2)}) %collective-permute-start.27) | collective-permute-done | bytes 3145760 | tf_op jit(solution)/shard_map/ppermute | solution.py:26
  437.5 14.6 %fusion.20 = f32[24,2,2,128,128]{4,0,3,2,1:T(8,128)} fusion(bf16[24,24,3,3,3]{1,0,4,3,2:T(8,128)(2,1)S(1)} %copy-done, bf16[24,1,4,128,128]{4,0,3,2,1:T(8,128)(2,1)} %collective-permute-done.27, bf16[24,2,1,128,128]{4,0,3,2,1:T(8,128)(2,1)S(1)} %copy-done.38, bf16[24,2,2,128,128]{4,0,3,2,1:T(8,128)(2,1)S(1)} %copy-done.14, ...), kind=kOutput, calls=%fused_computation.20 | convolution fusion | flops 2090729472 | bytes 18905472 | tf_op jit(solution)/shard_map/conv_general_dilated | solution.py:40
  452.1 25.2 %fusion.54 = f32[2,4,4,128,128]{4,0,3,2,1:T(2,128)S(1)} fusion(bf16[24,2,3,3,3]{0,1,4,3,2:T(2,128)(2,1)S(1)} %copy-done.41, f32[24,2,2,128,128]{4,0,3,2,1:T(8,128)} %fusion.20, f32[24,2,2,128,128]{4,0,3,2,1:T(8,128)S(1)} %bitcast.178, f32[24]{0:T(128)S(1)} %copy-done.43), kind=kOutput, calls=%fused_computation.69 | convolution fusion | flops 187858944 | bytes 14682752 | tf_op jit(solution)/shard_map/conv_general_dilated | solution.py:40
  479.0 32.7 %collective-permute-start.29 = (f32[2,4,1,128,128]{4,3,2,1,0:T(8,128)S(1)}, f32[2,4,1,128,128]{4,3,2,1,0:T(8,128)S(1)}, u32[]{:S(2)}, u32[]{:S(2)}) collective-permute-start(f32[2,4,1,128,128]{4,3,2,1,0:T(8,128)S(1)} %copy.111), channel_id=1, source_target_pairs={{0,4},{4,8},{8,12},{12,16},{16,20},{20,24},{24,28},{1,5},{5,9},{9,... | collective-permute-start | bytes 1572872 | tf_op jit(solution)/shard_map/ppermute | solution.py:36
  511.7 4.7 fusion.50
  522.8 5.3 collective-permute-start.31
  534.8 69.6 %all-reduce.8 = (f32[2]{0:T(128)S(1)}, f32[1]{0:T(128)}) all-reduce(f32[2]{0:T(128)S(1)} %pad_maximum_fusion.12, f32[1]{0:T(128)} %bitcast.37), channel_id=1, replica_groups=mesh['readout'=8,'frame'=4] {'readout','frame'}, use_global_device_ids=true, to_apply=%region_8.9 | all-reduce | flops 3 | bytes 24 | tf_op jit(solution)/shard_map/psum | solution.py:180
  (220 shorter events, 134.9 us)
Async XLA Ops:
  1.7 3.7 collective-permute-start
  4.1 5.3 collective-permute-start.1
  10.6 7.6 %collective-permute-start.2 = (bf16[2,1,4,128,128]{4,0,3,2,1:T(2,128)(2,1)S(1)}, bf16[2,1,4,128,128]{4,0,3,2,1:T(2,128)(2,1)S(1)}, u32[]{:S(2)}, u32[]{:S(2)}) collective-permute-start(bf16[2,1,4,128,128]{4,0,3,2,1:T(2,128)(2,1)S(1)} %get-tuple-element.51), channel_id=1, source_target_pairs={{0,1},{1,2},{2,3},{4,5},{5,6},{6,7},{8,9},{9,10},{10,11},{12,13},{... | collective-permute-start | bytes 786440 | tf_op jit(solution)/shard_map/ppermute | solution.py:24
  14.1 8.8 %collective-permute-start.3 = (bf16[2,1,4,128,128]{4,0,3,2,1:T(2,128)(2,1)S(1)}, bf16[2,1,4,128,128]{4,0,3,2,1:T(2,128)(2,1)S(1)}, u32[]{:S(2)}, u32[]{:S(2)}) collective-permute-start(bf16[2,1,4,128,128]{4,0,3,2,1:T(2,128)(2,1)S(1)} %get-tuple-element.52), channel_id=1, source_target_pairs={{1,0},{2,1},{3,2},{5,4},{6,5},{7,6},{9,8},{10,9},{11,10},{13,12},{... | collective-permute-start | bytes 786440 | tf_op jit(solution)/shard_map/ppermute | solution.py:26
  30.1 7.0 %collective-permute-start.4 = (bf16[24,2,1,128,128]{4,0,3,2,1:T(8,128)(2,1)S(1)}, bf16[24,2,1,128,128]{4,0,3,2,1:T(8,128)(2,1)S(1)}, u32[]{:S(2)}, u32[]{:S(2)}) collective-permute-start(bf16[24,2,1,128,128]{4,0,3,2,1:T(8,128)(2,1)S(1)} %get-tuple-element.27), channel_id=1, source_target_pairs={{0,4},{4,8},{8,12},{12,16},{16,20},{20,24},{24,28},{1,5},{5,9},{9,... | collective-permute-start | bytes 4718600 | tf_op jit(solution)/shard_map/ppermute | solution.py:24
  34.2 6.9 %collective-permute-start.5 = (bf16[24,2,1,128,128]{4,0,3,2,1:T(8,128)(2,1)S(1)}, bf16[24,2,1,128,128]{4,0,3,2,1:T(8,128)(2,1)S(1)}, u32[]{:S(2)}, u32[]{:S(2)}) collective-permute-start(bf16[24,2,1,128,128]{4,0,3,2,1:T(8,128)(2,1)S(1)} %get-tuple-element.28), channel_id=1, source_target_pairs={{4,0},{8,4},{12,8},{16,12},{20,16},{24,20},{28,24},{5,1},{9,5},{13... | collective-permute-start | bytes 4718600 | tf_op jit(solution)/shard_map/ppermute | solution.py:26
  43.5 50.6 %collective-permute-start.6 = (bf16[24,1,4,128,128]{4,0,3,2,1:T(8,128)(2,1)S(1)}, bf16[24,1,4,128,128]{4,0,3,2,1:T(8,128)(2,1)S(1)}, u32[]{:S(2)}, u32[]{:S(2)}) collective-permute-start(bf16[24,1,4,128,128]{4,0,3,2,1:T(8,128)(2,1)S(1)} %get-tuple-element.21), channel_id=1, source_target_pairs={{0,1},{1,2},{2,3},{4,5},{5,6},{6,7},{8,9},{9,10},{10,11},{12,13},{... | collective-permute-start | bytes 9437192 | tf_op jit(solution)/shard_map/ppermute | solution.py:24
  47.2 46.9 %collective-permute-start.7 = (bf16[24,1,4,128,128]{4,0,3,2,1:T(8,128)(2,1)S(1)}, bf16[24,1,4,128,128]{4,0,3,2,1:T(8,128)(2,1)S(1)}, u32[]{:S(2)}, u32[]{:S(2)}) collective-permute-start(bf16[24,1,4,128,128]{4,0,3,2,1:T(8,128)(2,1)S(1)} %get-tuple-element.22), channel_id=1, source_target_pairs={{1,0},{2,1},{3,2},{5,4},{6,5},{7,6},{9,8},{10,9},{11,10},{13,12},{... | collective-permute-start | bytes 9437192 | tf_op jit(solution)/shard_map/ppermute | solution.py:26
  49.1 36.1 %collective-permute-start.8 = (bf16[2,2,1,128,128]{4,0,3,2,1:T(2,128)(2,1)S(1)}, bf16[2,2,1,128,128]{4,0,3,2,1:T(2,128)(2,1)S(1)}, u32[]{:S(2)}, u32[]{:S(2)}) collective-permute-start(bf16[2,2,1,128,128]{4,0,3,2,1:T(2,128)(2,1)S(1)} %get-tuple-element.55), channel_id=1, source_target_pairs={{0,4},{4,8},{8,12},{12,16},{16,20},{20,24},{24,28},{1,5},{5,9},{9,... | collective-permute-start | bytes 393224 | tf_op jit(solution)/shard_map/ppermute | solution.py:24
  83.9 3.2 collective-permute-start.9
  88.3 17.8 %collective-permute-start.10 = (bf16[2,1,4,128,128]{4,0,3,2,1:T(2,128)(2,1)S(1)}, bf16[2,1,4,128,128]{4,0,3,2,1:T(2,128)(2,1)S(1)}, u32[]{:S(2)}, u32[]{:S(2)}) collective-permute-start(bf16[2,1,4,128,128]{4,0,3,2,1:T(2,128)(2,1)S(1)} %get-tuple-element.49), channel_id=1, source_target_pairs={{0,1},{1,2},{2,3},{4,5},{5,6},{6,7},{8,9},{9,10},{10,11},{12,13},{... | collective-permute-start | bytes 786440 | tf_op jit(solution)/shard_map/ppermute | solution.py:24
  92.6 13.5 %collective-permute-start.11 = (bf16[2,1,4,128,128]{4,0,3,2,1:T(2,128)(2,1)S(1)}, bf16[2,1,4,128,128]{4,0,3,2,1:T(2,128)(2,1)S(1)}, u32[]{:S(2)}, u32[]{:S(2)}) collective-permute-start(bf16[2,1,4,128,128]{4,0,3,2,1:T(2,128)(2,1)S(1)} %get-tuple-element.50), channel_id=1, source_target_pairs={{1,0},{2,1},{3,2},{5,4},{6,5},{7,6},{9,8},{10,9},{11,10},{13,12},{... | collective-permute-start | bytes 786440 | tf_op jit(solution)/shard_map/ppermute | solution.py:26
  111.0 33.4 %collective-permute-start.12 = (bf16[24,2,1,128,128]{4,0,3,2,1:T(8,128)(2,1)S(1)}, bf16[24,2,1,128,128]{4,0,3,2,1:T(8,128)(2,1)S(1)}, u32[]{:S(2)}, u32[]{:S(2)}) collective-permute-start(bf16[24,2,1,128,128]{4,0,3,2,1:T(8,128)(2,1)S(1)} %get-tuple-element.25), channel_id=1, source_target_pairs={{0,4},{4,8},{8,12},{12,16},{16,20},{20,24},{24,28},{1,5},{5,9},{9,... | collective-permute-start | bytes 4718600 | tf_op jit(solution)/shard_map/ppermute | solution.py:24
  141.6 34.8 %collective-permute-start.13 = (bf16[24,2,1,128,128]{4,0,3,2,1:T(8,128)(2,1)S(1)}, bf16[24,2,1,128,128]{4,0,3,2,1:T(8,128)(2,1)S(1)}, u32[]{:S(2)}, u32[]{:S(2)}) collective-permute-start(bf16[24,2,1,128,128]{4,0,3,2,1:T(8,128)(2,1)S(1)} %get-tuple-element.26), channel_id=1, source_target_pairs={{4,0},{8,4},{12,8},{16,12},{20,16},{24,20},{28,24},{5,1},{9,5},{13... | collective-permute-start | bytes 4718600 | tf_op jit(solution)/shard_map/ppermute | solution.py:26
  181.7 45.8 %collective-permute-start.14 = (bf16[24,1,4,128,128]{4,0,3,2,1:T(8,128)(2,1)}, bf16[24,1,4,128,128]{4,0,3,2,1:T(8,128)(2,1)}, u32[]{:S(2)}, u32[]{:S(2)}) collective-permute-start(bf16[24,1,4,128,128]{4,0,3,2,1:T(8,128)(2,1)} %get-tuple-element.19), channel_id=1, source_target_pairs={{0,1},{1,2},{2,3},{4,5},{5,6},{6,7},{8,9},{9,10},{10,11},{12,13},{... | collective-permute-start | bytes 9437192 | tf_op jit(solution)/shard_map/ppermute | solution.py:24
  186.8 47.2 %collective-permute-start.15 = (bf16[24,1,4,128,128]{4,0,3,2,1:T(8,128)(2,1)}, bf16[24,1,4,128,128]{4,0,3,2,1:T(8,128)(2,1)}, u32[]{:S(2)}, u32[]{:S(2)}) collective-permute-start(bf16[24,1,4,128,128]{4,0,3,2,1:T(8,128)(2,1)} %get-tuple-element.20), channel_id=1, source_target_pairs={{1,0},{2,1},{3,2},{5,4},{6,5},{7,6},{9,8},{10,9},{11,10},{13,12},{... | collective-permute-start | bytes 9437192 | tf_op jit(solution)/shard_map/ppermute | solution.py:26
  273.9 38.9 %collective-permute-start.16 = (f32[2,4,1,128,128]{4,3,2,1,0:T(8,128)S(1)}, f32[2,4,1,128,128]{4,3,2,1,0:T(8,128)S(1)}, u32[]{:S(2)}, u32[]{:S(2)}) collective-permute-start(f32[2,4,1,128,128]{4,3,2,1,0:T(8,128)S(1)} %copy.107), channel_id=1, source_target_pairs={{4,0},{8,4},{12,8},{16,12},{20,16},{24,20},{28,24},{5,1},{9,5},{13... | collective-permute-start | bytes 1572872 | tf_op jit(solution)/shard_map/ppermute | solution.py:36
  275.5 37.3 %collective-permute-start.17 = (f32[2,4,1,128,128]{4,3,2,1,0:T(8,128)S(1)}, f32[2,4,1,128,128]{4,3,2,1,0:T(8,128)S(1)}, u32[]{:S(2)}, u32[]{:S(2)}) collective-permute-start(f32[2,4,1,128,128]{4,3,2,1,0:T(8,128)S(1)} %copy.108), channel_id=1, source_target_pairs={{0,4},{4,8},{8,12},{12,16},{16,20},{20,24},{24,28},{1,5},{5,9},{9,... | collective-permute-start | bytes 1572872 | tf_op jit(solution)/shard_map/ppermute | solution.py:36
  316.0 9.4 %collective-permute-start.18 = (f32[2,1,2,128,128]{4,3,2,1,0:T(8,128)}, f32[2,1,2,128,128]{4,3,2,1,0:T(8,128)}, u32[]{:S(2)}, u32[]{:S(2)}) collective-permute-start(f32[2,1,2,128,128]{4,3,2,1,0:T(8,128)} %get-tuple-element.41), channel_id=1, source_target_pairs={{1,0},{2,1},{3,2},{5,4},{6,5},{7,6},{9,8},{10,9},{11,10},{13,12},{... | collective-permute-start | bytes 786440 | tf_op jit(solution)/shard_map/ppermute | solution.py:36
  317.4 8.7 %collective-permute-start.19 = (f32[2,1,2,128,128]{4,3,2,1,0:T(8,128)}, f32[2,1,2,128,128]{4,3,2,1,0:T(8,128)}, u32[]{:S(2)}, u32[]{:S(2)}) collective-permute-start(f32[2,1,2,128,128]{4,3,2,1,0:T(8,128)} %get-tuple-element.42), channel_id=1, source_target_pairs={{0,1},{1,2},{2,3},{4,5},{5,6},{6,7},{8,9},{9,10},{10,11},{12,13},{... | collective-permute-start | bytes 786440 | tf_op jit(solution)/shard_map/ppermute | solution.py:36
  327.8 21.8 %collective-permute-start.20 = (bf16[2,2,1,128,128]{4,3,2,1,0:T(8,128)(2,1)S(1)}, bf16[2,2,1,128,128]{4,3,2,1,0:T(8,128)(2,1)S(1)}, u32[]{:S(2)}, u32[]{:S(2)}) collective-permute-start(bf16[2,2,1,128,128]{4,3,2,1,0:T(8,128)(2,1)S(1)} %get-tuple-element.53), channel_id=1, source_target_pairs={{0,4},{4,8},{8,12},{12,16},{16,20},{20,24},{24,28},{1,5},{5,9},{9,... | collective-permute-start | bytes 393224 | tf_op jit(solution)/shard_map/ppermute | solution.py:24
  348.3 6.7 %collective-permute-start.21 = (bf16[2,2,1,128,128]{4,3,2,1,0:T(8,128)(2,1)S(1)}, bf16[2,2,1,128,128]{4,3,2,1,0:T(8,128)(2,1)S(1)}, u32[]{:S(2)}, u32[]{:S(2)}) collective-permute-start(bf16[2,2,1,128,128]{4,3,2,1,0:T(8,128)(2,1)S(1)} %get-tuple-element.54), channel_id=1, source_target_pairs={{4,0},{8,4},{12,8},{16,12},{20,16},{24,20},{28,24},{5,1},{9,5},{13... | collective-permute-start | bytes 393224 | tf_op jit(solution)/shard_map/ppermute | solution.py:26
  355.2 8.5 %collective-permute-start.22 = (bf16[2,1,4,128,128]{4,3,2,1,0:T(8,128)(2,1)S(1)}, bf16[2,1,4,128,128]{4,3,2,1,0:T(8,128)(2,1)S(1)}, u32[]{:S(2)}, u32[]{:S(2)}) collective-permute-start(bf16[2,1,4,128,128]{4,3,2,1,0:T(8,128)(2,1)S(1)} %get-tuple-element.45), channel_id=1, source_target_pairs={{0,1},{1,2},{2,3},{4,5},{5,6},{6,7},{8,9},{9,10},{10,11},{12,13},{... | collective-permute-start | bytes 786440 | tf_op jit(solution)/shard_map/ppermute | solution.py:24
  359.6 8.8 %collective-permute-start.23 = (bf16[2,1,4,128,128]{4,3,2,1,0:T(8,128)(2,1)S(1)}, bf16[2,1,4,128,128]{4,3,2,1,0:T(8,128)(2,1)S(1)}, u32[]{:S(2)}, u32[]{:S(2)}) collective-permute-start(bf16[2,1,4,128,128]{4,3,2,1,0:T(8,128)(2,1)S(1)} %get-tuple-element.46), channel_id=1, source_target_pairs={{1,0},{2,1},{3,2},{5,4},{6,5},{7,6},{9,8},{10,9},{11,10},{13,12},{... | collective-permute-start | bytes 786440 | tf_op jit(solution)/shard_map/ppermute | solution.py:26
  373.4 7.0 %collective-permute-start.24 = (bf16[24,2,1,128,128]{4,0,3,2,1:T(8,128)(2,1)S(1)}, bf16[24,2,1,128,128]{4,0,3,2,1:T(8,128)(2,1)S(1)}, u32[]{:S(2)}, u32[]{:S(2)}) collective-permute-start(bf16[24,2,1,128,128]{4,0,3,2,1:T(8,128)(2,1)S(1)} %get-tuple-element.23), channel_id=1, source_target_pairs={{0,4},{4,8},{8,12},{12,16},{16,20},{20,24},{24,28},{1,5},{5,9},{9,... | collective-permute-start | bytes 4718600 | tf_op jit(solution)/shard_map/ppermute | solution.py:24
  377.6 6.7 %collective-permute-start.25 = (bf16[24,2,1,128,128]{4,0,3,2,1:T(8,128)(2,1)S(1)}, bf16[24,2,1,128,128]{4,0,3,2,1:T(8,128)(2,1)S(1)}, u32[]{:S(2)}, u32[]{:S(2)}) collective-permute-start(bf16[24,2,1,128,128]{4,0,3,2,1:T(8,128)(2,1)S(1)} %get-tuple-element.24), channel_id=1, source_target_pairs={{4,0},{8,4},{12,8},{16,12},{20,16},{24,20},{28,24},{5,1},{9,5},{13... | collective-permute-start | bytes 4718600 | tf_op jit(solution)/shard_map/ppermute | solution.py:26
  390.5 40.7 %collective-permute-start.26 = (bf16[24,1,4,128,128]{4,0,3,2,1:T(8,128)(2,1)}, bf16[24,1,4,128,128]{4,0,3,2,1:T(8,128)(2,1)}, u32[]{:S(2)}, u32[]{:S(2)}) collective-permute-start(bf16[24,1,4,128,128]{4,0,3,2,1:T(8,128)(2,1)} %get-tuple-element.17), channel_id=1, source_target_pairs={{0,1},{1,2},{2,3},{4,5},{5,6},{6,7},{8,9},{9,10},{10,11},{12,13},{... | collective-permute-start | bytes 9437192 | tf_op jit(solution)/shard_map/ppermute | solution.py:24
  394.3 43.2 %collective-permute-start.27 = (bf16[24,1,4,128,128]{4,0,3,2,1:T(8,128)(2,1)}, bf16[24,1,4,128,128]{4,0,3,2,1:T(8,128)(2,1)}, u32[]{:S(2)}, u32[]{:S(2)}) collective-permute-start(bf16[24,1,4,128,128]{4,0,3,2,1:T(8,128)(2,1)} %get-tuple-element.18), channel_id=1, source_target_pairs={{1,0},{2,1},{3,2},{5,4},{6,5},{7,6},{9,8},{10,9},{11,10},{13,12},{... | collective-permute-start | bytes 9437192 | tf_op jit(solution)/shard_map/ppermute | solution.py:26
  477.4 43.0 %collective-permute-start.28 = (f32[2,4,1,128,128]{4,3,2,1,0:T(8,128)S(1)}, f32[2,4,1,128,128]{4,3,2,1,0:T(8,128)S(1)}, u32[]{:S(2)}, u32[]{:S(2)}) collective-permute-start(f32[2,4,1,128,128]{4,3,2,1,0:T(8,128)S(1)} %copy.110), channel_id=1, source_target_pairs={{4,0},{8,4},{12,8},{16,12},{20,16},{24,20},{28,24},{5,1},{9,5},{13... | collective-permute-start | bytes 1572872 | tf_op jit(solution)/shard_map/ppermute | solution.py:36
  479.0 41.4 %collective-permute-start.29 = (f32[2,4,1,128,128]{4,3,2,1,0:T(8,128)S(1)}, f32[2,4,1,128,128]{4,3,2,1,0:T(8,128)S(1)}, u32[]{:S(2)}, u32[]{:S(2)}) collective-permute-start(f32[2,4,1,128,128]{4,3,2,1,0:T(8,128)S(1)} %copy.111), channel_id=1, source_target_pairs={{0,4},{4,8},{8,12},{12,16},{16,20},{20,24},{24,28},{1,5},{5,9},{9,... | collective-permute-start | bytes 1572872 | tf_op jit(solution)/shard_map/ppermute | solution.py:36
  521.4 8.7 %collective-permute-start.30 = (f32[2,1,2,128,128]{4,3,2,1,0:T(8,128)}, f32[2,1,2,128,128]{4,3,2,1,0:T(8,128)}, u32[]{:S(2)}, u32[]{:S(2)}) collective-permute-start(f32[2,1,2,128,128]{4,3,2,1,0:T(8,128)} %get-tuple-element.39), channel_id=1, source_target_pairs={{1,0},{2,1},{3,2},{5,4},{6,5},{7,6},{9,8},{10,9},{11,10},{13,12},{... | collective-permute-start | bytes 786440 | tf_op jit(solution)/shard_map/ppermute | solution.py:36
  522.8 8.7 %collective-permute-start.31 = (f32[2,1,2,128,128]{4,3,2,1,0:T(8,128)}, f32[2,1,2,128,128]{4,3,2,1,0:T(8,128)}, u32[]{:S(2)}, u32[]{:S(2)}) collective-permute-start(f32[2,1,2,128,128]{4,3,2,1,0:T(8,128)} %get-tuple-element.40), channel_id=1, source_target_pairs={{0,1},{1,2},{2,3},{4,5},{5,6},{6,7},{8,9},{9,10},{10,11},{12,13},{... | collective-permute-start | bytes 786440 | tf_op jit(solution)/shard_map/ppermute | solution.py:36
  (50 other events, 1159.4 us)
where the time goes:
time: 622 us; the launch traced here: 614 us
  starting transfers between devices  215 us (35%)
  matrix products  144 us (23%)
  waiting for transfers between devices  127 us (20%)
  blocking collectives  69.6 us (11%)
  local copies, waits for them, and re-layouts  29.2 us (5%)
  other arithmetic  23.8 us (4%)
    ppermute x12, starting transfers between devices, padded_2(): lax.ppermute(tail, axis, [(i, (i + 1) % count) for i in range(ends)])  121 us
    conv_general_dilated x8, matrix products, correlate(): lax.conv_general_dilated(padded, kernel, (1, 1, 1), 'VALID', dimension_nu...  107 us
    ppermute x8, starting transfers between devices, from_behind(): return lax.ppermute(block, axis, route)  77.8 us
    ppermute x12, waiting for transfers between devices, padded_2(): lax.ppermute(head, axis, [((i + 1) % count, i) for i in range(ends)])  73.2 us
    psum x1, blocking collectives, per_device(): summed = lax.psum(partial_value, ('readout', 'frame'))  69.6 us
    ppermute x12, waiting for transfers between devices, padded_2(): lax.ppermute(tail, axis, [(i, (i + 1) % count) for i in range(ends)])  51 us
    dot_general x4, matrix products, transform(): jnp.einsum('qcfxyz,qzpk->pcfxyk', middle, block_z, precision=lax.Precisio...  20 us
    dot_general x4, matrix products, transform(): jnp.einsum('pkqy,qcfxyz->pcfxkz', block_y, stacked, precision=lax.Precisi...  16.8 us
  transfers between devices with their start and end apart: 32, of which 20 were waited for; matrix products, arithmetic and copies ran while one was open for 11% of the time, Pallas kernels for 0%

commit v1 on v0

v1 whole, which is shorter than its diff:
```python
import functools
import math

import jax
import jax.numpy as jnp
import numpy as np
from jax import lax
from jax.experimental import pallas as pl
from jax.experimental.pallas import tpu as pltpu
from jax.sharding import PartitionSpec as P

ETA = 0.5
RIDGE = 0.0001
AXES = ("readout", "frame")
F32 = jnp.float32
BF16 = jnp.bfloat16
VMEM = pl.BlockSpec(memory_space=pltpu.VMEM)
GROUP = 8
WIDE = 16


class Plan:
    def __init__(self, devices_x, devices_t, frames, width, ny, nz, channels):
        self.R, self.F, self.tl, self.xl = devices_x, devices_t, frames, width
        self.ny, self.nz, self.ch = ny, nz, channels
        self.D = devices_x * devices_t
        self.T, self.X = frames * devices_t, width * devices_x
        self.zl = nz // self.D
        self.nzb = min(2, self.zl)
        self.NZB = self.zl // self.nzb
        self.L = self.nzb * ny
        self.unit = frames * 2 * width
        self.rows = self.X * channels
        self.M = GROUP * channels
        self.G = self.X // GROUP
        if self.G == 1:
            self.W, self.ws = self.M, [0]
        else:
            self.W = self.M + 32 if self.G == 2 else self.M + 64
            self.ws = [min(max(self.M * g - 32, 0), self.rows - self.W) for g in range(self.G)]
        self.GI = self.X // WIDE
        near = WIDE // width
        self.near = near
        extra = 0 if self.GI == 1 else 2
        self.UW = (near + extra) * self.unit
        self.us = [min(max(near * g - extra // 2, 0), devices_x - near - extra) for g in range(self.GI)]
        wide = WIDE * channels
        self.KW = wide if self.GI == 1 else wide + 64
        self.ks = [min(max(wide * g - 32, 0), self.rows - self.KW) for g in range(self.GI)]

    def mid_table(self, g):
        k = np.arange(9 * self.W)
        row = self.ws[g] + k % self.W
        tap = k // self.W
        return pack(tap * self.ch + row % self.ch, row // self.ch)

    def in_table(self, g, t2):
        k = np.arange(9 * self.UW)
        slot, c, rest = k // (3 * self.UW), k // self.UW % 3, k % self.UW
        r, rest = self.us[g] + rest // self.unit, rest % self.unit
        frame, part, x2 = rest // (2 * self.xl), rest // self.xl % 2, rest % self.xl
        a = self.tl * (slot - 1) + frame - t2 + 1
        q = np.where((a >= 0) & (a <= 2), (a * 3 + c) * 2 + part, -1)
        return pack(q, r * self.xl + x2)

    def out_rows(self, g, s):
        m = np.arange(2 * 3 * self.near * self.unit)
        target, rest = m // (3 * self.near * self.unit), m % (3 * self.near * self.unit)
        c, rest = rest // (self.near * self.unit), rest % (self.near * self.unit)
        r, rest = self.near * g + rest // self.unit, rest % self.unit
        frame, part, x2 = rest // (2 * self.xl), rest // self.xl % 2, rest % self.xl
        offset = self.tl if s == 0 else -self.tl
        a = s - frame + 1 + np.where(target == 1, offset, 0)
        q = np.where((a >= 0) & (a <= 2), (a * 3 + c) * 2 + part, -1)
        pick = (q[:, None] == np.arange(24)[None, :]).astype(np.float32).astype(BF16)
        return pick, (r * self.xl + x2).astype(np.int32)

    def out_cols(self, g):
        row = self.ks[g] + np.arange(self.KW)
        return pack(row % self.ch, row // self.ch)


def pack(q, position):
    return np.stack([q, position] + [np.zeros_like(q)] * 6).astype(np.int32)


def dot(a, b):
    return jnp.dot(a, b, preferred_element_type=F32)


def one_hot_rows(table, rows):
    k = table.shape[1]
    index = lax.broadcasted_iota(jnp.int32, (rows, k), 0)
    return (index == jnp.broadcast_to(table[0:1, :], (rows, k))).astype(F32).astype(BF16)


def banded(weights, table, first, count, channels, out_ref, where, row0):
    spread = dot(weights, one_hot_rows(table, weights.shape[1]))
    parts = [spread[b * channels : (b + 1) * channels] for b in range(3)]
    position = table[1:2, :]
    for pair in range(count // 2):
        rows = []
        for x in (first + 2 * pair, first + 2 * pair + 1):
            rows.append(
                jnp.where(
                    position == x - 1,
                    parts[0],
                    jnp.where(position == x, parts[1], jnp.where(position == x + 1, parts[2], 0.0)),
                )
            )
        out_ref[where, row0 + 2 * pair * channels : row0 + 2 * (pair + 1) * channels, :] = jnp.concatenate(
            rows, axis=0
        ).astype(BF16)


def weights_kernel(
    p, w_in, w_mid, w_out, b_mid, b_in, mid_tab, in_tab, pick, row_x, col_tab, m_in, m_out, m_mid, m_back, m_last
):
    for g in range(p.G):
        table = mid_tab[g]
        banded(w_mid[...], table, g * GROUP, GROUP, p.ch, m_mid, g, 0)
        banded(b_mid[...], table, g * GROUP, GROUP, p.ch, m_back, g, 0)
    for g in range(p.GI):
        for t2 in range(p.tl):
            table = in_tab[g, t2]
            banded(w_in[...], table, g * WIDE, WIDE, p.ch, m_in, g, t2 * WIDE * p.ch)
            banded(w_out[...], table, g * WIDE, WIDE, p.ch, m_out, g, t2 * WIDE * p.ch)
        cols = col_tab[g]
        place = one_hot_rows(cols, p.ch)
        position = cols[1:2, :]
        taps = [dot(b_in[b], place).astype(BF16) for b in range(3)]
        for s in range(p.tl):
            x = row_x[g, s]
            total = jnp.zeros((x.shape[0], p.KW), F32)
            for b in range(3):
                total = jnp.where(position == x + (b - 1), dot(pick[g, s], taps[b]), total)
            m_last[g, s] = total.astype(BF16)


def shifted(value, c, ny):
    if c == 1:
        return value
    pieces = []
    for at in range(0, value.shape[1], ny):
        piece = value[:, at : at + ny]
        lane = lax.broadcasted_iota(jnp.int32, piece.shape, 1)
        if c == 0:
            pieces.append(jnp.where(lane == 0, 0.0, pltpu.roll(piece, 1, 1)))
        else:
            pieces.append(jnp.where(lane == ny - 1, 0.0, pltpu.roll(piece, ny - 1, 1)))
    return pieces[0] if len(pieces) == 1 else jnp.concatenate(pieces, axis=1)


def gather_field(p, load, u_ref):
    for f in range(p.F):
        pieces = [load(f, j).reshape(p.R * p.unit, p.ny) for j in range(p.nzb)]
        value = pieces[0] if p.nzb == 1 else jnp.concatenate(pieces, axis=1)
        for c in range(3):
            moved = shifted(value, c, p.ny)
            for g in range(p.GI):
                lo = p.us[g] * p.unit
                start = ((f + 1) * 3 + c) * p.UW
                u_ref[g, start : start + p.UW, :] = moved[lo : lo + p.UW].astype(BF16)


def put_window(p, h_ref, g, t, value):
    for c in range(3):
        moved = shifted(value, c, p.ny).astype(BF16)
        for h in range(p.G):
            lo, hi = max(p.M * g, p.ws[h]), min(p.M * (g + 1), p.ws[h] + p.W)
            if lo < hi:
                start = pl.multiple_of((t + 1) * (3 * p.W) + (c * p.W + lo - p.ws[h]), 16)
                h_ref[h, pl.ds(start, hi - lo), :] = moved[lo - p.M * g : hi - p.M * g]


def first_layer(p, matrix, u_ref, each):
    def body(f, carry):
        for t2 in range(p.tl):
            for g in range(p.G):
                gi, at = g * GROUP // WIDE, g * GROUP % WIDE
                rows = pl.ds(t2 * WIDE * p.ch + at * p.ch, p.M)
                start = pl.multiple_of(f * (3 * p.UW), 16)
                each(f * p.tl + t2, g, dot(matrix[gi, rows, :], u_ref[gi, pl.ds(start, 9 * p.UW), :]))
        return carry

    lax.fori_loop(0, p.F, body, 0)


def middle_layer(p, matrix, h_ref, each):
    def body(t, carry):
        for g in range(p.G):
            start = pl.multiple_of(t * (3 * p.W), 16)
            each(t, g, dot(matrix[g], h_ref[g, pl.ds(start, 9 * p.W), :]))
        return carry

    lax.fori_loop(0, p.T, body, 0)


def last_layer(p, matrix, g_ref, acc_ref):
    acc_ref[...] = jnp.zeros_like(acc_ref)
    size = p.near * p.unit

    def body(f, carry):
        for g in range(p.GI):
            for s in range(p.tl):
                out = dot(matrix[g, s], g_ref[f * p.tl + s, pl.ds(p.ks[g], p.KW), :])
                for target in range(2):
                    slot = f + 1 if target == 0 else (f if s == 0 else f + 2)
                    value = sum(
                        shifted(out[(target * 3 + c) * size : (target * 3 + c + 1) * size], c, p.ny) for c in range(3)
                    )
                    acc_ref[slot, pl.ds(g * size, size), :] += value
        return carry

    lax.fori_loop(0, p.F, body, 0)


def backward(p, zb, load, m_out, m_back, m_last, slope_one, slope_two, back, u_ref, h_ref, g_ref, acc_ref):
    gather_field(p, load, u_ref)

    def after_out(t, g, value):
        rows = pl.ds(p.M * g, p.M)
        put_window(p, h_ref, g, t, slope_two[zb, t, rows, :].astype(F32) * value)

    first_layer(p, m_out, u_ref, after_out)

    def after_mid(t, g, value):
        rows = pl.ds(p.M * g, p.M)
        g_ref[t, rows, :] = (slope_one[zb, t, rows, :].astype(F32) * value).astype(BF16)

    middle_layer(p, m_back, h_ref, after_mid)
    last_layer(p, m_last, g_ref, acc_ref)
    for f in range(p.F):
        for j in range(p.nzb):
            value = acc_ref[f + 1, :, j * p.ny : (j + 1) * p.ny].reshape(p.R, p.unit, p.ny)
            back[:, f, zb * p.nzb + j, :, :] = value.astype(BF16)


def clear_edges(p, u_ref, h_ref):
    u_ref[:, : 3 * p.UW, :] = jnp.zeros((p.GI, 3 * p.UW, p.L), BF16)
    u_ref[:, (p.F + 1) * 3 * p.UW :, :] = jnp.zeros((p.GI, 3 * p.UW, p.L), BF16)
    h_ref[:, : 3 * p.W, :] = jnp.zeros((p.G, 3 * p.W, p.L), BF16)
    h_ref[:, (p.T + 1) * 3 * p.W :, :] = jnp.zeros((p.G, 3 * p.W, p.L), BF16)


def both_kernel(
    p, got, bias_one, bias_two, m_in, m_out, m_mid, m_back, m_last,
    slope_one, slope_two, back, u_ref, h_ref, g_ref, acc_ref,
):
    clear_edges(p, u_ref, h_ref)

    def block(zb, carry):
        def load(which, f, j):
            value = got[:, f, zb * p.nzb + j, :, :].astype(F32)
            return value[:, which * p.unit : (which + 1) * p.unit]

        gather_field(p, functools.partial(load, 0), u_ref)

        def after_in(t, g, value):
            pre = value + bias_one[...]
            sigma = jax.nn.sigmoid(pre)
            slope_one[zb, t, pl.ds(p.M * g, p.M), :] = (sigma * (1.0 + pre * (1.0 - sigma))).astype(BF16)
            put_window(p, h_ref, g, t, pre * sigma)

        first_layer(p, m_in, u_ref, after_in)

        def after_mid(t, g, value):
            pre = value + bias_two[...]
            sigma = jax.nn.sigmoid(pre)
            slope_two[zb, t, pl.ds(p.M * g, p.M), :] = (sigma * (1.0 + pre * (1.0 - sigma))).astype(BF16)

        middle_layer(p, m_mid, h_ref, after_mid)
        backward(
            p, zb, functools.partial(load, 1), m_out, m_back, m_last,
            slope_one, slope_two, back, u_ref, h_ref, g_ref, acc_ref,
        )
        return carry

    lax.fori_loop(0, p.NZB, block, 0)


def back_kernel(
    p, got, before, m_out, m_back, m_last, slope_one, slope_two, back, u_ref, h_ref, g_ref, acc_ref
):
    clear_edges(p, u_ref, h_ref)

    def block(zb, carry):
        def load(f, j):
            at = zb * p.nzb + j
            return got[:, f, at, :, :].astype(F32) - before[:, f, at, :, :].astype(F32)

        backward(p, zb, load, m_out, m_back, m_last, slope_one, slope_two, back, u_ref, h_ref, g_ref, acc_ref)
        return carry

    lax.fori_loop(0, p.NZB, block, 0)


def planes(p):
    for t2 in range(p.tl):
        for part in range(2):
            for x2 in range(p.xl):
                yield (t2 * 2 + part) * p.xl + x2, (part, t2, x2)


def pack_kernel(p, *refs):
    fields, out, scratch = refs[:-2], refs[-2], refs[-1]
    total = len(fields) * p.unit
    for n, field in enumerate(fields):
        for row, at in planes(p):
            scratch[pl.ds(n * p.unit + row, p.nz, stride=total), :] = field[at].T
    out[...] = scratch[...].reshape(p.nz, total, p.ny).astype(BF16)


def less_kernel(p, field, got, out, scratch):
    scratch[...] = got[...].astype(F32).reshape(p.nz * p.unit, p.ny)
    for row, at in planes(p):
        out[at] = field[at] - scratch[pl.ds(row, p.nz, stride=p.unit), :].T


def finish_kernel(p, field, got, first, cotangent, out, gram, scratch):
    scratch[...] = got[...].astype(F32).reshape(p.nz * p.unit, p.ny)
    sums = [jnp.zeros((1, p.nz), F32) for _ in range(3)]
    for row, at in planes(p):
        mapped = field[at] - scratch[pl.ds(row, p.nz, stride=p.unit), :].T
        out[at] = mapped
        old = first[at] - cotangent[at]
        new = mapped - first[at]
        for n, product in enumerate((old * old, new * old, new * new)):
            sums[n] = sums[n] + jnp.sum(product, axis=0, keepdims=True)
    lane = lax.broadcasted_iota(jnp.int32, (1, 128), 1)
    line = jnp.zeros((1, 128), F32)
    for n in range(3):
        line = jnp.where(lane == n, jnp.sum(sums[n], axis=1, keepdims=True), line)
    gram[...] = line


def small_solve(lines, values):
    order = len(values)
    lines = [list(line) for line in lines]
    values = list(values)
    for column in range(order):
        for line in range(column + 1, order):
            factor = lines[line][column] / lines[column][column]
            lines[line] = [a - factor * b for a, b in zip(lines[line], lines[column])]
            values[line] = values[line] - factor * values[column]
    solution = [None] * order
    for line in reversed(range(order)):
        running = values[line]
        for column in range(line + 1, order):
            running = running - lines[line][column] * solution[column]
        solution[line] = running / lines[line][line]
    return solution


def mix_kernel(gathered, first, second, out):
    total = jnp.sum(gathered[...], axis=0)
    g00, g10, g11 = (total[:, n : n + 1] for n in range(3))
    ridge = RIDGE * (g00 + g11) / 2
    one = jnp.ones_like(g00)
    solution = small_solve([[g00 + ridge, g10], [g10, g11 + ridge]], [one, one])
    whole = solution[0] + solution[1]
    alpha = [value / whole for value in solution]
    for part in range(out.shape[0]):
        for t in range(out.shape[1]):
            for x in range(out.shape[2]):
                at = (part, t, x)
                out[at] = alpha[0] * first[at] + alpha[1] * second[at]


def split(value, axis, order):
    high = value.astype(BF16)
    low = (value - high.astype(F32)).astype(BF16)
    return jnp.concatenate([high if kind == "h" else low for kind in order], axis=axis)


def dft_blocks(length, sign, left):
    index = np.arange(length)
    angle = 2.0 * math.pi / length * (index[:, None] * index[None, :] % length)
    cosine, sine = np.cos(angle) / math.sqrt(length), sign * np.sin(angle) / math.sqrt(length)
    if left:
        table = np.block([[cosine, sine], [-sine, cosine]])
    else:
        table = np.block([[cosine, -sine], [sine, cosine]])
    table = table.astype(np.float32)
    high = table.astype(BF16)
    low = (table - high.astype(np.float32)).astype(BF16)
    return np.concatenate([high, high, low], axis=1 if left else 0)


def normal_kernel(field, cotangent, sens, mask, right, left, left_back, right_back, out):
    coils, ny, nz = sens.shape[1], sens.shape[3], sens.shape[4]
    real, imag = field[0, 0, 0], field[1, 0, 0]
    total_real, total_imag = jnp.zeros((ny, nz), F32), jnp.zeros((ny, nz), F32)
    for first in range(0, coils, 2):
        pair = (first, first + 1)
        lines = []
        for c in pair:
            s_real, s_imag = sens[0, c, 0], sens[1, c, 0]
            lines.append(jnp.concatenate([s_real * real - s_imag * imag, s_real * imag + s_imag * real], axis=1))
        value = dot(split(jnp.concatenate(lines, axis=0), 1, "hlh"), right[...])
        value = turn(value, ny, nz)
        value = dot(left[...], split(value, 0, "hlh"))
        keep = jnp.concatenate([mask[0, c].astype(F32) for c in pair], axis=1)
        value = value * jnp.concatenate([keep, keep], axis=0)
        value = dot(left_back[...], split(value, 0, "hlh"))
        value = turn(value, ny, nz)
        value = dot(split(value, 1, "hlh"), right_back[...])
        for n, c in enumerate(pair):
            s_real, s_imag = sens[0, c, 0], sens[1, c, 0]
            z_real, z_imag = value[n * ny : (n + 1) * ny, :nz], value[n * ny : (n + 1) * ny, nz:]
            total_real += s_real * z_real + s_imag * z_imag
            total_imag += s_real * z_imag - s_imag * z_real
    out[0, 0, 0] = cotangent[0, 0, 0] + real - ETA * total_real
    out[1, 0, 0] = cotangent[1, 0, 0] + imag - ETA * total_imag


def turn(value, ny, nz):
    top = jnp.concatenate([value[:ny, :nz], value[ny:, :nz]], axis=1)
    bottom = jnp.concatenate([value[:ny, nz:], value[ny:, nz:]], axis=1)
    return jnp.concatenate([top, bottom], axis=0)


def normal_step(field, cotangent, sensitivity, sampling, tables):
    _, frames, width, ny, nz = field.shape
    coils = sensitivity.shape[1]
    image = pl.BlockSpec((2, 1, 1, ny, nz), lambda x, t: (0, t, x, 0, 0))
    whole = [pl.BlockSpec(table.shape, lambda x, t: (0, 0)) for table in tables]
    return pl.pallas_call(
        normal_kernel,
        grid=(width, frames),
        in_specs=[
            image,
            image,
            pl.BlockSpec((2, coils, 1, ny, nz), lambda x, t: (0, 0, x, 0, 0)),
            pl.BlockSpec((1, coils, ny, nz), lambda x, t: (t, 0, 0, 0)),
            *whole,
        ],
        out_specs=image,
        out_shape=jax.ShapeDtypeStruct(field.shape, F32),
        compiler_params=pltpu.CompilerParams(vmem_limit_bytes=48 << 20),
        cost_estimate=pl.CostEstimate(
            flops=width * frames * coils * 4 * 3 * 2 * 2 * ny * nz * 2 * nz,
            bytes_accessed=20 << 20,
            transcendentals=0,
        ),
        name="normal",
    )(field, cotangent, sensitivity, sampling, *tables)


def call(kernel, outs, args, name, scratch=(), flops=1 << 20, moved=4 << 20):
    shapes = [jax.ShapeDtypeStruct(shape, kind) for shape, kind in outs]
    single = len(shapes) == 1
    return pl.pallas_call(
        kernel,
        in_specs=[VMEM] * len(args),
        out_specs=VMEM if single else [VMEM] * len(shapes),
        out_shape=shapes[0] if single else shapes,
        scratch_shapes=list(scratch),
        compiler_params=pltpu.CompilerParams(vmem_limit_bytes=60 << 20),
        cost_estimate=pl.CostEstimate(flops=flops, bytes_accessed=moved, transcendentals=0),
        name=name,
    )(*args)


def flip_kernel(weight):
    return jnp.transpose(jnp.flip(weight, (2, 3, 4)), (1, 0, 2, 3, 4))


def by_offset(weight):
    outs, ins = weight.shape[:2]
    return jnp.transpose(weight, (3, 0, 2, 4, 1)).reshape(3 * outs, 9 * ins)


def exchange(blocks):
    return lax.all_to_all(blocks, AXES, 0, 0, tiled=True)


def per_device(
    equilibrium, cotangent, sensitivity, sampling, weight_in, bias_in, weight_mid, bias_mid, weight_out
):
    _, frames, width, ny, nz = cotangent.shape
    p = Plan(lax.axis_size("readout"), lax.axis_size("frame"), frames, width, ny, nz, weight_in.shape[0])
    field_shape = cotangent.shape
    z_shape = (p.R, p.F, p.zl, p.unit, ny)
    tables = [
        jnp.asarray(dft_blocks(nz, 1.0, False)),
        jnp.asarray(dft_blocks(ny, 1.0, True)),
        jnp.asarray(dft_blocks(ny, -1.0, True)),
        jnp.asarray(dft_blocks(nz, -1.0, False)),
    ]

    def pack_fields(*fields):
        rows = len(fields) * p.unit
        packed = call(
            functools.partial(pack_kernel, p),
            [((nz, rows, ny), BF16)],
            fields,
            "pack",
            [pltpu.VMEM((nz * rows, ny), F32)],
        )
        return packed.reshape(p.D, p.zl, rows, ny)

    got = exchange(pack_fields(equilibrium, cotangent)).reshape(p.R, p.F, p.zl, 2 * p.unit, ny)

    picks = [[p.out_rows(g, s) for s in range(p.tl)] for g in range(p.GI)]
    back_in = flip_kernel(weight_in)
    last = jnp.transpose(back_in, (3, 2, 4, 0, 1)).reshape(3, 18, p.ch)
    last = jnp.pad(last, ((0, 0), (0, 6), (0, 0)))
    weight_args = [
        by_offset(weight_in),
        by_offset(weight_mid),
        by_offset(flip_kernel(weight_out)),
        by_offset(flip_kernel(weight_mid)),
        last,
        jnp.asarray(np.stack([p.mid_table(g) for g in range(p.G)])),
        jnp.asarray(np.stack([np.stack([p.in_table(g, s) for s in range(p.tl)]) for g in range(p.GI)])),
        jnp.asarray(np.stack([np.stack([pick for pick, _ in line]) for line in picks])),
        jnp.asarray(np.stack([np.stack([x[:, None] for _, x in line]) for line in picks])),
        jnp.asarray(np.stack([p.out_cols(g) for g in range(p.GI)])),
    ]
    in_shape = (p.GI, p.tl * WIDE * p.ch, 9 * p.UW)
    mid_shape = (p.G, p.M, 9 * p.W)
    last_shape = (p.GI, p.tl, 6 * p.near * p.unit, p.KW)
    m_in, m_out, m_mid, m_back, m_last = call(
        functools.partial(weights_kernel, p),
        [(in_shape, BF16), (in_shape, BF16), (mid_shape, BF16), (mid_shape, BF16), (last_shape, BF16)],
        weight_args,
        "weights",
    )
    bias_one = jnp.broadcast_to(jnp.tile(bias_in, GROUP)[:, None], (p.M, p.L))
    bias_two = jnp.broadcast_to(jnp.tile(bias_mid, GROUP)[:, None], (p.M, p.L))

    point = normal_step(cotangent, cotangent, sensitivity, sampling, tables)
    got_point = exchange(pack_fields(point)).reshape(z_shape)

    slope = ((p.NZB, p.T, p.rows, p.L), BF16)
    scratch = [
        pltpu.VMEM((p.GI, (p.F + 2) * 3 * p.UW, p.L), BF16),
        pltpu.VMEM((p.G, (p.T + 2) * 3 * p.W, p.L), BF16),
        pltpu.VMEM((p.T, p.rows, p.L), BF16),
        pltpu.VMEM((p.F + 2, p.R * p.unit, p.L), F32),
    ]
    work = 2 * p.NZB * p.T * p.L * p.rows * 9 * p.W
    slope_one, slope_two, back = call(
        functools.partial(both_kernel, p),
        [slope, slope, (z_shape, BF16)],
        [got, bias_one, bias_two, m_in, m_out, m_mid, m_back, m_last],
        "both",
        scratch,
        3 * work,
        16 << 20,
    )
    returned = exchange(back.reshape(p.D, p.zl, p.unit, ny)).reshape(nz, p.unit, ny)
    back_two = call(
        functools.partial(back_kernel, p),
        [(z_shape, BF16)],
        [got_point, back, m_out, m_back, m_last, slope_one, slope_two],
        "back",
        scratch,
        3 * work // 2,
        12 << 20,
    )
    returned_two = exchange(back_two.reshape(p.D, p.zl, p.unit, ny)).reshape(nz, p.unit, ny)
    turn_scratch = [pltpu.VMEM((nz * p.unit, ny), F32)]
    first = call(
        functools.partial(less_kernel, p), [(field_shape, F32)], [point, returned], "less", turn_scratch
    )
    point_two = normal_step(first, cotangent, sensitivity, sampling, tables)
    second, gram = call(
        functools.partial(finish_kernel, p),
        [(field_shape, F32), ((1, 128), F32)],
        [point_two, returned_two, first, cotangent],
        "finish",
        turn_scratch,
    )
    gathered = exchange(jnp.broadcast_to(gram[None], (p.D, 1, 128)))
    return call(mix_kernel, [(field_shape, F32)], [gathered, first, second], "mix")


def solution(mesh):
    placed = (
        P(None, "frame", "readout", None, None),
        P(None, "frame", "readout", None, None),
        P(None, None, "readout", None, None),
        P("frame", None, None, None),
        P(),
        P(),
        P(),
        P(),
        P(),
    )
    return jax.shard_map(
        per_device,
        mesh=mesh,
        in_specs=placed,
        out_specs=P(None, "frame", "readout", None, None),
        check_vma=False,
    )
```

time: 622 us -> 173 us (0.28); the launches traced: 614 us -> 172 us
  starting transfers between devices: 215 us -> 25 us
  matrix products: 144 us -> 0 us
  waiting for transfers between devices: 127 us -> 0.01 us
  Pallas kernels: 0 us -> 115 us
  blocking collectives: 69.6 us -> 12.7 us
  other arithmetic: 23.8 us -> 0 us
  local copies, waits for them, and re-layouts: 29.2 us -> 19 us
    ppermute x32 -> x0, starting transfers between devices: 215 us -> none  [the longest x12 121 us: padded_2(): lax.ppermute(tail, axis, [(i, (i + 1) % count) for i in range(ends)])]
    ppermute x32 -> x0, waiting for transfers between devices: 127 us -> none  [the longest x12 73.2 us: padded_2(): lax.ppermute(head, axis, [((i + 1) % count, i) for i in range(ends)])]
    pallas_call x0 -> x10, Pallas kernels: none -> 115 us  [the longest x8 82.2 us: call(): pl.pallas_call(kernel, in_specs=[VMEM] * len(args), out_specs=VMEM if sin...]
    conv_general_dilated x8 -> x0, matrix products: 107 us -> none  [correlate(): lax.conv_general_dilated(padded, kernel, (1, 1, 1), 'VALID', dimension_nu...]
    psum x1 -> x0, blocking collectives: 69.6 us -> none  [per_device(): summed = lax.psum(partial_value, ('readout', 'frame'))]
    dot_general x8 -> x0, matrix products: 36.8 us -> none  [the longest x4 20 us: transform(): jnp.einsum('qcfxyz,qzpk->pcfxyk', middle, block_z, precision=lax.Precisio...]
    all_to_all x0 -> x4, starting transfers between devices: none -> 25 us  [exchange(): return lax.all_to_all(blocks, AXES, 0, 0, tiled=True)]
    slice x21 -> x0, local copies, waits for them, and re-layouts: 16.5 us -> none  [the longest x12 11.7 us: padded_2(): lax.slice_in_dim(cells, cells.shape[dim] - width, cells.shape[dim], axis=...]
  transfers between devices with their start and end apart: 32 -> 4, of which waited for: 20 -> 0; matrix products, arithmetic and copies ran while one was open for 11% -> 7% of each run, Pallas kernels for 0% -> 62%
where the time goes in v1:
time: 173 us; the launch traced here: 172 us
  Pallas kernels  115 us (66%)
  starting transfers between devices  25 us (14%)
  local copies, waits for them, and re-layouts  19 us (11%)
  blocking collectives  12.7 us (7%)
    pallas_call x8, Pallas kernels, call(): pl.pallas_call(kernel, in_specs=[VMEM] * len(args), out_specs=VMEM if sin...  82.2 us
    pallas_call x2, Pallas kernels, normal_step(): pl.pallas_call(normal_kernel, grid=(width, frames), in_specs=[image, imag...  32.9 us
    all_to_all x4, starting transfers between devices, exchange(): return lax.all_to_all(blocks, AXES, 0, 0, tiled=True)  25 us
    all_to_all x1, blocking collectives, exchange(): return lax.all_to_all(blocks, AXES, 0, 0, tiled=True)  12.7 us
    unnamed x38, local copies, waits for them, and re-layouts  5.88 us
    reshape x6, local copies, waits for them, and re-layouts, by_offset(): return jnp.transpose(weight, (3, 0, 2, 4, 1)).reshape(3 * outs, 9 * ins)  5.05 us
  transfers between devices with their start and end apart: 4, of which 0 were waited for; matrix products, arithmetic and copies ran while one was open for 7% of the time, Pallas kernels for 62%

profile of v1, /device:TPU:0, one launch (start us, length us, event | category | flops | bytes accessed | tf_op | source)
XLA Modules:
  0.0 172.2 jit_solution(11377674224029815439)
XLA Ops:
  0.0 2.6 %pack.2 = bf16[128,16,128]{2,1,0:T(8,128)(2,1)} custom-call(f32[2,2,2,128,128]{4,3,2,1,0:T(8,128)} %refs_0_.1, f32[2,2,2,128,128]{4,3,2,1,0:T(8,128)} %cotangent.5), custom_call_target="tpu_custom_call" | custom-call | flops 1048576 | bytes 4194304 | tf_op jit(solution)/shard_map/pack/pallas_call | solution.py:453
  2.7 7.5 %all-to-all-start = ((bf16[32,4,16,128]{3,2,1,0:T(8,128)(2,1)}), bf16[32,4,16,128]{3,2,1,0:T(8,128)(2,1)}, u32[]{:S(2)}, u32[]{:S(2)}) async-start(bf16[32,4,16,128]{3,2,1,0:T(8,128)(2,1)} %bitcast.21), calls=%async_computation | async-start | bytes 1048576 | tf_op jit(solution)/shard_map/all_to_all | solution.py:475
  10.1 1.6 reverse_bitcast_fusion
  11.7 1.7 %copy.27 = bf16[3,24,3,3,24]{4,3,2,1,0:T(4,128)(2,1)} copy(bf16[3,24,3,3,24]{1,4,3,0,2:T(8,128)(2,1)} %reverse_bitcast_fusion) | data formatting | bytes 62208 | tf_op jit(solution)/shard_map/transpose;transpose | solution.py:471
  13.5 1.7 %reshape.51.b_mid = bf16[72,216]{1,0:T(8,128)(2,1)} reshape(bf16[3,24,3,3,24]{4,3,2,1,0:T(4,128)(2,1)} %copy.27) | data formatting | bytes 62208 | tf_op jit(solution)/shard_map/reshape | solution.py:471
  15.2 1.7 copy.25
  16.9 1.7 reshape.49.w_mid
  18.8 0.7 copy.30.w_out
  19.6 0.7 copy.29.w_in
  20.5 0.6 pad.4.b_in
  21.2 1.2 copy-done.5
  22.4 1.0 copy-done.9
  23.4 1.0 copy-done.11
  24.4 15.9 %normal.2.field.refs_0_ = f32[2,2,2,128,128]{4,3,2,1,0:T(8,128)S(1)} custom-call(f32[2,2,2,128,128]{4,3,2,1,0:T(8,128)S(1)} %copy-done.1, f32[2,2,2,128,128]{4,3,2,1,0:T(8,128)S(1)} %copy-done.1, f32[2,8,2,128,128]{4,3,2,1,0:T(8,128)S(1)} %copy-done.4, s32[2,8,128,128]{3,2,1,0:T(8,128)S(1)} %copy-done.5, bf16[768,256]{1,0:T(8,128)(2,1)S(1)} %copy-done.7, ...), custom_call_target="tpu_custom_call" | custom-call | flops 6442450944 | bytes 20971520 | tf_op jit(solution)/shard_map/normal/pallas_call | solution.py:428
  40.3 0.8 copy-done.2
  41.1 2.0 %pack.3 = bf16[128,8,128]{2,1,0:T(8,128)(2,1)} custom-call(f32[2,2,2,128,128]{4,3,2,1,0:T(8,128)} %copy-done.2), custom_call_target="tpu_custom_call" | custom-call | flops 1048576 | bytes 4194304 | tf_op jit(solution)/shard_map/pack/pallas_call | solution.py:453
  43.1 6.0 %weights.1 = (bf16[1,768,576]{2,1,0:T(8,128)(2,1)}, bf16[1,768,576]{2,1,0:T(8,128)(2,1)}, bf16[2,192,2016]{2,1,0:T(8,128)(2,1)}, bf16[2,192,2016]{2,1,0:T(8,128)(2,1)}, bf16[1,2,384,384]{3,2,1,0:T(8,128)(2,1)}) custom-call(bf16[72,18]{1,0:T(8,128)(2,1)} %copy.29.w_in, bf16[72,216]{1,0:T(8,128)(2,1)} %reshape.49.w_mid, bf16[72,18]{1,0:T(8,128)(2,1)} %copy.30.w_out, ...), custom_call_target="tpu_custom_call" | custom-call | flops 1048576 | bytes 4194304 | tf_op jit(solution)/shard_map/weights/pallas_call | solution.py:453
  49.1 5.8 %all-to-all-start.2 = ((bf16[32,4,8,128]{3,2,1,0:T(8,128)(2,1)}), bf16[32,4,8,128]{3,2,1,0:T(8,128)(2,1)S(1)}, u32[]{:S(2)}, u32[]{:S(2)}) async-start(bf16[32,4,8,128]{3,2,1,0:T(8,128)(2,1)} %bitcast.22), calls=%async_computation.2 | async-start | bytes 524288 | tf_op jit(solution)/shard_map/all_to_all | solution.py:475
  54.9 0.8 broadcast_in_dim.23.bias_one
  55.6 0.8 broadcast_in_dim.25.bias_two
  56.4 41.1 %both.1 = (bf16[2,8,384,256]{3,2,1,0:T(8,128)(2,1)}, bf16[2,8,384,256]{3,2,1,0:T(8,128)(2,1)}, bf16[8,4,4,8,128]{4,3,2,1,0:T(8,128)(2,1)}) custom-call(bf16[8,4,4,16,128]{4,3,2,1,0:T(8,128)(2,1)} %bitcast.1.got, f32[192,256]{1,0:T(8,128)} %broadcast_in_dim.23.bias_one, f32[192,256]{1,0:T(8,128)} %broadcast_in_dim.25.bias_two, ...), custom_call_target="tpu_custom_call" | custom-call | flops 19025362944 | bytes 16777216 | tf_op jit(solution)/shard_map/both/pallas_call | solution.py:453
  97.5 6.0 %all-to-all-start.1 = ((bf16[32,4,8,128]{3,2,1,0:T(8,128)(2,1)}), bf16[32,4,8,128]{3,2,1,0:T(8,128)(2,1)S(1)}, u32[]{:S(2)}, u32[]{:S(2)}) async-start(bf16[32,4,8,128]{3,2,1,0:T(8,128)(2,1)} %bitcast.27), calls=%async_computation.1 | async-start | bytes 524288 | tf_op jit(solution)/shard_map/all_to_all | solution.py:475
  103.5 23.4 %back.1 = bf16[8,4,4,8,128]{4,3,2,1,0:T(8,128)(2,1)} custom-call(bf16[8,4,4,8,128]{4,3,2,1,0:T(8,128)(2,1)} %bitcast.25, bf16[8,4,4,8,128]{4,3,2,1,0:T(8,128)(2,1)} %get-tuple-element.20.before, bf16[1,768,576]{2,1,0:T(8,128)(2,1)} %get-tuple-element.16.m_out, bf16[2,192,2016]{2,1,0:T(8,128)(2,1)} %get-tuple-element.18.m_back, ...), custom_call_target="tpu_custom_call" | custom-call | flops 9512681472 | bytes 12582912 | tf_op jit(solution)/shard_map/back/pallas_call | solution.py:453
  127.0 5.8 %all-to-all-start.3 = ((bf16[32,4,8,128]{3,2,1,0:T(8,128)(2,1)}), bf16[32,4,8,128]{3,2,1,0:T(8,128)(2,1)}, u32[]{:S(2)}, u32[]{:S(2)}) async-start(bf16[32,4,8,128]{3,2,1,0:T(8,128)(2,1)} %bitcast.26), calls=%async_computation.3 | async-start | bytes 524288 | tf_op jit(solution)/shard_map/all_to_all | solution.py:475
  132.8 2.1 %less.1.field.first = f32[2,2,2,128,128]{4,3,2,1,0:T(8,128)} custom-call(f32[2,2,2,128,128]{4,3,2,1,0:T(8,128)} %copy-done.2, bf16[128,8,128]{2,1,0:T(8,128)(2,1)} %bitcast.23), custom_call_target="tpu_custom_call" | custom-call | flops 1048576 | bytes 4194304 | tf_op jit(solution)/shard_map/less/pallas_call | solution.py:453
  134.9 1.0 copy-done
  136.0 17.0 %normal.3.field = f32[2,2,2,128,128]{4,3,2,1,0:T(8,128)S(1)} custom-call(f32[2,2,2,128,128]{4,3,2,1,0:T(8,128)S(1)} %copy-done, f32[2,2,2,128,128]{4,3,2,1,0:T(8,128)S(1)} %copy-done.1, f32[2,8,2,128,128]{4,3,2,1,0:T(8,128)} %sens.3, s32[2,8,128,128]{3,2,1,0:T(8,128)S(1)} %copy-done.6, bf16[768,256]{1,0:T(8,128)(2,1)S(1)} %copy-done.7, ...), custom_call_target="tpu_custom_call" | custom-call | flops 6442450944 | bytes 20971520 | tf_op jit(solution)/shard_map/normal/pallas_call | solution.py:428
  153.0 0.8 copy-done.3
  153.8 2.5 %finish.1 = (f32[2,2,2,128,128]{4,3,2,1,0:T(8,128)}, f32[1,128]{1,0:T(1,128)}) custom-call(f32[2,2,2,128,128]{4,3,2,1,0:T(8,128)} %copy-done.3, bf16[128,8,128]{2,1,0:T(8,128)(2,1)} %bitcast.12.got, f32[2,2,2,128,128]{4,3,2,1,0:T(8,128)} %less.1.field.first, f32[2,2,2,128,128]{4,3,2,1,0:T(8,128)} %cotangent.5), custom_call_target="tpu_custom_call" | custom-call | flops 1048576 | bytes 4194304 | tf_op jit(solution)/shard_map/finish/pallas_call | solution.py:453
  156.3 0.7 broadcast_in_dim.27
  157.0 12.7 %all_to_all.25.gathered = f32[32,1,128]{2,1,0:T(1,128)} all-to-all(f32[32,1,128]{2,1,0:T(1,128)S(1)} %broadcast_in_dim.27), channel_id=1, replica_groups=mesh['readout'=8,'frame'=4] {'readout','frame'}, dimensions={0} | all-to-all | bytes 32768 | tf_op jit(solution)/shard_map/all_to_all | solution.py:475
  169.7 2.5 %mix.1 = f32[2,2,2,128,128]{4,3,2,1,0:T(8,128)} custom-call(f32[32,1,128]{2,1,0:T(1,128)} %all_to_all.25.gathered, f32[2,2,2,128,128]{4,3,2,1,0:T(8,128)} %less.1.field.first, f32[2,2,2,128,128]{4,3,2,1,0:T(8,128)} %get-tuple-element.24.second), custom_call_target="tpu_custom_call" | custom-call | flops 1048576 | bytes 4194304 | tf_op jit(solution)/shard_map/mix/pallas_call | solution.py:453
  (48 shorter events, 0.5 us)
Async XLA Ops:
  0.0 21.1 %copy-start.7 = (bf16[768,256]{1,0:T(8,128)(2,1)S(1)}, bf16[768,256]{1,0:T(8,128)(2,1)}, u32[]{:S(2)}) copy-start(bf16[768,256]{1,0:T(8,128)(2,1)} %constant.21.clone.right) | copy-start | bytes 1179652
  0.0 21.1 %copy-start.8 = (bf16[256,768]{1,0:T(8,128)(2,1)S(1)}, bf16[256,768]{1,0:T(8,128)(2,1)}, u32[]{:S(2)}) copy-start(bf16[256,768]{1,0:T(8,128)(2,1)} %constant.22.clone.left) | copy-start | bytes 1179652
  0.0 21.1 %copy-start.1 = (f32[2,2,2,128,128]{4,3,2,1,0:T(8,128)S(1)}, f32[2,2,2,128,128]{4,3,2,1,0:T(8,128)}, u32[]{:S(2)}) copy-start(f32[2,2,2,128,128]{4,3,2,1,0:T(8,128)} %cotangent.5) | copy-start | bytes 1572868
  0.0 18.6 %copy-start.15 = (bf16[24,2,3,3,3]{0,1,4,3,2:T(2,128)(2,1)S(1)}, bf16[24,2,3,3,3]{0,1,4,3,2:T(2,128)(2,1)}, u32[]{:S(2)}) copy-start(bf16[24,2,3,3,3]{0,1,4,3,2:T(2,128)(2,1)} %param.22) | copy-start | bytes 7780
  0.0 18.7 %copy-start.16 = (bf16[2,24,3,3,3]{1,0,4,3,2:T(2,128)(2,1)S(1)}, bf16[2,24,3,3,3]{1,0,4,3,2:T(2,128)(2,1)}, u32[]{:S(2)}) copy-start(bf16[2,24,3,3,3]{1,0,4,3,2:T(2,128)(2,1)} %param.26) | copy-start | bytes 7780
  0.0 20.3 %copy-start.17 = (f32[24]{0:T(128)S(1)}, f32[24]{0:T(128)}, u32[]{:S(2)}) copy-start(f32[24]{0:T(128)} %param.23) | copy-start | bytes 292
  0.0 20.4 %copy-start.18 = (f32[24]{0:T(128)S(1)}, f32[24]{0:T(128)}, u32[]{:S(2)}) copy-start(f32[24]{0:T(128)} %param.25) | copy-start | bytes 292
  0.0 21.1 %copy-start.4 = (f32[2,8,2,128,128]{4,3,2,1,0:T(8,128)S(1)}, f32[2,8,2,128,128]{4,3,2,1,0:T(8,128)}, u32[]{:S(2)}) copy-start(f32[2,8,2,128,128]{4,3,2,1,0:T(8,128)} %sens.3) | copy-start | bytes 6291460
  2.7 46.4 %all-to-all-start = ((bf16[32,4,16,128]{3,2,1,0:T(8,128)(2,1)}), bf16[32,4,16,128]{3,2,1,0:T(8,128)(2,1)}, u32[]{:S(2)}, u32[]{:S(2)}) async-start(bf16[32,4,16,128]{3,2,1,0:T(8,128)(2,1)} %bitcast.21), calls=%async_computation | async-start | bytes 1048576 | tf_op jit(solution)/shard_map/all_to_all | solution.py:475
  21.1 1.2 copy-start.5
  22.4 1.0 copy-start.9
  23.4 1.0 copy-start.11
  40.3 0.8 copy-start.2
  49.1 48.4 %all-to-all-start.2 = ((bf16[32,4,8,128]{3,2,1,0:T(8,128)(2,1)}), bf16[32,4,8,128]{3,2,1,0:T(8,128)(2,1)S(1)}, u32[]{:S(2)}, u32[]{:S(2)}) async-start(bf16[32,4,8,128]{3,2,1,0:T(8,128)(2,1)} %bitcast.22), calls=%async_computation.2 | async-start | bytes 524288 | tf_op jit(solution)/shard_map/all_to_all | solution.py:475
  97.5 6.0 %copy-start.14 = (bf16[32,4,8,128]{3,2,1,0:T(8,128)(2,1)}, bf16[32,4,8,128]{3,2,1,0:T(8,128)(2,1)S(1)}, u32[]{:S(2)}) copy-start(bf16[32,4,8,128]{3,2,1,0:T(8,128)(2,1)S(1)} %all-to-all-done.2) | copy-start | bytes 786436
  97.5 29.5 %all-to-all-start.1 = ((bf16[32,4,8,128]{3,2,1,0:T(8,128)(2,1)}), bf16[32,4,8,128]{3,2,1,0:T(8,128)(2,1)S(1)}, u32[]{:S(2)}, u32[]{:S(2)}) async-start(bf16[32,4,8,128]{3,2,1,0:T(8,128)(2,1)} %bitcast.27), calls=%async_computation.1 | async-start | bytes 524288 | tf_op jit(solution)/shard_map/all_to_all | solution.py:475
  103.5 31.4 %copy-start.6 = (s32[2,8,128,128]{3,2,1,0:T(8,128)S(1)}, s32[2,8,128,128]{3,2,1,0:T(8,128)}, u32[]{:S(2)}) copy-start(s32[2,8,128,128]{3,2,1,0:T(8,128)} %mask.3) | copy-start | bytes 3145732
  103.5 31.4 %copy-start.10 = (bf16[256,768]{1,0:T(8,128)(2,1)S(1)}, bf16[256,768]{1,0:T(8,128)(2,1)}, u32[]{:S(2)}) copy-start(bf16[256,768]{1,0:T(8,128)(2,1)} %constant.23.clone.left_back) | copy-start | bytes 1179652
  103.5 31.4 %copy-start.12 = (bf16[768,256]{1,0:T(8,128)(2,1)S(1)}, bf16[768,256]{1,0:T(8,128)(2,1)}, u32[]{:S(2)}) copy-start(bf16[768,256]{1,0:T(8,128)(2,1)} %constant.24.clone.right_back) | copy-start | bytes 1179652
  127.0 5.8 %copy-start.13 = (bf16[32,4,8,128]{3,2,1,0:T(8,128)(2,1)}, bf16[32,4,8,128]{3,2,1,0:T(8,128)(2,1)S(1)}, u32[]{:S(2)}) copy-start(bf16[32,4,8,128]{3,2,1,0:T(8,128)(2,1)S(1)} %all-to-all-done.1) | copy-start | bytes 786436
  127.0 26.8 %all-to-all-start.3 = ((bf16[32,4,8,128]{3,2,1,0:T(8,128)(2,1)}), bf16[32,4,8,128]{3,2,1,0:T(8,128)(2,1)}, u32[]{:S(2)}, u32[]{:S(2)}) async-start(bf16[32,4,8,128]{3,2,1,0:T(8,128)(2,1)} %bitcast.26), calls=%async_computation.3 | async-start | bytes 524288 | tf_op jit(solution)/shard_map/all_to_all | solution.py:475
  134.9 1.0 copy-start
  153.0 0.8 copy-start.3

commit v2 on v1

v2 whole, which is shorter than its diff:
```python
import functools
import math

import jax
import jax.numpy as jnp
import numpy as np
from jax import lax
from jax.experimental import pallas as pl
from jax.experimental.pallas import tpu as pltpu
from jax.sharding import PartitionSpec as P

ETA = 0.5
RIDGE = 0.0001
AXES = ("readout", "frame")
F32 = jnp.float32
BF16 = jnp.bfloat16
VMEM = pl.BlockSpec(memory_space=pltpu.VMEM)
GROUP = 4
WIDE = 16
LAST = 8


class Plan:
    def __init__(self, devices_x, devices_t, frames, width, ny, nz, channels):
        self.R, self.F, self.tl, self.xl = devices_x, devices_t, frames, width
        self.ny, self.nz, self.ch = ny, nz, channels
        self.D = devices_x * devices_t
        self.T, self.X = frames * devices_t, width * devices_x
        self.zl = nz // self.D
        self.nzb = min(4, self.zl)
        self.NZB = self.zl // self.nzb
        self.L = self.nzb * ny
        self.unit = frames * 2 * width
        self.rows = self.X * channels
        self.M = GROUP * channels
        self.G = self.X // GROUP
        if self.G == 1:
            self.W, self.ws = self.M, [0]
        else:
            self.W = self.M + 32 if self.G == 2 else self.M + 64
            self.ws = [min(max(self.M * g - 32, 0), self.rows - self.W) for g in range(self.G)]
        self.quad = 2 * width
        self.GI = self.X // WIDE
        near = WIDE // width
        extra = 0 if self.GI == 1 else 4
        self.RW = near + extra
        self.UW = self.RW * self.quad
        self.us = [min(max(near * g - extra // 2, 0), devices_x - near - extra) for g in range(self.GI)]
        self.GL = self.X // LAST
        self.near = LAST // width
        wide = LAST * channels
        self.KW = min(wide + (32 if self.GL == 2 else 64), self.rows)
        self.ks = [min(max(wide * g - 32, 0), self.rows - self.KW) for g in range(self.GL)]
        self.part = 6 * self.near * self.unit

    def mid_table(self, g):
        k = np.arange(3 * self.W)
        row = self.ws[g] + k % self.W
        return pack(k // self.W * self.ch + row % self.ch, row // self.ch)

    def in_table(self, g, t2):
        k = np.arange((self.tl + 2) * 3 * self.UW)
        slot, c, rest = k // (3 * self.UW), k // self.UW % 3, k % self.UW
        part, x2, r = rest // (self.xl * self.RW), rest // self.RW % self.xl, self.us[g] + rest % self.RW
        a = slot - t2
        q = np.where((a >= 0) & (a <= 2), (a * 3 + c) * 2 + part, -1)
        return pack(q, r * self.xl + x2)

    def out_rows(self, g, s):
        m = np.arange(2 * 3 * self.near * self.unit)
        target, rest = m // (3 * self.near * self.unit), m % (3 * self.near * self.unit)
        c, rest = rest // (self.near * self.unit), rest % (self.near * self.unit)
        r, rest = self.near * g + rest // self.unit, rest % self.unit
        frame, part, x2 = rest // (2 * self.xl), rest // self.xl % 2, rest % self.xl
        offset = self.tl if s == 0 else -self.tl
        a = s - frame + 1 + np.where(target == 1, offset, 0)
        q = np.where((a >= 0) & (a <= 2), (a * 3 + c) * 2 + part, -1)
        pick = (q[:, None] == np.arange(24)[None, :]).astype(np.float32).astype(BF16)
        return pick, (r * self.xl + x2).astype(np.int32)

    def out_cols(self, g):
        row = self.ks[g] + np.arange(self.KW)
        return pack(row % self.ch, row // self.ch)


def pack(q, position):
    return np.stack([q, position] + [np.zeros_like(q)] * 6).astype(np.int32)


def dot(a, b):
    return jnp.dot(a, b, preferred_element_type=F32)


def one_hot_rows(table, rows, first=0):
    k = table.shape[1]
    index = lax.broadcasted_iota(jnp.int32, (rows, k), 0) + first
    return (index == jnp.broadcast_to(table[0:1, :], (rows, k))).astype(F32).astype(BF16)


def banded(weights, table, first, count, channels, out_ref, where, row0):
    spread = dot(weights, one_hot_rows(table, weights.shape[1]))
    parts = [spread[b * channels : (b + 1) * channels] for b in range(3)]
    position = table[1:2, :]
    for pair in range(count // 2):
        rows = []
        for x in (first + 2 * pair, first + 2 * pair + 1):
            rows.append(
                jnp.where(
                    position == x - 1,
                    parts[0],
                    jnp.where(position == x, parts[1], jnp.where(position == x + 1, parts[2], 0.0)),
                )
            )
        out_ref[where, row0 + 2 * pair * channels : row0 + 2 * (pair + 1) * channels, :] = jnp.concatenate(
            rows, axis=0
        ).astype(BF16)


def banded_taps(raw, flipped, table, first, channels, out_ref, where, scale):
    order = [26 - n if flipped else n for n in range(27)]
    spread = None
    for c in range(3):
        stack = jnp.concatenate([raw[order[ab * 3 + c]].astype(F32) for ab in range(9)], axis=0).astype(BF16)
        part = dot(stack, one_hot_rows(table, channels, c * channels))
        spread = part if spread is None else spread + part
    position = table[1:2, :]
    for a in range(3):
        parts = [spread[(a * 3 + b) * channels : (a * 3 + b + 1) * channels] * scale for b in range(3)]
        for pair in range(GROUP // 2):
            rows = []
            for x in (first + 2 * pair, first + 2 * pair + 1):
                rows.append(
                    jnp.where(
                        position == x - 1,
                        parts[0],
                        jnp.where(position == x, parts[1], jnp.where(position == x + 1, parts[2], 0.0)),
                    )
                )
            at = (a * GROUP + 2 * pair) * channels
            out_ref[where, at : at + 2 * channels, :] = jnp.concatenate(rows, axis=0).astype(BF16)


def weights_kernel(
    p, w_in, w_mid, w_out, b_mid, b_in, mid_tab, in_tab, pick, row_x, col_tab, m_in, m_out, m_mid, m_back, m_last
):
    for g in range(p.G):
        table = mid_tab[g]
        banded_taps(w_mid, False, table, g * GROUP, p.ch, m_mid, g, 0.5)
        banded_taps(b_mid, True, table, g * GROUP, p.ch, m_back, g, 1.0)
    for g in range(p.GI):
        for t2 in range(p.tl):
            table = in_tab[g, t2]
            banded(w_in[...], table, g * WIDE, WIDE, p.ch, m_in, g, t2 * WIDE * p.ch)
            banded(w_out[...], table, g * WIDE, WIDE, p.ch, m_out, g, t2 * WIDE * p.ch)
    for g in range(p.GL):
        cols = col_tab[g]
        place = one_hot_rows(cols, p.ch)
        position = cols[1:2, :]
        taps = [dot(b_in[b], place).astype(BF16) for b in range(3)]
        for s in range(p.tl):
            x = row_x[g, s]
            total = jnp.zeros((x.shape[0], p.KW), F32)
            for b in range(3):
                total = jnp.where(position == x + (b - 1), dot(pick[g, s], taps[b]), total)
            m_last[g, s] = total.astype(BF16)


def shifted(value, c, ny):
    if c == 1:
        return value
    pieces = []
    for at in range(0, value.shape[1], ny):
        piece = value[:, at : at + ny]
        lane = lax.broadcasted_iota(jnp.int32, piece.shape, 1)
        if c == 0:
            pieces.append(jnp.where(lane == 0, jnp.zeros_like(piece), pltpu.roll(piece, 1, 1)))
        else:
            pieces.append(jnp.where(lane == ny - 1, jnp.zeros_like(piece), pltpu.roll(piece, ny - 1, 1)))
    return pieces[0] if len(pieces) == 1 else jnp.concatenate(pieces, axis=1)


def silu_of_half(half):
    double = 1.0 + jnp.tanh(half)
    value = half * double
    sigma = 0.5 * double
    return value, sigma + value * (1.0 - sigma)


def gather_field(p, load, u_ref, row_ref):
    for f in range(p.F):
        for j in range(p.nzb):
            row_ref[f, j] = load(f, j).reshape(p.R * p.unit, p.ny)
        for t2 in range(p.tl):
            lines = []
            for k in range(p.quad):
                start = t2 * p.quad + k
                line = [row_ref[f, j, pl.ds(start, p.R, stride=p.unit), :] for j in range(p.nzb)]
                lines.append(line[0] if p.nzb == 1 else jnp.concatenate(line, axis=1))
            for g in range(p.GI):
                value = jnp.concatenate([line[p.us[g] : p.us[g] + p.RW] for line in lines], axis=0).astype(BF16)
                for c in range(3):
                    start = ((f * p.tl + t2 + 1) * 3 + c) * p.UW
                    u_ref[g, start : start + p.UW, :] = shifted(value, c, p.ny)


def put_window(p, h_ref, g, t, value):
    value = value.astype(BF16)
    for c in range(3):
        moved = shifted(value, c, p.ny)
        for h in range(p.G):
            lo, hi = max(p.M * g, p.ws[h]), min(p.M * (g + 1), p.ws[h] + p.W)
            if lo < hi:
                start = c * p.W + lo - p.ws[h]
                h_ref[h, t, start : start + hi - lo, :] = moved[lo - p.M * g : hi - p.M * g]


def first_layer(p, matrix, u_ref, d_ref, each):
    def issue(f):
        start = pl.multiple_of(f * (p.tl * 3 * p.UW), 16)
        size = (p.tl + 2) * 3 * p.UW
        for gi in range(p.GI):
            d_ref[gi] = dot(matrix[gi], u_ref[gi, pl.ds(start, size), :])

    def finish(f):
        for gi in range(p.GI):
            for t2 in range(p.tl):
                for at in range(WIDE // GROUP):
                    row = (t2 * WIDE + at * GROUP) * p.ch
                    each(f * p.tl + t2, gi * (WIDE // GROUP) + at, d_ref[gi, row : row + p.M, :])

    def body(f, carry):
        finish(f - 1)
        issue(f)
        return carry

    issue(0)
    lax.fori_loop(1, p.F, body, 0)
    finish(p.F - 1)


def middle_layer(p, matrix, h_ref, d_ref, run_ref, each):
    run_ref[...] = jnp.zeros_like(run_ref)

    def issue(t):
        for g in range(p.G):
            d_ref[g] = dot(matrix[g], h_ref[g, t])

    def finish(t):
        for g in range(p.G):
            each(jnp.maximum(t - 1, 0), g, run_ref[g, 0] + d_ref[g, 2 * p.M :, :])
            run_ref[g, 0] = run_ref[g, 1] + d_ref[g, p.M : 2 * p.M, :]
            run_ref[g, 1] = d_ref[g, : p.M, :]

    def body(t, carry):
        finish(t - 1)
        issue(t)
        return carry

    issue(0)
    lax.fori_loop(1, p.T, body, 0)
    finish(p.T - 1)
    for g in range(p.G):
        each(p.T - 1, g, run_ref[g, 0])


def last_layer(p, matrix, g_ref, l_ref, acc_ref):
    acc_ref[...] = jnp.zeros_like(acc_ref)
    size = p.near * p.unit

    def issue(f):
        for g in range(p.GL):
            for s in range(p.tl):
                l_ref[g, s] = dot(matrix[g, s], g_ref[f * p.tl + s, pl.ds(p.ks[g], p.KW), :])

    def finish(f):
        for g in range(p.GL):
            for s in range(p.tl):
                for target in range(2):
                    slot = f + 1 if target == 0 else (f if s == 0 else f + 2)
                    first = target * 3 * size
                    value = l_ref[g, s, first + size : first + 2 * size, :]
                    for c in (0, 2):
                        value = value + shifted(l_ref[g, s, first + c * size : first + (c + 1) * size, :], c, p.ny)
                    acc_ref[slot, pl.ds(g * size, size), :] += value

    def body(f, carry):
        finish(f - 1)
        issue(f)
        return carry

    issue(0)
    lax.fori_loop(1, p.F, body, 0)
    finish(p.F - 1)


def backward(p, zb, load, m_out, m_back, m_last, slope_one, slope_two, back, u_ref, h_ref, g_ref, acc_ref, run_ref, d_ref, e_ref, row_ref, l_ref):
    gather_field(p, load, u_ref, row_ref)

    def after_out(t, g, value):
        rows = pl.ds(p.M * g, p.M)
        put_window(p, h_ref, g, t, slope_two[zb, t, rows, :].astype(F32) * value)

    first_layer(p, m_out, u_ref, d_ref, after_out)

    def after_mid(t, g, value):
        rows = pl.ds(p.M * g, p.M)
        g_ref[t, rows, :] = (slope_one[zb, t, rows, :].astype(F32) * value).astype(BF16)

    middle_layer(p, m_back, h_ref, e_ref, run_ref, after_mid)
    last_layer(p, m_last, g_ref, l_ref, acc_ref)
    for f in range(p.F):
        for j in range(p.nzb):
            value = acc_ref[f + 1, :, j * p.ny : (j + 1) * p.ny].reshape(p.R, p.unit, p.ny)
            back[:, f, zb * p.nzb + j, :, :] = value.astype(BF16)


def clear_edges(p, u_ref):
    u_ref[:, : 3 * p.UW, :] = jnp.zeros((p.GI, 3 * p.UW, p.L), BF16)
    u_ref[:, (p.T + 1) * 3 * p.UW :, :] = jnp.zeros((p.GI, 3 * p.UW, p.L), BF16)


def both_kernel(
    p, got, bias_one, bias_two, m_in, m_out, m_mid, m_back, m_last,
    slope_one, slope_two, back, u_ref, h_ref, g_ref, acc_ref, run_ref, d_ref, e_ref, row_ref, l_ref,
):
    clear_edges(p, u_ref)

    def block(zb, carry):
        def load(which, f, j):
            value = got[:, f, zb * p.nzb + j, :, :].astype(F32)
            return value[:, which * p.unit : (which + 1) * p.unit]

        gather_field(p, functools.partial(load, 0), u_ref, row_ref)

        def after_in(t, g, value):
            hidden, slope = silu_of_half(value + bias_one[...])
            slope_one[zb, t, pl.ds(p.M * g, p.M), :] = slope.astype(BF16)
            put_window(p, h_ref, g, t, hidden)

        first_layer(p, m_in, u_ref, d_ref, after_in)

        def after_mid(t, g, value):
            _, slope = silu_of_half(value + bias_two[...])
            slope_two[zb, t, pl.ds(p.M * g, p.M), :] = slope.astype(BF16)

        middle_layer(p, m_mid, h_ref, e_ref, run_ref, after_mid)
        backward(
            p, zb, functools.partial(load, 1), m_out, m_back, m_last,
            slope_one, slope_two, back, u_ref, h_ref, g_ref, acc_ref, run_ref, d_ref, e_ref, row_ref, l_ref,
        )
        return carry

    lax.fori_loop(0, p.NZB, block, 0)


def back_kernel(
    p, got, before, m_out, m_back, m_last, slope_one, slope_two, back, u_ref, h_ref, g_ref, acc_ref, run_ref, d_ref, e_ref, row_ref, l_ref
):
    clear_edges(p, u_ref)

    def block(zb, carry):
        def load(f, j):
            at = zb * p.nzb + j
            return got[:, f, at, :, :].astype(F32) - before[:, f, at, :, :].astype(F32)

        backward(p, zb, load, m_out, m_back, m_last, slope_one, slope_two, back, u_ref, h_ref, g_ref, acc_ref, run_ref, d_ref, e_ref, row_ref, l_ref)
        return carry

    lax.fori_loop(0, p.NZB, block, 0)


def planes(p):
    for t2 in range(p.tl):
        for part in range(2):
            for x2 in range(p.xl):
                yield (t2 * 2 + part) * p.xl + x2, (part, t2, x2)


def pack_kernel(p, equilibrium, cotangent, out, turned, scratch):
    total = 2 * p.unit
    for row, at in planes(p):
        scratch[pl.ds(row, p.nz, stride=total), :] = equilibrium[at].T
        plane = cotangent[at].T
        turned[at] = plane
        scratch[pl.ds(p.unit + row, p.nz, stride=total), :] = plane
    out[...] = scratch[...].reshape(p.nz, total, p.ny).astype(BF16)


def finish_kernel(p, field, got, first, cotangent, out, gram, scratch):
    scratch[...] = got[...].astype(F32).reshape(p.nz * p.unit, p.ny)
    sums = [jnp.zeros((1, p.ny), F32) for _ in range(3)]
    for row, at in planes(p):
        mapped = field[at] - scratch[pl.ds(row, p.nz, stride=p.unit), :]
        out[at] = mapped
        old = first[at] - cotangent[at]
        new = mapped - first[at]
        for n, product in enumerate((old * old, new * old, new * new)):
            sums[n] = sums[n] + jnp.sum(product, axis=0, keepdims=True)
    lane = lax.broadcasted_iota(jnp.int32, (1, 128), 1)
    line = jnp.zeros((1, 128), F32)
    for n in range(3):
        line = jnp.where(lane == n, jnp.sum(sums[n], axis=1, keepdims=True), line)
    gram[...] = jnp.broadcast_to(line[None], gram.shape)


def small_solve(lines, values):
    order = len(values)
    lines = [list(line) for line in lines]
    values = list(values)
    for column in range(order):
        for line in range(column + 1, order):
            factor = lines[line][column] / lines[column][column]
            lines[line] = [a - factor * b for a, b in zip(lines[line], lines[column])]
            values[line] = values[line] - factor * values[column]
    solution = [None] * order
    for line in reversed(range(order)):
        running = values[line]
        for column in range(line + 1, order):
            running = running - lines[line][column] * solution[column]
        solution[line] = running / lines[line][line]
    return solution


def mix_kernel(gathered, first, second, out):
    total = jnp.sum(gathered[...], axis=0)
    g00, g10, g11 = (total[:, n : n + 1] for n in range(3))
    ridge = RIDGE * (g00 + g11) / 2
    one = jnp.ones_like(g00)
    solution = small_solve([[g00 + ridge, g10], [g10, g11 + ridge]], [one, one])
    whole = solution[0] + solution[1]
    alpha = [value / whole for value in solution]
    for part in range(out.shape[0]):
        for t in range(out.shape[1]):
            for x in range(out.shape[2]):
                at = (part, t, x)
                out[at] = (alpha[0] * first[at] + alpha[1] * second[at]).T


def dft_table(length, sign):
    index = np.arange(length)
    angle = 2.0 * math.pi / length * (index[:, None] * index[None, :] % length)
    cosine, sine = np.cos(angle) / math.sqrt(length), sign * np.sin(angle) / math.sqrt(length)
    table = np.block([[cosine, -sine], [sine, cosine]]).astype(np.float32)
    high = table.astype(BF16)
    low = (table - high.astype(np.float32)).astype(BF16)
    return np.concatenate([high, high, low], axis=0)


def transform(value, table):
    high = value.astype(BF16)
    low = (value - high.astype(F32)).astype(BF16)
    return dot(jnp.concatenate([high, low, high], axis=1), table[...])


def turned_images(value, count, rows, columns):
    images = []
    for n in range(count):
        image = value[n * rows : (n + 1) * rows]
        images.append(jnp.concatenate([image[:, :columns].T, image[:, columns:].T], axis=1))
    return jnp.concatenate(images, axis=0)


def normal_sum(real, imag, sens, mask, tables):
    forward_y, forward_z, inverse_z, inverse_y = tables
    coils, nz, ny = sens.shape[1], sens.shape[3], sens.shape[4]
    total_real, total_imag = jnp.zeros((nz, ny), F32), jnp.zeros((nz, ny), F32)
    count = math.gcd(coils, 4)
    groups = [range(first, first + count) for first in range(0, coils, count)]
    values, keeps = [], []
    for group in groups:
        lines, keep = [], []
        for c in group:
            s_real, s_imag = sens[0, c, 0], sens[1, c, 0]
            lines.append(jnp.concatenate([s_real * real - s_imag * imag, s_real * imag + s_imag * real], axis=1))
            line = mask[0, c].astype(F32)
            keep.append(jnp.concatenate([line, line], axis=1))
        values.append(jnp.concatenate(lines, axis=0))
        keeps.append(jnp.concatenate(keep, axis=0))
    values = [transform(value, forward_y) for value in values]
    values = [transform(turned_images(value, count, nz, ny), forward_z) for value in values]
    values = [transform(value * keep, inverse_z) for value, keep in zip(values, keeps)]
    values = [transform(turned_images(value, count, ny, nz), inverse_y) for value in values]
    for group, value in zip(groups, values):
        for n, c in enumerate(group):
            s_real, s_imag = sens[0, c, 0], sens[1, c, 0]
            z_real, z_imag = value[n * nz : (n + 1) * nz, :ny], value[n * nz : (n + 1) * nz, ny:]
            total_real += s_real * z_real + s_imag * z_imag
            total_imag += s_real * z_imag - s_imag * z_real
    return total_real, total_imag


def first_normal_kernel(
    p, cotangent, sens, mask, forward_y, forward_z, inverse_z, inverse_y, point, turned, packed, scratch
):
    x, t = pl.program_id(0), pl.program_id(1)

    @pl.when(t == 0)
    def _():
        for part in range(2):
            for c in range(sens.shape[1]):
                turned[part, c, 0] = sens[part, c, 0].T

    real, imag = cotangent[0, 0, 0], cotangent[1, 0, 0]
    sums = normal_sum(real, imag, turned, mask, (forward_y, forward_z, inverse_z, inverse_y))
    for part, (value, total) in enumerate(zip((real, imag), sums)):
        value = value + value - ETA * total
        point[part, 0, 0] = value
        scratch[pl.ds((t * 2 + part) * p.xl + x, p.nz, stride=p.unit), :] = value

    @pl.when((x == p.xl - 1) & (t == p.tl - 1))
    def _():
        packed[...] = scratch[...].reshape(p.nz, p.unit, p.ny).astype(BF16)


def next_normal_kernel(
    p, point, returned, cotangent, sens, mask, forward_y, forward_z, inverse_z, inverse_y, field, out, scratch
):
    x, t = pl.program_id(0), pl.program_id(1)

    @pl.when((x == 0) & (t == 0))
    def _():
        scratch[...] = returned[...].astype(F32).reshape(p.nz * p.unit, p.ny)

    values = []
    for part in range(2):
        plane = scratch[pl.ds((t * 2 + part) * p.xl + x, p.nz, stride=p.unit), :]
        values.append(point[part, 0, 0] - plane)
        field[part, 0, 0] = values[part]
    sums = normal_sum(values[0], values[1], sens, mask, (forward_y, forward_z, inverse_z, inverse_y))
    for part, (value, total) in enumerate(zip(values, sums)):
        out[part, 0, 0] = cotangent[part, 0, 0] + value - ETA * total


def normal_call(p, kernel, args, specs, outs, out_specs, name, coils):
    return pl.pallas_call(
        functools.partial(kernel, p),
        grid=(p.xl, p.tl),
        in_specs=specs,
        out_specs=out_specs,
        out_shape=[jax.ShapeDtypeStruct(shape, kind) for shape, kind in outs],
        scratch_shapes=[pltpu.VMEM((p.nz * p.unit, p.ny), F32)],
        compiler_params=pltpu.CompilerParams(vmem_limit_bytes=48 << 20),
        cost_estimate=pl.CostEstimate(
            flops=p.xl * p.tl * coils * 4 * 3 * 2 * 2 * p.ny * p.nz * 2 * p.nz,
            bytes_accessed=20 << 20,
            transcendentals=0,
        ),
        name=name,
    )(*args)


def call(kernel, outs, args, name, scratch=(), flops=1 << 20, moved=4 << 20):
    shapes = [jax.ShapeDtypeStruct(shape, kind) for shape, kind in outs]
    single = len(shapes) == 1
    return pl.pallas_call(
        kernel,
        in_specs=[VMEM] * len(args),
        out_specs=VMEM if single else [VMEM] * len(shapes),
        out_shape=shapes[0] if single else shapes,
        scratch_shapes=list(scratch),
        compiler_params=pltpu.CompilerParams(vmem_limit_bytes=60 << 20),
        cost_estimate=pl.CostEstimate(flops=flops, bytes_accessed=moved, transcendentals=0),
        name=name,
    )(*args)


def flip_kernel(weight):
    return jnp.transpose(jnp.flip(weight, (2, 3, 4)), (1, 0, 2, 3, 4))


def by_offset(weight):
    outs, ins = weight.shape[:2]
    return jnp.transpose(weight, (3, 0, 2, 4, 1)).reshape(3 * outs, 9 * ins)


def exchange(blocks):
    return lax.all_to_all(blocks, AXES, 0, 0, tiled=True)


def per_device(
    equilibrium, cotangent, sensitivity, sampling, weight_in, bias_in, weight_mid, bias_mid, weight_out
):
    _, frames, width, ny, nz = cotangent.shape
    p = Plan(lax.axis_size("readout"), lax.axis_size("frame"), frames, width, ny, nz, weight_in.shape[0])
    coils = sensitivity.shape[1]
    turned_shape = (2, frames, width, nz, ny)
    z_shape = (p.R, p.F, p.zl, p.unit, ny)
    tables = [
        jnp.asarray(dft_table(ny, 1.0)),
        jnp.asarray(dft_table(nz, 1.0)),
        jnp.asarray(dft_table(nz, -1.0)),
        jnp.asarray(dft_table(ny, -1.0)),
    ]
    if ny == nz:
        tables[1], tables[3] = tables[0], tables[2]
    image = pl.BlockSpec((2, 1, 1, nz, ny), lambda x, t: (0, t, x, 0, 0))
    lines = pl.BlockSpec((nz, p.unit, ny), lambda x, t: (0, 0, 0))
    maps = pl.BlockSpec((2, coils, 1, ny, nz), lambda x, t: (0, 0, x, 0, 0))
    turned_maps = pl.BlockSpec((2, coils, 1, nz, ny), lambda x, t: (0, 0, x, 0, 0))
    masks = pl.BlockSpec((1, coils, ny, nz), lambda x, t: (t, 0, 0, 0))
    whole = [pl.BlockSpec(table.shape, lambda x, t: (0, 0)) for table in tables]

    packed, turned = call(
        functools.partial(pack_kernel, p),
        [((nz, 2 * p.unit, ny), BF16), (turned_shape, F32)],
        (equilibrium, cotangent),
        "pack",
        [pltpu.VMEM((nz * 2 * p.unit, ny), F32)],
    )
    got = exchange(packed.reshape(p.D, p.zl, 2 * p.unit, ny)).reshape(p.R, p.F, p.zl, 2 * p.unit, ny)

    picks = [[p.out_rows(g, s) for s in range(p.tl)] for g in range(p.GL)]
    back_in = flip_kernel(weight_in)
    last = jnp.transpose(back_in, (3, 2, 4, 0, 1)).reshape(3, 18, p.ch)
    last = jnp.pad(last, ((0, 0), (0, 6), (0, 0)))
    weight_args = [
        by_offset(weight_in) * jnp.asarray(0.5, BF16),
        jnp.transpose(weight_mid, (2, 3, 4, 0, 1)).reshape(27, p.ch, p.ch),
        by_offset(flip_kernel(weight_out)),
        jnp.transpose(weight_mid, (2, 3, 4, 1, 0)).reshape(27, p.ch, p.ch),
        last,
        jnp.asarray(np.stack([p.mid_table(g) for g in range(p.G)])),
        jnp.asarray(np.stack([np.stack([p.in_table(g, s) for s in range(p.tl)]) for g in range(p.GI)])),
        jnp.asarray(np.stack([np.stack([pick for pick, _ in line]) for line in picks])),
        jnp.asarray(np.stack([np.stack([x[:, None] for _, x in line]) for line in picks])),
        jnp.asarray(np.stack([p.out_cols(g) for g in range(p.GL)])),
    ]
    in_shape = (p.GI, p.tl * WIDE * p.ch, (p.tl + 2) * 3 * p.UW)
    mid_shape = (p.G, 3 * p.M, 3 * p.W)
    last_shape = (p.GL, p.tl, p.part, p.KW)
    m_in, m_out, m_mid, m_back, m_last = call(
        functools.partial(weights_kernel, p),
        [(in_shape, BF16), (in_shape, BF16), (mid_shape, BF16), (mid_shape, BF16), (last_shape, BF16)],
        weight_args,
        "weights",
    )
    bias_one = jnp.broadcast_to(jnp.tile(0.5 * bias_in, GROUP)[:, None], (p.M, p.L))
    bias_two = jnp.broadcast_to(jnp.tile(0.5 * bias_mid, GROUP)[:, None], (p.M, p.L))

    point, turned_sens, packed = normal_call(
        p,
        first_normal_kernel,
        [turned, sensitivity, sampling, *tables],
        [image, maps, masks, *whole],
        [(turned_shape, F32), ((2, coils, width, nz, ny), F32), ((nz, p.unit, ny), BF16)],
        [image, turned_maps, lines],
        "normal_one",
        coils,
    )
    got_point = exchange(packed.reshape(p.D, p.zl, p.unit, ny)).reshape(z_shape)

    slope = ((p.NZB, p.T, p.rows, p.L), BF16)
    scratch = [
        pltpu.VMEM((p.GI, (p.T + 2) * 3 * p.UW, p.L), BF16),
        pltpu.VMEM((p.G, p.T, 3 * p.W, p.L), BF16),
        pltpu.VMEM((p.T, p.rows, p.L), BF16),
        pltpu.VMEM((p.F + 2, p.R * p.unit, p.L), F32),
        pltpu.VMEM((p.G, 2, p.M, p.L), F32),
        pltpu.VMEM((p.GI, p.tl * WIDE * p.ch, p.L), F32),
        pltpu.VMEM((p.G, 3 * p.M, p.L), F32),
        pltpu.VMEM((p.F, p.nzb, p.R * p.unit, ny), F32),
        pltpu.VMEM((p.GL, p.tl, p.part, p.L), F32),
    ]
    work = 2 * p.NZB * p.T * p.L * p.rows * 9 * p.W
    slope_one, slope_two, back = call(
        functools.partial(both_kernel, p),
        [slope, slope, (z_shape, BF16)],
        [got, bias_one, bias_two, m_in, m_out, m_mid, m_back, m_last],
        "both",
        scratch,
        3 * work,
        16 << 20,
    )
    returned = exchange(back.reshape(p.D, p.zl, p.unit, ny)).reshape(nz, p.unit, ny)
    back_two = call(
        functools.partial(back_kernel, p),
        [(z_shape, BF16)],
        [got_point, back, m_out, m_back, m_last, slope_one, slope_two],
        "back",
        scratch,
        3 * work // 2,
        12 << 20,
    )
    returned_two = exchange(back_two.reshape(p.D, p.zl, p.unit, ny)).reshape(nz, p.unit, ny)
    first, point_two = normal_call(
        p,
        next_normal_kernel,
        [point, returned, turned, turned_sens, sampling, *tables],
        [image, lines, image, turned_maps, masks, *whole],
        [(turned_shape, F32), (turned_shape, F32)],
        [image, image],
        "normal_two",
        coils,
    )
    second, gram = call(
        functools.partial(finish_kernel, p),
        [(turned_shape, F32), ((p.D, 1, 128), F32)],
        [point_two, returned_two, first, turned],
        "finish",
        [pltpu.VMEM((nz * p.unit, ny), F32)],
    )
    return call(mix_kernel, [(cotangent.shape, F32)], [exchange(gram), first, second], "mix")


def solution(mesh):
    placed = (
        P(None, "frame", "readout", None, None),
        P(None, "frame", "readout", None, None),
        P(None, None, "readout", None, None),
        P("frame", None, None, None),
        P(),
        P(),
        P(),
        P(),
        P(),
    )
    return jax.shard_map(
        per_device,
        mesh=mesh,
        in_specs=placed,
        out_specs=P(None, "frame", "readout", None, None),
        check_vma=False,
    )
```

time: 173 us -> 125 us (0.72)
  Pallas kernels: 115 us -> 77.6 us
  local copies, waits for them, and re-layouts: 19 us -> 8.5 us
    pallas_call x8 -> x6, Pallas kernels: 82.2 us -> 55.6 us  [call(): pl.pallas_call(kernel, in_specs=[VMEM] * len(args), out_specs=VMEM if sin...]
    pallas_call x2, Pallas kernels: 32.9 us -> 22 us  [normal_call(): pl.pallas_call(functools.partial(kernel, p), grid=(p.xl, p.tl), in_specs=...]
    reshape x6 -> x2, local copies, waits for them, and re-layouts: 5.05 us -> 0.79 us  [by_offset(): return jnp.transpose(weight, (3, 0, 2, 4, 1)).reshape(3 * outs, 9 * ins)]
    another operation x4 -> x2, local copies, waits for them, and re-layouts: 3.36 us -> 0.02 us  [by_offset(): return jnp.transpose(weight, (3, 0, 2, 4, 1)).reshape(3 * outs, 9 * ins)]
    unnamed x38 -> x28, local copies, waits for them, and re-layouts: 5.88 us -> 3.74 us
  transfers between devices with their start and end apart: 4 -> 4, of which waited for: 0 -> 0; matrix products, arithmetic and copies ran while one was open for 7% -> 4% of each run, Pallas kernels for 62% -> 56%
where the time goes in v2:
time: 125 us; the launch traced here: 124 us
  Pallas kernels  77.6 us (62%)
  starting transfers between devices  25.1 us (20%)
  blocking collectives  12.9 us (10%)
  local copies, waits for them, and re-layouts  8.5 us (7%)
    pallas_call x6, Pallas kernels, call(): pl.pallas_call(kernel, in_specs=[VMEM] * len(args), out_specs=VMEM if sin...  55.6 us
    all_to_all x4, starting transfers between devices, exchange(): return lax.all_to_all(blocks, AXES, 0, 0, tiled=True)  25.1 us
    pallas_call x2, Pallas kernels, normal_call(): pl.pallas_call(functools.partial(kernel, p), grid=(p.xl, p.tl), in_specs=...  22 us
    all_to_all x1, blocking collectives, exchange(): return lax.all_to_all(blocks, AXES, 0, 0, tiled=True)  12.9 us
    unnamed x28, local copies, waits for them, and re-layouts  3.74 us
  transfers between devices with their start and end apart: 4, of which 0 were waited for; matrix products, arithmetic and copies ran while one was open for 4% of the time, Pallas kernels for 56%

profile of v2, /device:TPU:0, one launch (start us, length us, event | category | flops | bytes accessed | tf_op | source)
XLA Modules:
  0.0 124.4 jit_solution(6834351119225527632)
XLA Ops:
  0.0 2.8 %pack.1 = (bf16[128,16,128]{2,1,0:T(8,128)(2,1)}, f32[2,2,2,128,128]{4,3,2,1,0:T(8,128)}) custom-call(f32[2,2,2,128,128]{4,3,2,1,0:T(8,128)} %equilibrium.1, f32[2,2,2,128,128]{4,3,2,1,0:T(8,128)} %cotangent.1), custom_call_target="tpu_custom_call" | custom-call | flops 1048576 | bytes 4194304 | tf_op jit(solution)/shard_map/pack/pallas_call | solution.py:555
  2.8 7.5 %all-to-all-start = ((bf16[32,4,16,128]{3,2,1,0:T(8,128)(2,1)}), bf16[32,4,16,128]{3,2,1,0:T(8,128)(2,1)}, u32[]{:S(2)}, u32[]{:S(2)}) async-start(bf16[32,4,16,128]{3,2,1,0:T(8,128)(2,1)} %bitcast.28), calls=%async_computation | async-start | bytes 1048576 | tf_op jit(solution)/shard_map/all_to_all | solution.py:577
  10.4 0.1 mul.21
  10.5 0.7 copy.25.w_in
  11.2 0.8 copy.23
  12.0 0.1 reshape.46
  12.1 0.7 copy.26.w_out
  12.8 0.1 broadcast_in_dim.14
  12.9 0.1 broadcast_in_dim.16
  13.0 0.6 pad.4.b_in
  13.6 5.3 %weights.1 = (bf16[1,768,384]{2,1,0:T(8,128)(2,1)}, bf16[1,768,384]{2,1,0:T(8,128)(2,1)}, bf16[4,288,480]{2,1,0:T(8,128)(2,1)}, bf16[4,288,480]{2,1,0:T(8,128)(2,1)}, bf16[2,2,192,224]{3,2,1,0:T(8,128)(2,1)}) custom-call(bf16[72,18]{1,0:T(8,128)(2,1)} %copy.25.w_in, bf16[27,24,24]{2,1,0:T(8,128)(2,1)} %bitcast.25, bf16[72,18]{1,0:T(8,128)(2,1)} %copy.26.w_out, ...), custom_call_target="tpu_custom_call" | custom-call | flops 1048576 | bytes 4194304 | tf_op jit(solution)/shard_map/weights/pallas_call | solution.py:555
  18.9 0.0 copy-done.5
  19.0 11.7 %normal_one.1 = (f32[2,2,2,128,128]{4,3,2,1,0:T(8,128)S(1)}, f32[2,8,2,128,128]{4,3,2,1,0:T(8,128)S(1)}, bf16[128,8,128]{2,1,0:T(8,128)(2,1)}) custom-call(f32[2,2,2,128,128]{4,3,2,1,0:T(8,128)S(1)} %copy-done.1, f32[2,8,2,128,128]{4,3,2,1,0:T(8,128)} %sens.1, s32[2,8,128,128]{3,2,1,0:T(8,128)S(1)} %copy-done.3, bf16[768,256]{1,0:T(8,128)(2,1)S(1)} %copy-done.4, ...), custom_call_target="tpu_custom_call" | custom-call | flops 6442450944 | bytes 20971520 | tf_op jit(solution)/shard_map/normal_one/pallas_call | solution.py:535
  30.7 1.4 %copy-done.6 = f32[2,8,2,128,128]{4,3,2,1,0:T(8,128)} copy-done((f32[2,8,2,128,128]{4,3,2,1,0:T(8,128)}, f32[2,8,2,128,128]{4,3,2,1,0:T(8,128)S(1)}, u32[]{:S(2)}) %copy-start.6) | copy-done | bytes 2097176
  32.1 0.0 all-to-all-done
  32.1 5.9 %all-to-all-start.2 = ((bf16[32,4,8,128]{3,2,1,0:T(8,128)(2,1)}), bf16[32,4,8,128]{3,2,1,0:T(8,128)(2,1)S(1)}, u32[]{:S(2)}, u32[]{:S(2)}) async-start(bf16[32,4,8,128]{3,2,1,0:T(8,128)(2,1)} %bitcast.11), calls=%async_computation.2 | async-start | bytes 524288 | tf_op jit(solution)/shard_map/all_to_all | solution.py:577
  38.0 0.8 broadcast_in_dim.15.bias_one
  38.8 0.8 broadcast_in_dim.17.bias_two
  39.6 26.9 %both.1 = (bf16[1,8,384,512]{3,2,1,0:T(8,128)(2,1)}, bf16[1,8,384,512]{3,2,1,0:T(8,128)(2,1)}, bf16[8,4,4,8,128]{4,3,2,1,0:T(8,128)(2,1)}) custom-call(bf16[8,4,4,16,128]{4,3,2,1,0:T(8,128)(2,1)} %bitcast.1.got, f32[96,512]{1,0:T(8,128)} %broadcast_in_dim.15.bias_one, f32[96,512]{1,0:T(8,128)} %broadcast_in_dim.17.bias_two, ...), custom_call_target="tpu_custom_call" | custom-call | flops 13589544960 | bytes 16777216 | tf_op jit(solution)/shard_map/both/pallas_call | solution.py:555
  66.5 0.0 all-to-all-done.2
  66.5 5.7 %all-to-all-start.1 = ((bf16[32,4,8,128]{3,2,1,0:T(8,128)(2,1)}), bf16[32,4,8,128]{3,2,1,0:T(8,128)(2,1)S(1)}, u32[]{:S(2)}, u32[]{:S(2)}) async-start(bf16[32,4,8,128]{3,2,1,0:T(8,128)(2,1)} %bitcast.31), calls=%async_computation.1 | async-start | bytes 524288 | tf_op jit(solution)/shard_map/all_to_all | solution.py:577
  72.1 15.4 %back.1 = bf16[8,4,4,8,128]{4,3,2,1,0:T(8,128)(2,1)} custom-call(bf16[8,4,4,8,128]{4,3,2,1,0:T(8,128)(2,1)} %bitcast.29, bf16[8,4,4,8,128]{4,3,2,1,0:T(8,128)(2,1)} %get-tuple-element.30.before, bf16[1,768,384]{2,1,0:T(8,128)(2,1)} %get-tuple-element.26.m_out, bf16[4,288,480]{2,1,0:T(8,128)(2,1)} %get-tuple-element.28.m_back, ...), custom_call_target="tpu_custom_call" | custom-call | flops 6794772480 | bytes 12582912 | tf_op jit(solution)/shard_map/back/pallas_call | solution.py:555
  87.6 0.0 all-to-all-done.1
  87.6 6.1 %all-to-all-start.3 = ((bf16[32,4,8,128]{3,2,1,0:T(8,128)(2,1)}), bf16[32,4,8,128]{3,2,1,0:T(8,128)(2,1)S(1)}, u32[]{:S(2)}, u32[]{:S(2)}) async-start(bf16[32,4,8,128]{3,2,1,0:T(8,128)(2,1)} %bitcast.30), calls=%async_computation.3 | async-start | bytes 524288 | tf_op jit(solution)/shard_map/all_to_all | solution.py:577
  93.6 10.3 %normal_two.1 = (f32[2,2,2,128,128]{4,3,2,1,0:T(8,128)S(1)}, f32[2,2,2,128,128]{4,3,2,1,0:T(8,128)S(1)}) custom-call(f32[2,2,2,128,128]{4,3,2,1,0:T(8,128)S(1)} %get-tuple-element.23.point, bf16[128,8,128]{2,1,0:T(8,128)(2,1)S(1)} %bitcast.23, f32[2,2,2,128,128]{4,3,2,1,0:T(8,128)S(1)} %copy-done.1, f32[2,8,2,128,128]{4,3,2,1,0:T(8,128)} %copy-done.6, ...), custom_call_target="tpu_custom_call" | custom-call | flops 6442450944 | bytes 20971520 | tf_op jit(solution)/shard_map/normal_two/pallas_call | solution.py:535
  104.0 0.8 copy-done
  104.8 0.8 copy-done.2
  105.5 0.0 all-to-all-done.3
  105.6 0.7 copy-done.7
  106.3 2.6 %finish.1 = (f32[2,2,2,128,128]{4,3,2,1,0:T(8,128)}, f32[32,1,128]{2,1,0:T(1,128)}) custom-call(f32[2,2,2,128,128]{4,3,2,1,0:T(8,128)} %copy-done.2, bf16[128,8,128]{2,1,0:T(8,128)(2,1)} %bitcast.24, f32[2,2,2,128,128]{4,3,2,1,0:T(8,128)} %copy-done, f32[2,2,2,128,128]{4,3,2,1,0:T(8,128)} %get-tuple-element.22.cotangent), custom_call_target="tpu_custom_call" | custom-call | flops 1048576 | bytes 4194304 | tf_op jit(solution)/shard_map/finish/pallas_call | solution.py:555
  108.8 12.9 %all_to_all.25.gathered = f32[32,1,128]{2,1,0:T(1,128)} all-to-all(f32[32,1,128]{2,1,0:T(1,128)} %get-tuple-element.37), channel_id=1, replica_groups=mesh['readout'=8,'frame'=4] {'readout','frame'}, dimensions={0} | all-to-all | bytes 32768 | tf_op jit(solution)/shard_map/all_to_all | solution.py:577
  121.7 2.6 %mix.1 = f32[2,2,2,128,128]{4,3,2,1,0:T(8,128)} custom-call(f32[32,1,128]{2,1,0:T(1,128)} %all_to_all.25.gathered, f32[2,2,2,128,128]{4,3,2,1,0:T(8,128)} %copy-done, f32[2,2,2,128,128]{4,3,2,1,0:T(8,128)} %get-tuple-element.38.second), custom_call_target="tpu_custom_call" | custom-call | flops 1048576 | bytes 4194304 | tf_op jit(solution)/shard_map/mix/pallas_call | solution.py:555
  (33 shorter events, 0.1 us)
Async XLA Ops:
  0.0 18.9 %copy-start.4 = (bf16[768,256]{1,0:T(8,128)(2,1)S(1)}, bf16[768,256]{1,0:T(8,128)(2,1)}, u32[]{:S(2)}) copy-start(bf16[768,256]{1,0:T(8,128)(2,1)} %constant.21.clone.forward_y.forward_z) | copy-start | bytes 1179652
  0.0 18.9 %copy-start.5 = (bf16[768,256]{1,0:T(8,128)(2,1)S(1)}, bf16[768,256]{1,0:T(8,128)(2,1)}, u32[]{:S(2)}) copy-start(bf16[768,256]{1,0:T(8,128)(2,1)} %constant.22.clone.inverse_z.inverse_y) | copy-start | bytes 1179652
  0.0 10.3 %copy-start.11 = (bf16[24,2,3,3,3]{0,1,4,3,2:T(2,128)(2,1)S(1)}, bf16[24,2,3,3,3]{0,1,4,3,2:T(2,128)(2,1)}, u32[]{:S(2)}) copy-start(bf16[24,2,3,3,3]{0,1,4,3,2:T(2,128)(2,1)} %param.20) | copy-start | bytes 7780
  0.0 11.2 %copy-start.8 = (bf16[24,24,3,3,3]{1,0,4,3,2:T(8,128)(2,1)S(1)}, bf16[24,24,3,3,3]{1,0,4,3,2:T(8,128)(2,1)}, u32[]{:S(2)}) copy-start(bf16[24,24,3,3,3]{1,0,4,3,2:T(8,128)(2,1)} %param.22) | copy-start | bytes 93316
  0.0 12.0 %copy-start.10 = (bf16[2,24,3,3,3]{1,0,4,3,2:T(2,128)(2,1)S(1)}, bf16[2,24,3,3,3]{1,0,4,3,2:T(2,128)(2,1)}, u32[]{:S(2)}) copy-start(bf16[2,24,3,3,3]{1,0,4,3,2:T(2,128)(2,1)} %param.24) | copy-start | bytes 7780
  0.0 12.8 %copy-start.12 = (f32[24]{0:T(128)S(1)}, f32[24]{0:T(128)}, u32[]{:S(2)}) copy-start(f32[24]{0:T(128)} %param.21) | copy-start | bytes 292
  0.0 12.9 %copy-start.13 = (f32[24]{0:T(128)S(1)}, f32[24]{0:T(128)}, u32[]{:S(2)}) copy-start(f32[24]{0:T(128)} %param.23) | copy-start | bytes 292
  0.0 18.9 %copy-start.3 = (s32[2,8,128,128]{3,2,1,0:T(8,128)S(1)}, s32[2,8,128,128]{3,2,1,0:T(8,128)}, u32[]{:S(2)}) copy-start(s32[2,8,128,128]{3,2,1,0:T(8,128)} %mask.3) | copy-start | bytes 3145732
  2.8 16.1 %copy-start.1 = (f32[2,2,2,128,128]{4,3,2,1,0:T(8,128)S(1)}, f32[2,2,2,128,128]{4,3,2,1,0:T(8,128)}, u32[]{:S(2)}) copy-start(f32[2,2,2,128,128]{4,3,2,1,0:T(8,128)} %get-tuple-element.22.cotangent) | copy-start | bytes 1572868
  2.8 29.3 %all-to-all-start = ((bf16[32,4,16,128]{3,2,1,0:T(8,128)(2,1)}), bf16[32,4,16,128]{3,2,1,0:T(8,128)(2,1)}, u32[]{:S(2)}, u32[]{:S(2)}) async-start(bf16[32,4,16,128]{3,2,1,0:T(8,128)(2,1)} %bitcast.28), calls=%async_computation | async-start | bytes 1048576 | tf_op jit(solution)/shard_map/all_to_all | solution.py:577
  30.7 1.4 %copy-start.6 = (f32[2,8,2,128,128]{4,3,2,1,0:T(8,128)}, f32[2,8,2,128,128]{4,3,2,1,0:T(8,128)S(1)}, u32[]{:S(2)}) copy-start(f32[2,8,2,128,128]{4,3,2,1,0:T(8,128)S(1)} %get-tuple-element.31.sens) | copy-start | bytes 6291460
  32.1 34.4 %all-to-all-start.2 = ((bf16[32,4,8,128]{3,2,1,0:T(8,128)(2,1)}), bf16[32,4,8,128]{3,2,1,0:T(8,128)(2,1)S(1)}, u32[]{:S(2)}, u32[]{:S(2)}) async-start(bf16[32,4,8,128]{3,2,1,0:T(8,128)(2,1)} %bitcast.11), calls=%async_computation.2 | async-start | bytes 524288 | tf_op jit(solution)/shard_map/all_to_all | solution.py:577
  66.5 5.7 %copy-start.9 = (bf16[32,4,8,128]{3,2,1,0:T(8,128)(2,1)}, bf16[32,4,8,128]{3,2,1,0:T(8,128)(2,1)S(1)}, u32[]{:S(2)}) copy-start(bf16[32,4,8,128]{3,2,1,0:T(8,128)(2,1)S(1)} %all-to-all-done.2) | copy-start | bytes 786436
  66.5 21.1 %all-to-all-start.1 = ((bf16[32,4,8,128]{3,2,1,0:T(8,128)(2,1)}), bf16[32,4,8,128]{3,2,1,0:T(8,128)(2,1)S(1)}, u32[]{:S(2)}, u32[]{:S(2)}) async-start(bf16[32,4,8,128]{3,2,1,0:T(8,128)(2,1)} %bitcast.31), calls=%async_computation.1 | async-start | bytes 524288 | tf_op jit(solution)/shard_map/all_to_all | solution.py:577
  87.6 18.0 %all-to-all-start.3 = ((bf16[32,4,8,128]{3,2,1,0:T(8,128)(2,1)}), bf16[32,4,8,128]{3,2,1,0:T(8,128)(2,1)S(1)}, u32[]{:S(2)}, u32[]{:S(2)}) async-start(bf16[32,4,8,128]{3,2,1,0:T(8,128)(2,1)} %bitcast.30), calls=%async_computation.3 | async-start | bytes 524288 | tf_op jit(solution)/shard_map/all_to_all | solution.py:577
  103.9 0.8 copy-start
  104.8 0.8 copy-start.2
  105.5 0.7 copy-start.7

commit v3 on v2

--- a/solution.py
+++ b/solution.py
@@ -15,6 +15,7 @@
 F32 = jnp.float32
 BF16 = jnp.bfloat16
 VMEM = pl.BlockSpec(memory_space=pltpu.VMEM)
+ANY = pl.BlockSpec(memory_space=pl.ANY)
 GROUP = 4
 WIDE = 16
 LAST = 8
@@ -53,6 +54,13 @@
         self.ks = [min(max(wide * g - 32, 0), self.rows - self.KW) for g in range(self.GL)]
         self.part = 6 * self.near * self.unit
 
+    def mid_of(self, g):
+        offsets = [self.ws[n] - self.M * n for n in range(self.G)]
+        return sorted(set(offsets), reverse=True).index(offsets[g])
+
+    def mid_first(self):
+        return [next(g for g in range(self.G) if self.mid_of(g) == n) for n in range(self.mid_of(self.G - 1) + 1)]
+
     def mid_table(self, g):
         k = np.arange(3 * self.W)
         row = self.ws[g] + k % self.W
@@ -141,12 +149,19 @@
 
 
 def weights_kernel(
-    p, w_in, w_mid, w_out, b_mid, b_in, mid_tab, in_tab, pick, row_x, col_tab, m_in, m_out, m_mid, m_back, m_last
+    p, w_in, w_mid, w_out, b_mid, b_in, one, two, mid_tab, in_tab, pick, row_x, col_tab,
+    m_in, m_out, m_mid, m_back, m_last, bias_one, bias_two,
 ):
-    for g in range(p.G):
-        table = mid_tab[g]
-        banded_taps(w_mid, False, table, g * GROUP, p.ch, m_mid, g, 0.5)
-        banded_taps(b_mid, True, table, g * GROUP, p.ch, m_back, g, 1.0)
+    for line, out in ((one, bias_one), (two, bias_two)):
+        shape = (p.ch, p.ch)
+        same = lax.broadcasted_iota(jnp.int32, shape, 0) == lax.broadcasted_iota(jnp.int32, shape, 1)
+        column = 0.5 * jnp.sum(jnp.where(same, line[...], 0.0), axis=1, keepdims=True)
+        for n in range(GROUP):
+            out[n * p.ch : (n + 1) * p.ch, :] = jnp.broadcast_to(column, (p.ch, p.L))
+    for n, g in enumerate(p.mid_first()):
+        table = mid_tab[n]
+        banded_taps(w_mid, False, table, g * GROUP, p.ch, m_mid, n, 0.5)
+        banded_taps(b_mid, True, table, g * GROUP, p.ch, m_back, n, 1.0)
     for g in range(p.GI):
         for t2 in range(p.tl):
             table = in_tab[g, t2]
@@ -214,9 +229,32 @@
                 h_ref[h, t, start : start + hi - lo, :] = moved[lo - p.M * g : hi - p.M * g]
 
 
+class Layer:
+    def __init__(self, steps, issue, finish, end=None):
+        self.steps, self.issue, self.finish, self.end = steps, issue, finish, end
+
+    def start(self):
+        self.issue(0)
+
+    def run(self, ahead=None):
+        def body(n, carry):
+            self.finish(n - 1)
+            self.issue(n)
+            return carry
+
+        lax.fori_loop(1, self.steps, body, 0)
+        if ahead is not None:
+            ahead()
+        self.finish(self.steps - 1)
+        if self.end is not None:
+            self.end()
+
+
 def first_layer(p, matrix, u_ref, d_ref, each):
     def issue(f):
-        start = pl.multiple_of(f * (p.tl * 3 * p.UW), 16)
+        start = f * (p.tl * 3 * p.UW)
+        if not isinstance(f, int):
+            start = pl.multiple_of(start, 16)
         size = (p.tl + 2) * 3 * p.UW
         for gi in range(p.GI):
             d_ref[gi] = dot(matrix[gi], u_ref[gi, pl.ds(start, size), :])
@@ -228,46 +266,36 @@
                     row = (t2 * WIDE + at * GROUP) * p.ch
                     each(f * p.tl + t2, gi * (WIDE // GROUP) + at, d_ref[gi, row : row + p.M, :])
 
-    def body(f, carry):
-        finish(f - 1)
-        issue(f)
-        return carry
-
-    issue(0)
-    lax.fori_loop(1, p.F, body, 0)
-    finish(p.F - 1)
+    return Layer(p.F, issue, finish)
 
 
 def middle_layer(p, matrix, h_ref, d_ref, run_ref, each):
-    run_ref[...] = jnp.zeros_like(run_ref)
-
     def issue(t):
+        if isinstance(t, int):
+            run_ref[...] = jnp.zeros_like(run_ref)
         for g in range(p.G):
-            d_ref[g] = dot(matrix[g], h_ref[g, t])
+            d_ref[g] = dot(matrix[p.mid_of(g)], h_ref[g, t])
 
     def finish(t):
         for g in range(p.G):
-            each(jnp.maximum(t - 1, 0), g, run_ref[g, 0] + d_ref[g, 2 * p.M :, :])
+            before = jnp.maximum(t - 1, 0) if not isinstance(t, int) else t - 1
+            each(before, g, run_ref[g, 0] + d_ref[g, 2 * p.M :, :])
             run_ref[g, 0] = run_ref[g, 1] + d_ref[g, p.M : 2 * p.M, :]
             run_ref[g, 1] = d_ref[g, : p.M, :]
 
-    def body(t, carry):
-        finish(t - 1)
-        issue(t)
-        return carry
-
-    issue(0)
-    lax.fori_loop(1, p.T, body, 0)
-    finish(p.T - 1)
-    for g in range(p.G):
-        each(p.T - 1, g, run_ref[g, 0])
+    def end():
+        for g in range(p.G):
+            each(p.T - 1, g, run_ref[g, 0])
+
+    return Layer(p.T, issue, finish, end)
 
 
 def last_layer(p, matrix, g_ref, l_ref, acc_ref):
-    acc_ref[...] = jnp.zeros_like(acc_ref)
     size = p.near * p.unit
 
     def issue(f):
+        if isinstance(f, int):
+            acc_ref[...] = jnp.zeros_like(acc_ref)
         for g in range(p.GL):
             for s in range(p.tl):
                 l_ref[g, s] = dot(matrix[g, s], g_ref[f * p.tl + s, pl.ds(p.ks[g], p.KW), :])
@@ -283,35 +311,44 @@
                         value = value + shifted(l_ref[g, s, first + c * size : first + (c + 1) * size, :], c, p.ny)
                     acc_ref[slot, pl.ds(g * size, size), :] += value
 
-    def body(f, carry):
-        finish(f - 1)
-        issue(f)
-        return carry
-
-    issue(0)
-    lax.fori_loop(1, p.F, body, 0)
-    finish(p.F - 1)
-
-
-def backward(p, zb, load, m_out, m_back, m_last, slope_one, slope_two, back, u_ref, h_ref, g_ref, acc_ref, run_ref, d_ref, e_ref, row_ref, l_ref):
-    gather_field(p, load, u_ref, row_ref)
+    return Layer(p.F, issue, finish)
+
+
+def backward(p, load, m_out, m_back, m_last, slope_one, slope_two, put, scratch):
+    u_ref, h_ref, g_ref, acc_ref, run_ref, d_ref, e_ref, row_ref, l_ref = scratch
 
     def after_out(t, g, value):
         rows = pl.ds(p.M * g, p.M)
-        put_window(p, h_ref, g, t, slope_two[zb, t, rows, :].astype(F32) * value)
-
-    first_layer(p, m_out, u_ref, d_ref, after_out)
+        put_window(p, h_ref, g, t, slope_two[t, rows, :].astype(F32) * value)
 
     def after_mid(t, g, value):
         rows = pl.ds(p.M * g, p.M)
-        g_ref[t, rows, :] = (slope_one[zb, t, rows, :].astype(F32) * value).astype(BF16)
-
-    middle_layer(p, m_back, h_ref, e_ref, run_ref, after_mid)
-    last_layer(p, m_last, g_ref, l_ref, acc_ref)
-    for f in range(p.F):
-        for j in range(p.nzb):
-            value = acc_ref[f + 1, :, j * p.ny : (j + 1) * p.ny].reshape(p.R, p.unit, p.ny)
-            back[:, f, zb * p.nzb + j, :, :] = value.astype(BF16)
+        g_ref[t, rows, :] = (slope_one[t, rows, :].astype(F32) * value).astype(BF16)
+
+    out = first_layer(p, m_out, u_ref, d_ref, after_out)
+    middle = middle_layer(p, m_back, h_ref, e_ref, run_ref, after_mid)
+    last = last_layer(p, m_last, g_ref, l_ref, acc_ref)
+
+    def begin():
+        gather_field(p, load, u_ref, row_ref)
+        out.start()
+
+    def rest(before_two, before_one):
+        before_two()
+
+        def ahead():
+            before_one()
+            middle.start()
+
+        out.run(ahead)
+        middle.run(last.start)
+        last.run()
+        for f in range(p.F):
+            for j in range(p.nzb):
+                value = acc_ref[f + 1, :, j * p.ny : (j + 1) * p.ny].reshape(p.R, p.unit, p.ny)
+                put(f, j, value.astype(BF16))
+
+    return begin, rest
 
 
 def clear_edges(p, u_ref):
@@ -320,53 +357,87 @@
 
 
 def both_kernel(
-    p, got, bias_one, bias_two, m_in, m_out, m_mid, m_back, m_last,
-    slope_one, slope_two, back, u_ref, h_ref, g_ref, acc_ref, run_ref, d_ref, e_ref, row_ref, l_ref,
+    p, got, bias_one, bias_two, m_in, mid_far, out_far, back_far, last_far, one_far, two_far, back,
+    m_mid, m_out, m_back, m_last, slope_one, slope_two, in_sem, out_sem, *scratch,
 ):
+    u_ref, h_ref, g_ref, acc_ref, run_ref, d_ref, e_ref, row_ref, l_ref = scratch
+    copies = [
+        pltpu.make_async_copy(far, near, in_sem.at[n])
+        for n, (far, near) in enumerate(((mid_far, m_mid), (out_far, m_out), (back_far, m_back), (last_far, m_last)))
+    ]
+    for copy in copies:
+        copy.start()
     clear_edges(p, u_ref)
-
-    def block(zb, carry):
-        def load(which, f, j):
+    for zb in range(p.NZB):
+
+        def load(which, f, j, zb=zb):
             value = got[:, f, zb * p.nzb + j, :, :].astype(F32)
             return value[:, which * p.unit : (which + 1) * p.unit]
 
-        gather_field(p, functools.partial(load, 0), u_ref, row_ref)
+        def put(f, j, value, zb=zb):
+            back[:, f, zb * p.nzb + j, :, :] = value
 
         def after_in(t, g, value):
             hidden, slope = silu_of_half(value + bias_one[...])
-            slope_one[zb, t, pl.ds(p.M * g, p.M), :] = slope.astype(BF16)
+            slope_one[t, pl.ds(p.M * g, p.M), :] = slope.astype(BF16)
             put_window(p, h_ref, g, t, hidden)
-
-        first_layer(p, m_in, u_ref, d_ref, after_in)
 
         def after_mid(t, g, value):
             _, slope = silu_of_half(value + bias_two[...])
-            slope_two[zb, t, pl.ds(p.M * g, p.M), :] = slope.astype(BF16)
-
-        middle_layer(p, m_mid, h_ref, e_ref, run_ref, after_mid)
-        backward(
-            p, zb, functools.partial(load, 1), m_out, m_back, m_last,
-            slope_one, slope_two, back, u_ref, h_ref, g_ref, acc_ref, run_ref, d_ref, e_ref, row_ref, l_ref,
+            slope_two[t, pl.ds(p.M * g, p.M), :] = slope.astype(BF16)
+
+        into = first_layer(p, m_in, u_ref, d_ref, after_in)
+        middle = middle_layer(p, m_mid, h_ref, e_ref, run_ref, after_mid)
+        begin, rest = backward(
+            p, functools.partial(load, 1), m_out, m_back, m_last, slope_one, slope_two, put, scratch
         )
-        return carry
-
-    lax.fori_loop(0, p.NZB, block, 0)
+        one_copy = pltpu.make_async_copy(slope_one, one_far.at[zb], out_sem.at[0])
+        two_copy = pltpu.make_async_copy(slope_two, two_far.at[zb], out_sem.at[1])
+        gather_field(p, functools.partial(load, 0), u_ref, row_ref)
+        if zb == 0:
+            copies[0].wait()
+        into.start()
+        into.run(middle.start)
+        one_copy.start()
+        if zb == 0:
+            copies[1].wait()
+        middle.run(begin)
+        two_copy.start()
+        if zb == 0:
+            copies[2].wait()
+            copies[3].wait()
+        rest(lambda: None, lambda: None)
+        one_copy.wait()
+        two_copy.wait()
 
 
 def back_kernel(
-    p, got, before, m_out, m_back, m_last, slope_one, slope_two, back, u_ref, h_ref, g_ref, acc_ref, run_ref, d_ref, e_ref, row_ref, l_ref
+    p, got, before, m_out, back_far, last_far, one_far, two_far, back,
+    m_back, m_last, slope_one, slope_two, sem, *scratch,
 ):
-    clear_edges(p, u_ref)
-
-    def block(zb, carry):
-        def load(f, j):
+    clear_edges(p, scratch[0])
+    for zb in range(p.NZB):
+        pairs = [(two_far.at[zb], slope_two), (one_far.at[zb], slope_one)]
+        if zb == 0:
+            pairs += [(back_far, m_back), (last_far, m_last)]
+        copies = [pltpu.make_async_copy(far, near, sem.at[n]) for n, (far, near) in enumerate(pairs)]
+        for copy in copies:
+            copy.start()
+
+        def load(f, j, zb=zb):
             at = zb * p.nzb + j
             return got[:, f, at, :, :].astype(F32) - before[:, f, at, :, :].astype(F32)
 
-        backward(p, zb, load, m_out, m_back, m_last, slope_one, slope_two, back, u_ref, h_ref, g_ref, acc_ref, run_ref, d_ref, e_ref, row_ref, l_ref)
-        return carry
-
-    lax.fori_loop(0, p.NZB, block, 0)
+        def put(f, j, value, zb=zb):
+            back[:, f, zb * p.nzb + j, :, :] = value
+
+        def others():
+            for copy in copies[1:]:
+                copy.wait()
+
+        begin, rest = backward(p, load, m_out, m_back, m_last, slope_one, slope_two, put, scratch)
+        begin()
+        rest(copies[0].wait, others)
 
 
 def planes(p):
@@ -386,14 +457,12 @@
     out[...] = scratch[...].reshape(p.nz, total, p.ny).astype(BF16)
 
 
-def finish_kernel(p, field, got, first, cotangent, out, gram, scratch):
+def gram_kernel(p, field, got, first, cotangent, gram, scratch):
     scratch[...] = got[...].astype(F32).reshape(p.nz * p.unit, p.ny)
     sums = [jnp.zeros((1, p.ny), F32) for _ in range(3)]
     for row, at in planes(p):
-        mapped = field[at] - scratch[pl.ds(row, p.nz, stride=p.unit), :]
-        out[at] = mapped
         old = first[at] - cotangent[at]
-        new = mapped - first[at]
+        new = field[at] - scratch[pl.ds(row, p.nz, stride=p.unit), :] - first[at]
         for n, product in enumerate((old * old, new * old, new * new)):
             sums[n] = sums[n] + jnp.sum(product, axis=0, keepdims=True)
     lane = lax.broadcasted_iota(jnp.int32, (1, 128), 1)
@@ -401,6 +470,13 @@
     for n in range(3):
         line = jnp.where(lane == n, jnp.sum(sums[n], axis=1, keepdims=True), line)
     gram[...] = jnp.broadcast_to(line[None], gram.shape)
+
+
+def turn_kernel(p, field, got, first, turned_first, turned_second, scratch):
+    scratch[...] = got[...].astype(F32).reshape(p.nz * p.unit, p.ny)
+    for row, at in planes(p):
+        turned_second[at] = (field[at] - scratch[pl.ds(row, p.nz, stride=p.unit), :]).T
+        turned_first[at] = first[at].T
 
 
 def small_solve(lines, values):
@@ -433,7 +509,7 @@
         for t in range(out.shape[1]):
             for x in range(out.shape[2]):
                 at = (part, t, x)
-                out[at] = (alpha[0] * first[at] + alpha[1] * second[at]).T
+                out[at] = alpha[0] * first[at] + alpha[1] * second[at]
 
 
 def dft_table(length, sign):
@@ -531,7 +607,7 @@
         out[part, 0, 0] = cotangent[part, 0, 0] + value - ETA * total
 
 
-def normal_call(p, kernel, args, specs, outs, out_specs, name, coils):
+def normal_call(p, kernel, args, specs, outs, out_specs, name, coils, vmem):
     return pl.pallas_call(
         functools.partial(kernel, p),
         grid=(p.xl, p.tl),
@@ -539,7 +615,7 @@
         out_specs=out_specs,
         out_shape=[jax.ShapeDtypeStruct(shape, kind) for shape, kind in outs],
         scratch_shapes=[pltpu.VMEM((p.nz * p.unit, p.ny), F32)],
-        compiler_params=pltpu.CompilerParams(vmem_limit_bytes=48 << 20),
+        compiler_params=pltpu.CompilerParams(vmem_limit_bytes=vmem),
         cost_estimate=pl.CostEstimate(
             flops=p.xl * p.tl * coils * 4 * 3 * 2 * 2 * p.ny * p.nz * 2 * p.nz,
             bytes_accessed=20 << 20,
@@ -549,16 +625,18 @@
     )(*args)
 
 
-def call(kernel, outs, args, name, scratch=(), flops=1 << 20, moved=4 << 20):
+def call(
+    kernel, outs, args, name, scratch=(), flops=1 << 20, moved=4 << 20, vmem=60 << 20, far_args=(), far_outs=()
+):
     shapes = [jax.ShapeDtypeStruct(shape, kind) for shape, kind in outs]
     single = len(shapes) == 1
     return pl.pallas_call(
         kernel,
-        in_specs=[VMEM] * len(args),
-        out_specs=VMEM if single else [VMEM] * len(shapes),
+        in_specs=[ANY if n in far_args else VMEM for n in range(len(args))],
+        out_specs=VMEM if single else [ANY if n in far_outs else VMEM for n in range(len(shapes))],
         out_shape=shapes[0] if single else shapes,
         scratch_shapes=list(scratch),
-        compiler_params=pltpu.CompilerParams(vmem_limit_bytes=60 << 20),
+        compiler_params=pltpu.CompilerParams(vmem_limit_bytes=vmem),
         cost_estimate=pl.CostEstimate(flops=flops, bytes_accessed=moved, transcendentals=0),
         name=name,
     )(*args)
@@ -619,23 +697,27 @@
         by_offset(flip_kernel(weight_out)),
         jnp.transpose(weight_mid, (2, 3, 4, 1, 0)).reshape(27, p.ch, p.ch),
         last,
-        jnp.asarray(np.stack([p.mid_table(g) for g in range(p.G)])),
+        bias_in[None, :],
+        bias_mid[None, :],
+        jnp.asarray(np.stack([p.mid_table(g) for g in p.mid_first()])),
         jnp.asarray(np.stack([np.stack([p.in_table(g, s) for s in range(p.tl)]) for g in range(p.GI)])),
         jnp.asarray(np.stack([np.stack([pick for pick, _ in line]) for line in picks])),
         jnp.asarray(np.stack([np.stack([x[:, None] for _, x in line]) for line in picks])),
         jnp.asarray(np.stack([p.out_cols(g) for g in range(p.GL)])),
     ]
     in_shape = (p.GI, p.tl * WIDE * p.ch, (p.tl + 2) * 3 * p.UW)
-    mid_shape = (p.G, 3 * p.M, 3 * p.W)
+    mid_shape = (len(p.mid_first()), 3 * p.M, 3 * p.W)
     last_shape = (p.GL, p.tl, p.part, p.KW)
-    m_in, m_out, m_mid, m_back, m_last = call(
+    bias_shape = (p.M, p.L)
+    m_in, m_out, m_mid, m_back, m_last, bias_one, bias_two = call(
         functools.partial(weights_kernel, p),
-        [(in_shape, BF16), (in_shape, BF16), (mid_shape, BF16), (mid_shape, BF16), (last_shape, BF16)],
+        [
+            (in_shape, BF16), (in_shape, BF16), (mid_shape, BF16), (mid_shape, BF16), (last_shape, BF16),
+            (bias_shape, F32), (bias_shape, F32),
+        ],
         weight_args,
         "weights",
     )
-    bias_one = jnp.broadcast_to(jnp.tile(0.5 * bias_in, GROUP)[:, None], (p.M, p.L))
-    bias_two = jnp.broadcast_to(jnp.tile(0.5 * bias_mid, GROUP)[:, None], (p.M, p.L))
 
     point, turned_sens, packed = normal_call(
         p,
@@ -646,6 +728,7 @@
         [image, turned_maps, lines],
         "normal_one",
         coils,
+        60 << 20,
     )
     got_point = exchange(packed.reshape(p.D, p.zl, p.unit, ny)).reshape(z_shape)
 
@@ -665,11 +748,23 @@
     slope_one, slope_two, back = call(
         functools.partial(both_kernel, p),
         [slope, slope, (z_shape, BF16)],
-        [got, bias_one, bias_two, m_in, m_out, m_mid, m_back, m_last],
+        [got, bias_one, bias_two, m_in, m_mid, m_out, m_back, m_last],
         "both",
-        scratch,
+        [
+            pltpu.VMEM(mid_shape, BF16),
+            pltpu.VMEM(in_shape, BF16),
+            pltpu.VMEM(mid_shape, BF16),
+            pltpu.VMEM(last_shape, BF16),
+            pltpu.VMEM(slope[0][1:], BF16),
+            pltpu.VMEM(slope[0][1:], BF16),
+            pltpu.SemaphoreType.DMA((4,)),
+            pltpu.SemaphoreType.DMA((2,)),
+            *scratch,
+        ],
         3 * work,
         16 << 20,
+        far_args=(4, 5, 6, 7),
+        far_outs=(0, 1),
     )
     returned = exchange(back.reshape(p.D, p.zl, p.unit, ny)).reshape(nz, p.unit, ny)
     back_two = call(
@@ -677,9 +772,17 @@
         [(z_shape, BF16)],
         [got_point, back, m_out, m_back, m_last, slope_one, slope_two],
         "back",
-        scratch,
+        [
+            pltpu.VMEM(mid_shape, BF16),
+            pltpu.VMEM(last_shape, BF16),
+            pltpu.VMEM(slope[0][1:], BF16),
+            pltpu.VMEM(slope[0][1:], BF16),
+            pltpu.SemaphoreType.DMA((4,)),
+            *scratch,
+        ],
         3 * work // 2,
         12 << 20,
+        far_args=(3, 4, 5, 6),
     )
     returned_two = exchange(back_two.reshape(p.D, p.zl, p.unit, ny)).reshape(nz, p.unit, ny)
     first, point_two = normal_call(
@@ -691,15 +794,29 @@
         [image, image],
         "normal_two",
         coils,
-    )
-    second, gram = call(
-        functools.partial(finish_kernel, p),
-        [(turned_shape, F32), ((p.D, 1, 128), F32)],
+        48 << 20,
+    )
+    lines_scratch = [pltpu.VMEM((nz * p.unit, ny), F32)]
+    gram = call(
+        functools.partial(gram_kernel, p),
+        [((p.D, 1, 128), F32)],
         [point_two, returned_two, first, turned],
-        "finish",
-        [pltpu.VMEM((nz * p.unit, ny), F32)],
-    )
-    return call(mix_kernel, [(cotangent.shape, F32)], [exchange(gram), first, second], "mix")
+        "gram",
+        lines_scratch,
+        vmem=16 << 20,
+    )
+    gathered = exchange(gram)
+    first_out, second_out = call(
+        functools.partial(turn_kernel, p),
+        [(cotangent.shape, F32), (cotangent.shape, F32)],
+        [point_two, returned_two, first],
+        "turn",
+        lines_scratch,
+        4 << 20,
+        16 << 20,
+        vmem=16 << 20,
+    )
+    return call(mix_kernel, [(cotangent.shape, F32)], [gathered, first_out, second_out], "mix", vmem=16 << 20)
 
 
 def solution(mesh):

time: 125 us -> 119 us (0.952)
  blocking collectives: 12.9 us -> 0 us
  waiting for transfers between devices: 0.01 us -> 6.78 us
  starting transfers between devices: 25.1 us -> 30.7 us
  Pallas kernels: 77.6 us -> 72.8 us
  local copies, waits for them, and re-layouts: 8.5 us -> 6.72 us
    all_to_all x1 -> x0, blocking collectives: 12.9 us -> none  [exchange(): return lax.all_to_all(blocks, AXES, 0, 0, tiled=True)]
    all_to_all x4 -> x5, waiting for transfers between devices: 0.01 us -> 6.78 us  [exchange(): return lax.all_to_all(blocks, AXES, 0, 0, tiled=True)]
    pallas_call x6 -> x7, Pallas kernels: 55.6 us -> 49.6 us  [call(): pl.pallas_call(kernel, in_specs=[ANY if n in far_args else VMEM for n in...]
    all_to_all x4 -> x5, starting transfers between devices: 25.1 us -> 30.7 us  [exchange(): return lax.all_to_all(blocks, AXES, 0, 0, tiled=True)]
    broadcast_in_dim x4 -> x0, local copies, waits for them, and re-layouts: 1.7 us -> none  [the longest x2 0.85 us: per_device(): jnp.broadcast_to(jnp.tile(0.5 * bias_in, GROUP)[:, None], (p.M, p.L))]
    unnamed x28 -> x14, local copies, waits for them, and re-layouts: 3.74 us -> 2.06 us
  transfers between devices with their start and end apart: 4 -> 5, of which waited for: 0 -> 1; matrix products, arithmetic and copies ran while one was open for 4% -> 5% of each run, Pallas kernels for 56% -> 57%
where the time goes in v3:
time: 119 us; the launch traced here: 118 us
  Pallas kernels  72.8 us (61%)
  starting transfers between devices  30.7 us (26%)
  waiting for transfers between devices  6.78 us (6%)
  local copies, waits for them, and re-layouts  6.72 us (6%)
    pallas_call x7, Pallas kernels, call(): pl.pallas_call(kernel, in_specs=[ANY if n in far_args else VMEM for n in...  49.6 us
    all_to_all x5, starting transfers between devices, exchange(): return lax.all_to_all(blocks, AXES, 0, 0, tiled=True)  30.7 us
    pallas_call x2, Pallas kernels, normal_call(): pl.pallas_call(functools.partial(kernel, p), grid=(p.xl, p.tl), in_specs=...  23.2 us
    all_to_all x5, waiting for transfers between devices, exchange(): return lax.all_to_all(blocks, AXES, 0, 0, tiled=True)  6.78 us
  transfers between devices with their start and end apart: 5, of which 1 were waited for; matrix products, arithmetic and copies ran while one was open for 5% of the time, Pallas kernels for 57%

profile of v3, /device:TPU:0, one launch (start us, length us, event | category | flops | bytes accessed | tf_op | source)
XLA Modules:
  0.0 118.0 jit_solution(7428289592477379654)
XLA Ops:
  0.0 2.6 %pack.1 = (bf16[128,16,128]{2,1,0:T(8,128)(2,1)}, f32[2,2,2,128,128]{4,3,2,1,0:T(8,128)}) custom-call(f32[2,2,2,128,128]{4,3,2,1,0:T(8,128)} %equilibrium.1, f32[2,2,2,128,128]{4,3,2,1,0:T(8,128)} %cotangent.1), custom_call_target="tpu_custom_call" | custom-call | flops 1048576 | bytes 4194304 | tf_op jit(solution)/shard_map/pack/pallas_call | solution.py:633
  2.6 7.3 %all-to-all-start = ((bf16[32,4,16,128]{3,2,1,0:T(8,128)(2,1)}), bf16[32,4,16,128]{3,2,1,0:T(8,128)(2,1)S(1)}, u32[]{:S(2)}, u32[]{:S(2)}) async-start(bf16[32,4,16,128]{3,2,1,0:T(8,128)(2,1)} %bitcast.32), calls=%async_computation | async-start | bytes 1048576 | tf_op jit(solution)/shard_map/all_to_all | solution.py:655
  10.0 0.8 reverse_bitcast_fusion
  10.9 0.1 mul.13
  11.0 0.7 copy.25.w_in
  11.7 1.7 %copy.23 = bf16[3,3,3,24,24]{4,3,2,1,0:T(8,128)(2,1)} copy(bf16[3,3,3,24,24]{3,4,2,1,0:T(8,128)(2,1)} %bitcast.28) | data formatting | bytes 62208 | tf_op jit(solution)/shard_map/transpose | solution.py:698
  13.4 0.7 reverse_bitcast_fusion.1
  14.1 0.1 reshape.42
  14.2 0.7 copy.26.w_out
  14.9 0.6 pad.4.b_in
  15.5 4.8 %weights.1 = (bf16[1,768,384]{2,1,0:T(8,128)(2,1)}, bf16[1,768,384]{2,1,0:T(8,128)(2,1)}, bf16[3,288,480]{2,1,0:T(8,128)(2,1)}, bf16[3,288,480]{2,1,0:T(8,128)(2...) custom-call(bf16[72,18]{1,0:T(8,128)(2,1)} %copy.25.w_in, ...), custom_call_target="tpu_custom_call" | custom-call | flops 1048576 | bytes 4194304 | tf_op jit(solution)/shard_map/weights/pallas_call | solution.py:633
  20.3 13.0 %normal_one.1 = (f32[2,2,2,128,128]{4,3,2,1,0:T(8,128)}, f32[2,8,2,128,128]{4,3,2,1,0:T(8,128)}, bf16[128,8,128]{2,1,0:T(8,128)(2,1)}) custom-call(f32[2,2,2,128,128]{4,3,2,1,0:T(8,128)} %get-tuple-element.24.cotangent, f32[2,8,2,128,128]{4,3,2,1,0:T(8,128)} %sens.1, s32[2,8,128,128]{3,2,1,0:T(8,128)} %mask.3, ...), custom_call_target="tpu_custom_call" | custom-call | flops 6442450944 | bytes 20971520 | tf_op jit(solution)/shard_map/normal_one/pallas_call | solution.py:611
  33.3 0.0 copy-start.5
  33.3 6.0 %all-to-all-start.2 = ((bf16[32,4,8,128]{3,2,1,0:T(8,128)(2,1)}), bf16[32,4,8,128]{3,2,1,0:T(8,128)(2,1)S(1)}, u32[]{:S(2)}, u32[]{:S(2)}) async-start(bf16[32,4,8,128]{3,2,1,0:T(8,128)(2,1)} %bitcast.35), calls=%async_computation.2 | async-start | bytes 524288 | tf_op jit(solution)/shard_map/all_to_all | solution.py:655
  39.3 25.1 %both.1 = (bf16[1,8,384,512]{3,2,1,0:T(8,128)(2,1)}, bf16[1,8,384,512]{3,2,1,0:T(8,128)(2,1)}, bf16[8,4,4,8,128]{4,3,2,1,0:T(8,128)(2,1)}) custom-call(bf16[8,4,4,16,128]{4,3,2,1,0:T(8,128)(2,1)} %bitcast.31, f32[96,512]{1,0:T(8,128)} %get-tuple-element.27.bias_one, f32[96,512]{1,0:T(8,128)} %get-tuple-element.28.bias_two, ...), custom_call_target="tpu_custom_call" | custom-call | flops 13589544960 | bytes 16777216 | tf_op jit(solution)/shard_map/both/pallas_call | solution.py:633
  64.4 0.0 all-to-all-done.2
  64.4 0.0 copy-start.6
  64.5 5.6 %all-to-all-start.1 = ((bf16[32,4,8,128]{3,2,1,0:T(8,128)(2,1)}), bf16[32,4,8,128]{3,2,1,0:T(8,128)(2,1)S(1)}, u32[]{:S(2)}, u32[]{:S(2)}) async-start(bf16[32,4,8,128]{3,2,1,0:T(8,128)(2,1)} %bitcast.36), calls=%async_computation.1 | async-start | bytes 524288 | tf_op jit(solution)/shard_map/all_to_all | solution.py:655
  70.1 0.0 copy-start.1
  70.1 0.0 copy-start.2
  70.2 14.4 %back.1 = bf16[8,4,4,8,128]{4,3,2,1,0:T(8,128)(2,1)} custom-call(bf16[8,4,4,8,128]{4,3,2,1,0:T(8,128)(2,1)} %bitcast.33, bf16[8,4,4,8,128]{4,3,2,1,0:T(8,128)(2,1)} %get-tuple-element.34.before, bf16[1,768,384]{2,1,0:T(8,128)(2,1)} %get-tuple-element.31.out_far.m_out, bf16[3,288,480]{2,1,0:T(8,128)(2,1)} %get-tuple-element.32.back_far, ...), custom_call_target="tpu_custom_call" | custom-call | flops 6794772480 | bytes 12582912 | tf_op jit(solution)/shard_map/back/pallas_call | solution.py:633
  84.5 0.0 all-to-all-done.1
  84.5 6.1 %all-to-all-start.3 = ((bf16[32,4,8,128]{3,2,1,0:T(8,128)(2,1)}), bf16[32,4,8,128]{3,2,1,0:T(8,128)(2,1)S(1)}, u32[]{:S(2)}, u32[]{:S(2)}) async-start(bf16[32,4,8,128]{3,2,1,0:T(8,128)(2,1)} %bitcast.34), calls=%async_computation.3 | async-start | bytes 524288 | tf_op jit(solution)/shard_map/all_to_all | solution.py:655
  90.6 0.0 copy-start.3
  90.6 1.0 copy-done.3
  91.6 1.0 copy-done.4
  92.7 10.3 %normal_two.1 = (f32[2,2,2,128,128]{4,3,2,1,0:T(8,128)S(1)}, f32[2,2,2,128,128]{4,3,2,1,0:T(8,128)S(1)}) custom-call(f32[2,2,2,128,128]{4,3,2,1,0:T(8,128)S(1)} %copy-done.4, bf16[128,8,128]{2,1,0:T(8,128)(2,1)S(1)} %bitcast.27, f32[2,2,2,128,128]{4,3,2,1,0:T(8,128)S(1)} %copy-done, f32[2,8,2,128,128]{4,3,2,1,0:T(8,128)} %get-tuple-element.35.sens, ...), custom_call_target="tpu_custom_call" | custom-call | flops 6442450944 | bytes 20971520 | tf_op jit(solution)/shard_map/normal_two/pallas_call | solution.py:611
  103.0 1.0 gram.1
  104.0 5.6 %all-to-all-start.4 = ((f32[32,1,128]{2,1,0:T(1,128)}), f32[32,1,128]{2,1,0:T(1,128)S(1)}, u32[]{:S(2)}, u32[]{:S(2)}) async-start(f32[32,1,128]{2,1,0:T(1,128)} %gram.1), calls=%async_computation.4 | async-start | bytes 32768 | tf_op jit(solution)/shard_map/all_to_all | solution.py:655
  109.6 0.3 turn.1
  110.0 6.8 %all-to-all-done.4.gathered = f32[32,1,128]{2,1,0:T(1,128)S(1)} async-done(((f32[32,1,128]{2,1,0:T(1,128)}), f32[32,1,128]{2,1,0:T(1,128)S(1)}, u32[]{:S(2)}, u32[]{:S(2)}) %all-to-all-start.4) | async-done | bytes 16416 | tf_op jit(solution)/shard_map/all_to_all | solution.py:655
  116.7 1.3 %mix.1 = f32[2,2,2,128,128]{4,3,2,1,0:T(8,128)} custom-call(f32[32,1,128]{2,1,0:T(1,128)S(1)} %all-to-all-done.4.gathered, f32[2,2,2,128,128]{4,3,2,1,0:T(8,128)S(1)} %get-tuple-element.41.first, f32[2,2,2,128,128]{4,3,2,1,0:T(8,128)S(1)} %get-tuple-element.42.second), custom_call_target="tpu_custom_call" | custom-call | flops 1048576 | bytes 4194304 | tf_op jit(solution)/shard_map/mix/pallas_call | solution.py:633
  (13 shorter events, 0.1 us)
Async XLA Ops:
  2.6 30.6 %all-to-all-start = ((bf16[32,4,16,128]{3,2,1,0:T(8,128)(2,1)}), bf16[32,4,16,128]{3,2,1,0:T(8,128)(2,1)S(1)}, u32[]{:S(2)}, u32[]{:S(2)}) async-start(bf16[32,4,16,128]{3,2,1,0:T(8,128)(2,1)} %bitcast.32), calls=%async_computation | async-start | bytes 1048576 | tf_op jit(solution)/shard_map/all_to_all | solution.py:655
  33.3 6.0 %copy-start.5 = (bf16[32,4,16,128]{3,2,1,0:T(8,128)(2,1)}, bf16[32,4,16,128]{3,2,1,0:T(8,128)(2,1)S(1)}, u32[]{:S(2)}) copy-start(bf16[32,4,16,128]{3,2,1,0:T(8,128)(2,1)S(1)} %all-to-all-done) | copy-start | bytes 1572868
  33.3 31.1 %all-to-all-start.2 = ((bf16[32,4,8,128]{3,2,1,0:T(8,128)(2,1)}), bf16[32,4,8,128]{3,2,1,0:T(8,128)(2,1)S(1)}, u32[]{:S(2)}, u32[]{:S(2)}) async-start(bf16[32,4,8,128]{3,2,1,0:T(8,128)(2,1)} %bitcast.35), calls=%async_computation.2 | async-start | bytes 524288 | tf_op jit(solution)/shard_map/all_to_all | solution.py:655
  64.4 5.7 %copy-start.6 = (bf16[32,4,8,128]{3,2,1,0:T(8,128)(2,1)}, bf16[32,4,8,128]{3,2,1,0:T(8,128)(2,1)S(1)}, u32[]{:S(2)}) copy-start(bf16[32,4,8,128]{3,2,1,0:T(8,128)(2,1)S(1)} %all-to-all-done.2) | copy-start | bytes 786436
  64.5 20.1 %all-to-all-start.1 = ((bf16[32,4,8,128]{3,2,1,0:T(8,128)(2,1)}), bf16[32,4,8,128]{3,2,1,0:T(8,128)(2,1)S(1)}, u32[]{:S(2)}, u32[]{:S(2)}) async-start(bf16[32,4,8,128]{3,2,1,0:T(8,128)(2,1)} %bitcast.36), calls=%async_computation.1 | async-start | bytes 524288 | tf_op jit(solution)/shard_map/all_to_all | solution.py:655
  70.1 20.5 %copy-start = (f32[2,2,2,128,128]{4,3,2,1,0:T(8,128)S(1)}, f32[2,2,2,128,128]{4,3,2,1,0:T(8,128)}, u32[]{:S(2)}) copy-start(f32[2,2,2,128,128]{4,3,2,1,0:T(8,128)} %get-tuple-element.24.cotangent) | copy-start | bytes 1572868
  70.1 20.5 %copy-start.1 = (s32[2,8,128,128]{3,2,1,0:T(8,128)S(1)}, s32[2,8,128,128]{3,2,1,0:T(8,128)}, u32[]{:S(2)}) copy-start(s32[2,8,128,128]{3,2,1,0:T(8,128)} %mask.3) | copy-start | bytes 3145732
  70.1 20.5 %copy-start.2 = (bf16[768,256]{1,0:T(8,128)(2,1)S(1)}, bf16[768,256]{1,0:T(8,128)(2,1)}, u32[]{:S(2)}) copy-start(bf16[768,256]{1,0:T(8,128)(2,1)} %constant.19.clone.forward_y.forward_z) | copy-start | bytes 1179652
  84.5 18.4 %all-to-all-start.3 = ((bf16[32,4,8,128]{3,2,1,0:T(8,128)(2,1)}), bf16[32,4,8,128]{3,2,1,0:T(8,128)(2,1)S(1)}, u32[]{:S(2)}, u32[]{:S(2)}) async-start(bf16[32,4,8,128]{3,2,1,0:T(8,128)(2,1)} %bitcast.34), calls=%async_computation.3 | async-start | bytes 524288 | tf_op jit(solution)/shard_map/all_to_all | solution.py:655
  90.6 1.0 copy-start.3
  91.6 1.0 copy-start.4
  104.0 12.8 %all-to-all-start.4 = ((f32[32,1,128]{2,1,0:T(1,128)}), f32[32,1,128]{2,1,0:T(1,128)S(1)}, u32[]{:S(2)}, u32[]{:S(2)}) async-start(f32[32,1,128]{2,1,0:T(1,128)} %gram.1), calls=%async_computation.4 | async-start | bytes 32768 | tf_op jit(solution)/shard_map/all_to_all | solution.py:655

commit v4 on v3

--- a/solution.py
+++ b/solution.py
@@ -83,7 +83,7 @@
         offset = self.tl if s == 0 else -self.tl
         a = s - frame + 1 + np.where(target == 1, offset, 0)
         q = np.where((a >= 0) & (a <= 2), (a * 3 + c) * 2 + part, -1)
-        pick = (q[:, None] == np.arange(24)[None, :]).astype(np.float32).astype(BF16)
+        pick = (q[:, None] == np.arange(18)[None, :]).astype(np.float32).astype(BF16)
         return pick, (r * self.xl + x2).astype(np.int32)
 
     def out_cols(self, g):
@@ -124,12 +124,30 @@
         ).astype(BF16)
 
 
-def banded_taps(raw, flipped, table, first, channels, out_ref, where, scale):
-    order = [26 - n if flipped else n for n in range(27)]
+def tap_stacks(raw, adjoint):
+    stacks = []
+    for c in range(3):
+        blocks = []
+        for ab in range(9):
+            n = ab * 3 + c
+            blocks.append(raw[26 - n].astype(F32).T if adjoint else raw[n].astype(F32))
+        stacks.append(jnp.concatenate(blocks, axis=0).astype(BF16))
+    return stacks
+
+
+def pair_stacks(raw, adjoint):
+    stacks = []
+    for b in range(3):
+        taps = [(a * 3 + b) * 3 + c for a in range(3) for c in range(3)]
+        rows = [raw[26 - n if adjoint else n].astype(F32) for n in taps]
+        stacks.append(jnp.concatenate(rows, axis=0))
+    return stacks
+
+
+def banded_taps(stacks, table, first, channels, out_ref, where, scale):
     spread = None
     for c in range(3):
-        stack = jnp.concatenate([raw[order[ab * 3 + c]].astype(F32) for ab in range(9)], axis=0).astype(BF16)
-        part = dot(stack, one_hot_rows(table, channels, c * channels))
+        part = dot(stacks[c], one_hot_rows(table, channels, c * channels))
         spread = part if spread is None else spread + part
     position = table[1:2, :]
     for a in range(3):
@@ -149,7 +167,7 @@
 
 
 def weights_kernel(
-    p, w_in, w_mid, w_out, b_mid, b_in, one, two, mid_tab, in_tab, pick, row_x, col_tab,
+    p, w_in, w_mid, w_out, one, two, mid_tab, in_tab, pick, row_x, col_tab,
     m_in, m_out, m_mid, m_back, m_last, bias_one, bias_two,
 ):
     for line, out in ((one, bias_one), (two, bias_two)):
@@ -158,20 +176,24 @@
         column = 0.5 * jnp.sum(jnp.where(same, line[...], 0.0), axis=1, keepdims=True)
         for n in range(GROUP):
             out[n * p.ch : (n + 1) * p.ch, :] = jnp.broadcast_to(column, (p.ch, p.L))
+    forward, adjoint = tap_stacks(w_mid, False), tap_stacks(w_mid, True)
     for n, g in enumerate(p.mid_first()):
         table = mid_tab[n]
-        banded_taps(w_mid, False, table, g * GROUP, p.ch, m_mid, n, 0.5)
-        banded_taps(b_mid, True, table, g * GROUP, p.ch, m_back, n, 1.0)
+        banded_taps(forward, table, g * GROUP, p.ch, m_mid, n, 0.5)
+        banded_taps(adjoint, table, g * GROUP, p.ch, m_back, n, 1.0)
+    into = (0.5 * jnp.concatenate([stack.T for stack in pair_stacks(w_in, False)], axis=0)).astype(BF16)
+    outof = jnp.concatenate([stack.T for stack in pair_stacks(w_out, True)], axis=0).astype(BF16)
+    last = [stack.astype(BF16) for stack in pair_stacks(w_in, True)]
     for g in range(p.GI):
         for t2 in range(p.tl):
             table = in_tab[g, t2]
-            banded(w_in[...], table, g * WIDE, WIDE, p.ch, m_in, g, t2 * WIDE * p.ch)
-            banded(w_out[...], table, g * WIDE, WIDE, p.ch, m_out, g, t2 * WIDE * p.ch)
+            banded(into, table, g * WIDE, WIDE, p.ch, m_in, g, t2 * WIDE * p.ch)
+            banded(outof, table, g * WIDE, WIDE, p.ch, m_out, g, t2 * WIDE * p.ch)
     for g in range(p.GL):
         cols = col_tab[g]
         place = one_hot_rows(cols, p.ch)
         position = cols[1:2, :]
-        taps = [dot(b_in[b], place).astype(BF16) for b in range(3)]
+        taps = [dot(last[b], place).astype(BF16) for b in range(3)]
         for s in range(p.tl):
             x = row_x[g, s]
             total = jnp.zeros((x.shape[0], p.KW), F32)
@@ -642,15 +664,6 @@
     )(*args)
 
 
-def flip_kernel(weight):
-    return jnp.transpose(jnp.flip(weight, (2, 3, 4)), (1, 0, 2, 3, 4))
-
-
-def by_offset(weight):
-    outs, ins = weight.shape[:2]
-    return jnp.transpose(weight, (3, 0, 2, 4, 1)).reshape(3 * outs, 9 * ins)
-
-
 def exchange(blocks):
     return lax.all_to_all(blocks, AXES, 0, 0, tiled=True)
 
@@ -688,15 +701,10 @@
     got = exchange(packed.reshape(p.D, p.zl, 2 * p.unit, ny)).reshape(p.R, p.F, p.zl, 2 * p.unit, ny)
 
     picks = [[p.out_rows(g, s) for s in range(p.tl)] for g in range(p.GL)]
-    back_in = flip_kernel(weight_in)
-    last = jnp.transpose(back_in, (3, 2, 4, 0, 1)).reshape(3, 18, p.ch)
-    last = jnp.pad(last, ((0, 0), (0, 6), (0, 0)))
     weight_args = [
-        by_offset(weight_in) * jnp.asarray(0.5, BF16),
+        jnp.transpose(weight_in, (2, 3, 4, 1, 0)).reshape(27, 2, p.ch),
         jnp.transpose(weight_mid, (2, 3, 4, 0, 1)).reshape(27, p.ch, p.ch),
-        by_offset(flip_kernel(weight_out)),
-        jnp.transpose(weight_mid, (2, 3, 4, 1, 0)).reshape(27, p.ch, p.ch),
-        last,
+        jnp.transpose(weight_out, (2, 3, 4, 0, 1)).reshape(27, 2, p.ch),
         bias_in[None, :],
         bias_mid[None, :],
         jnp.asarray(np.stack([p.mid_table(g) for g in p.mid_first()])),

time: 119 us -> 113 us (0.950)
  local copies, waits for them, and re-layouts: 6.72 us -> 2.06 us
    transpose x1 -> x0, local copies, waits for them, and re-layouts: 1.69 us -> none  [per_device(): jnp.transpose(weight_mid, (2, 3, 4, 1, 0)).reshape(27, p.ch, p.ch)]
  transfers between devices with their start and end apart: 5 -> 5, of which waited for: 1 -> 1; matrix products, arithmetic and copies ran while one was open for 5% -> 0% of each run, Pallas kernels for 57% -> 60%
where the time goes in v4:
time: 113 us
  Pallas kernels  72.9 us (65%)
  starting transfers between devices  30.7 us (27%)
  waiting for transfers between devices  6.78 us (6%)
  local copies, waits for them, and re-layouts  2.06 us (2%)
    pallas_call x7, Pallas kernels, call(): pl.pallas_call(kernel, in_specs=[ANY if n in far_args else VMEM for n in...  49.6 us
    all_to_all x5, starting transfers between devices, exchange(): return lax.all_to_all(blocks, AXES, 0, 0, tiled=True)  30.7 us
    pallas_call x2, Pallas kernels, normal_call(): pl.pallas_call(functools.partial(kernel, p), grid=(p.xl, p.tl), in_specs=...  23.3 us
    all_to_all x5, waiting for transfers between devices, exchange(): return lax.all_to_all(blocks, AXES, 0, 0, tiled=True)  6.78 us
  transfers between devices with their start and end apart: 5, of which 1 were waited for; matrix products, arithmetic and copies ran while one was open for 0% of the time, Pallas kernels for 60%

profile of v4, /device:TPU:0, one launch (start us, length us, event | category | flops | bytes accessed | tf_op | source)
XLA Modules:
  0.0 112.6 jit_solution(496218864718107518)
XLA Ops:
  0.0 2.6 %pack.1 = (bf16[128,16,128]{2,1,0:T(8,128)(2,1)}, f32[2,2,2,128,128]{4,3,2,1,0:T(8,128)}) custom-call(f32[2,2,2,128,128]{4,3,2,1,0:T(8,128)} %equilibrium.1, f32[2,2,2,128,128]{4,3,2,1,0:T(8,128)} %cotangent.1), custom_call_target="tpu_custom_call" | custom-call | flops 1048576 | bytes 4194304 | tf_op jit(solution)/shard_map/pack/pallas_call | solution.py:655
  2.6 7.3 %all-to-all-start = ((bf16[32,4,16,128]{3,2,1,0:T(8,128)(2,1)}), bf16[32,4,16,128]{3,2,1,0:T(8,128)(2,1)S(1)}, u32[]{:S(2)}, u32[]{:S(2)}) async-start(bf16[32,4,16,128]{3,2,1,0:T(8,128)(2,1)} %bitcast.23), calls=%async_computation | async-start | bytes 1048576 | tf_op jit(solution)/shard_map/all_to_all | solution.py:668
  10.0 4.8 %weights.1 = (bf16[1,768,384]{2,1,0:T(8,128)(2,1)}, bf16[1,768,384]{2,1,0:T(8,128)(2,1)}, bf16[3,288,480]{2,1,0:T(8,128)(2,1)}, bf16[3,288,480]{2,1,0:T(8,128)(2...) custom-call(bf16[27,2,24]{2,1,0:T(2,128)(2,1)} %bitcast.29, ...), custom_call_target="tpu_custom_call" | custom-call | flops 1048576 | bytes 4194304 | tf_op jit(solution)/shard_map/weights/pallas_call | solution.py:655
  14.8 13.0 %normal_one.1 = (f32[2,2,2,128,128]{4,3,2,1,0:T(8,128)}, f32[2,8,2,128,128]{4,3,2,1,0:T(8,128)}, bf16[128,8,128]{2,1,0:T(8,128)(2,1)}) custom-call(f32[2,2,2,128,128]{4,3,2,1,0:T(8,128)} %get-tuple-element.24.cotangent, f32[2,8,2,128,128]{4,3,2,1,0:T(8,128)} %sens.1, s32[2,8,128,128]{3,2,1,0:T(8,128)} %mask.3, ...), custom_call_target="tpu_custom_call" | custom-call | flops 6442450944 | bytes 20971520 | tf_op jit(solution)/shard_map/normal_one/pallas_call | solution.py:633
  27.9 0.0 all-to-all-done
  27.9 0.0 copy-start.5
  27.9 6.0 %all-to-all-start.2 = ((bf16[32,4,8,128]{3,2,1,0:T(8,128)(2,1)}), bf16[32,4,8,128]{3,2,1,0:T(8,128)(2,1)S(1)}, u32[]{:S(2)}, u32[]{:S(2)}) async-start(bf16[32,4,8,128]{3,2,1,0:T(8,128)(2,1)} %bitcast.26), calls=%async_computation.2 | async-start | bytes 524288 | tf_op jit(solution)/shard_map/all_to_all | solution.py:668
  33.9 0.0 copy-done.5
  33.9 25.1 %both.1 = (bf16[1,8,384,512]{3,2,1,0:T(8,128)(2,1)}, bf16[1,8,384,512]{3,2,1,0:T(8,128)(2,1)}, bf16[8,4,4,8,128]{4,3,2,1,0:T(8,128)(2,1)}) custom-call(bf16[8,4,4,16,128]{4,3,2,1,0:T(8,128)(2,1)} %bitcast.22, f32[96,512]{1,0:T(8,128)} %get-tuple-element.27.bias_one, f32[96,512]{1,0:T(8,128)} %get-tuple-element.28.bias_two, ...), custom_call_target="tpu_custom_call" | custom-call | flops 13589544960 | bytes 16777216 | tf_op jit(solution)/shard_map/both/pallas_call | solution.py:655
  59.0 0.0 all-to-all-done.2
  59.0 0.0 copy-start.6
  59.0 5.7 %all-to-all-start.1 = ((bf16[32,4,8,128]{3,2,1,0:T(8,128)(2,1)}), bf16[32,4,8,128]{3,2,1,0:T(8,128)(2,1)S(1)}, u32[]{:S(2)}, u32[]{:S(2)}) async-start(bf16[32,4,8,128]{3,2,1,0:T(8,128)(2,1)} %bitcast.27), calls=%async_computation.1 | async-start | bytes 524288 | tf_op jit(solution)/shard_map/all_to_all | solution.py:668
  64.7 0.0 copy-done.6
  64.7 0.0 copy-start
  64.7 0.0 copy-start.1
  64.7 0.0 copy-start.2
  64.7 14.4 %back.1 = bf16[8,4,4,8,128]{4,3,2,1,0:T(8,128)(2,1)} custom-call(bf16[8,4,4,8,128]{4,3,2,1,0:T(8,128)(2,1)} %bitcast.24, bf16[8,4,4,8,128]{4,3,2,1,0:T(8,128)(2,1)} %get-tuple-element.34.before, bf16[1,768,384]{2,1,0:T(8,128)(2,1)} %get-tuple-element.31.out_far.m_out, bf16[3,288,480]{2,1,0:T(8,128)(2,1)} %get-tuple-element.32.back_far, ...), custom_call_target="tpu_custom_call" | custom-call | flops 6794772480 | bytes 12582912 | tf_op jit(solution)/shard_map/back/pallas_call | solution.py:655
  79.1 0.0 all-to-all-done.1
  79.1 6.1 %all-to-all-start.3 = ((bf16[32,4,8,128]{3,2,1,0:T(8,128)(2,1)}), bf16[32,4,8,128]{3,2,1,0:T(8,128)(2,1)S(1)}, u32[]{:S(2)}, u32[]{:S(2)}) async-start(bf16[32,4,8,128]{3,2,1,0:T(8,128)(2,1)} %bitcast.25), calls=%async_computation.3 | async-start | bytes 524288 | tf_op jit(solution)/shard_map/all_to_all | solution.py:668
  85.2 0.0 copy-done
  85.2 0.0 copy-done.1
  85.2 0.0 copy-done.2
  85.2 0.0 copy-start.3
  85.2 1.0 copy-done.3
  86.2 1.0 copy-done.4
  87.3 10.3 %normal_two.1 = (f32[2,2,2,128,128]{4,3,2,1,0:T(8,128)S(1)}, f32[2,2,2,128,128]{4,3,2,1,0:T(8,128)S(1)}) custom-call(f32[2,2,2,128,128]{4,3,2,1,0:T(8,128)S(1)} %copy-done.4, bf16[128,8,128]{2,1,0:T(8,128)(2,1)S(1)} %bitcast.21, f32[2,2,2,128,128]{4,3,2,1,0:T(8,128)S(1)} %copy-done, f32[2,8,2,128,128]{4,3,2,1,0:T(8,128)} %get-tuple-element.35.sens, ...), custom_call_target="tpu_custom_call" | custom-call | flops 6442450944 | bytes 20971520 | tf_op jit(solution)/shard_map/normal_two/pallas_call | solution.py:633
  97.5 0.0 all-to-all-done.3
  97.5 1.0 gram.1
  98.6 5.6 %all-to-all-start.4 = ((f32[32,1,128]{2,1,0:T(1,128)}), f32[32,1,128]{2,1,0:T(1,128)S(1)}, u32[]{:S(2)}, u32[]{:S(2)}) async-start(f32[32,1,128]{2,1,0:T(1,128)} %gram.1), calls=%async_computation.4 | async-start | bytes 32768 | tf_op jit(solution)/shard_map/all_to_all | solution.py:668
  104.2 0.3 turn.1
  104.5 6.8 %all-to-all-done.4.gathered = f32[32,1,128]{2,1,0:T(1,128)S(1)} async-done(((f32[32,1,128]{2,1,0:T(1,128)}), f32[32,1,128]{2,1,0:T(1,128)S(1)}, u32[]{:S(2)}, u32[]{:S(2)}) %all-to-all-start.4) | async-done | bytes 16416 | tf_op jit(solution)/shard_map/all_to_all | solution.py:668
  111.3 1.3 %mix.1 = f32[2,2,2,128,128]{4,3,2,1,0:T(8,128)} custom-call(f32[32,1,128]{2,1,0:T(1,128)S(1)} %all-to-all-done.4.gathered, f32[2,2,2,128,128]{4,3,2,1,0:T(8,128)S(1)} %get-tuple-element.41.first, f32[2,2,2,128,128]{4,3,2,1,0:T(8,128)S(1)} %get-tuple-element.42.second), custom_call_target="tpu_custom_call" | custom-call | flops 1048576 | bytes 4194304 | tf_op jit(solution)/shard_map/mix/pallas_call | solution.py:655
  (1 shorter events, 0.0 us)
Async XLA Ops:
  2.6 25.2 %all-to-all-start = ((bf16[32,4,16,128]{3,2,1,0:T(8,128)(2,1)}), bf16[32,4,16,128]{3,2,1,0:T(8,128)(2,1)S(1)}, u32[]{:S(2)}, u32[]{:S(2)}) async-start(bf16[32,4,16,128]{3,2,1,0:T(8,128)(2,1)} %bitcast.23), calls=%async_computation | async-start | bytes 1048576 | tf_op jit(solution)/shard_map/all_to_all | solution.py:668
  27.9 6.0 %copy-start.5 = (bf16[32,4,16,128]{3,2,1,0:T(8,128)(2,1)}, bf16[32,4,16,128]{3,2,1,0:T(8,128)(2,1)S(1)}, u32[]{:S(2)}) copy-start(bf16[32,4,16,128]{3,2,1,0:T(8,128)(2,1)S(1)} %all-to-all-done) | copy-start | bytes 1572868
  27.9 31.1 %all-to-all-start.2 = ((bf16[32,4,8,128]{3,2,1,0:T(8,128)(2,1)}), bf16[32,4,8,128]{3,2,1,0:T(8,128)(2,1)S(1)}, u32[]{:S(2)}, u32[]{:S(2)}) async-start(bf16[32,4,8,128]{3,2,1,0:T(8,128)(2,1)} %bitcast.26), calls=%async_computation.2 | async-start | bytes 524288 | tf_op jit(solution)/shard_map/all_to_all | solution.py:668
  59.0 5.7 %copy-start.6 = (bf16[32,4,8,128]{3,2,1,0:T(8,128)(2,1)}, bf16[32,4,8,128]{3,2,1,0:T(8,128)(2,1)S(1)}, u32[]{:S(2)}) copy-start(bf16[32,4,8,128]{3,2,1,0:T(8,128)(2,1)S(1)} %all-to-all-done.2) | copy-start | bytes 786436
  59.0 20.1 %all-to-all-start.1 = ((bf16[32,4,8,128]{3,2,1,0:T(8,128)(2,1)}), bf16[32,4,8,128]{3,2,1,0:T(8,128)(2,1)S(1)}, u32[]{:S(2)}, u32[]{:S(2)}) async-start(bf16[32,4,8,128]{3,2,1,0:T(8,128)(2,1)} %bitcast.27), calls=%async_computation.1 | async-start | bytes 524288 | tf_op jit(solution)/shard_map/all_to_all | solution.py:668
  64.7 20.5 %copy-start = (f32[2,2,2,128,128]{4,3,2,1,0:T(8,128)S(1)}, f32[2,2,2,128,128]{4,3,2,1,0:T(8,128)}, u32[]{:S(2)}) copy-start(f32[2,2,2,128,128]{4,3,2,1,0:T(8,128)} %get-tuple-element.24.cotangent) | copy-start | bytes 1572868
  64.7 20.5 %copy-start.1 = (s32[2,8,128,128]{3,2,1,0:T(8,128)S(1)}, s32[2,8,128,128]{3,2,1,0:T(8,128)}, u32[]{:S(2)}) copy-start(s32[2,8,128,128]{3,2,1,0:T(8,128)} %mask.3) | copy-start | bytes 3145732
  64.7 20.5 %copy-start.2 = (bf16[768,256]{1,0:T(8,128)(2,1)S(1)}, bf16[768,256]{1,0:T(8,128)(2,1)}, u32[]{:S(2)}) copy-start(bf16[768,256]{1,0:T(8,128)(2,1)} %constant.14.clone.forward_y.forward_z) | copy-start | bytes 1179652
  79.1 18.4 %all-to-all-start.3 = ((bf16[32,4,8,128]{3,2,1,0:T(8,128)(2,1)}), bf16[32,4,8,128]{3,2,1,0:T(8,128)(2,1)S(1)}, u32[]{:S(2)}, u32[]{:S(2)}) async-start(bf16[32,4,8,128]{3,2,1,0:T(8,128)(2,1)} %bitcast.25), calls=%async_computation.3 | async-start | bytes 524288 | tf_op jit(solution)/shard_map/all_to_all | solution.py:668
  85.2 1.0 copy-start.3
  86.2 1.0 copy-start.4
  98.6 12.8 %all-to-all-start.4 = ((f32[32,1,128]{2,1,0:T(1,128)}), f32[32,1,128]{2,1,0:T(1,128)S(1)}, u32[]{:S(2)}, u32[]{:S(2)}) async-start(f32[32,1,128]{2,1,0:T(1,128)} %gram.1), calls=%async_computation.4 | async-start | bytes 32768 | tf_op jit(solution)/shard_map/all_to_all | solution.py:668

commit v5 on v4

--- a/solution.py
+++ b/solution.py
@@ -168,7 +168,8 @@
 
 def weights_kernel(
     p, w_in, w_mid, w_out, one, two, mid_tab, in_tab, pick, row_x, col_tab,
-    m_in, m_out, m_mid, m_back, m_last, bias_one, bias_two,
+    in_far, out_far, mid_far, back_far, last_far, bias_one, bias_two,
+    m_in, m_out, m_mid, m_back, m_last, sem,
 ):
     for line, out in ((one, bias_one), (two, bias_two)):
         shape = (p.ch, p.ch)
@@ -181,6 +182,10 @@
         table = mid_tab[n]
         banded_taps(forward, table, g * GROUP, p.ch, m_mid, n, 0.5)
         banded_taps(adjoint, table, g * GROUP, p.ch, m_back, n, 1.0)
+    pairs = ((m_mid, mid_far), (m_back, back_far), (m_in, in_far), (m_out, out_far), (m_last, last_far))
+    copies = [pltpu.make_async_copy(near, far, sem.at[n]) for n, (near, far) in enumerate(pairs)]
+    copies[0].start()
+    copies[1].start()
     into = (0.5 * jnp.concatenate([stack.T for stack in pair_stacks(w_in, False)], axis=0)).astype(BF16)
     outof = jnp.concatenate([stack.T for stack in pair_stacks(w_out, True)], axis=0).astype(BF16)
     last = [stack.astype(BF16) for stack in pair_stacks(w_in, True)]
@@ -189,6 +194,8 @@
             table = in_tab[g, t2]
             banded(into, table, g * WIDE, WIDE, p.ch, m_in, g, t2 * WIDE * p.ch)
             banded(outof, table, g * WIDE, WIDE, p.ch, m_out, g, t2 * WIDE * p.ch)
+    copies[2].start()
+    copies[3].start()
     for g in range(p.GL):
         cols = col_tab[g]
         place = one_hot_rows(cols, p.ch)
@@ -200,6 +207,9 @@
             for b in range(3):
                 total = jnp.where(position == x + (b - 1), dot(pick[g, s], taps[b]), total)
             m_last[g, s] = total.astype(BF16)
+    copies[4].start()
+    for copy in copies:
+        copy.wait()
 
 
 def shifted(value, c, ny):
@@ -725,6 +735,9 @@
         ],
         weight_args,
         "weights",
+        [pltpu.VMEM(shape, BF16) for shape in (in_shape, in_shape, mid_shape, mid_shape, last_shape)]
+        + [pltpu.SemaphoreType.DMA((5,))],
+        far_outs=(0, 1, 2, 3, 4),
     )
 
     point, turned_sens, packed = normal_call(

time: 113 us -> 114 us (level)
  transfers between devices with their start and end apart: 5 -> 5, of which waited for: 1 -> 1; matrix products, arithmetic and copies ran while one was open for 0% -> 0% of each run, Pallas kernels for 60% -> 61%
where the time goes in v5:
time: 114 us; the launch traced here: 113 us
  Pallas kernels  73.5 us (64%)
  starting transfers between devices  30.7 us (27%)
  waiting for transfers between devices  6.78 us (6%)
  local copies, waits for them, and re-layouts  2.06 us (2%)
    pallas_call x7, Pallas kernels, call(): pl.pallas_call(kernel, in_specs=[ANY if n in far_args else VMEM for n in...  50.2 us
    all_to_all x5, starting transfers between devices, exchange(): return lax.all_to_all(blocks, AXES, 0, 0, tiled=True)  30.7 us
    pallas_call x2, Pallas kernels, normal_call(): pl.pallas_call(functools.partial(kernel, p), grid=(p.xl, p.tl), in_specs=...  23.3 us
    all_to_all x5, waiting for transfers between devices, exchange(): return lax.all_to_all(blocks, AXES, 0, 0, tiled=True)  6.78 us
  transfers between devices with their start and end apart: 5, of which 1 were waited for; matrix products, arithmetic and copies ran while one was open for 0% of the time, Pallas kernels for 61%

profile of v5, /device:TPU:0, one launch (start us, length us, event | category | flops | bytes accessed | tf_op | source)
XLA Modules:
  0.0 113.3 jit_solution(8552998805838440430)
XLA Ops:
  0.0 2.6 %pack.1 = (bf16[128,16,128]{2,1,0:T(8,128)(2,1)}, f32[2,2,2,128,128]{4,3,2,1,0:T(8,128)}) custom-call(f32[2,2,2,128,128]{4,3,2,1,0:T(8,128)} %equilibrium.1, f32[2,2,2,128,128]{4,3,2,1,0:T(8,128)} %cotangent.1), custom_call_target="tpu_custom_call" | custom-call | flops 1048576 | bytes 4194304 | tf_op jit(solution)/shard_map/pack/pallas_call | solution.py:665
  2.6 7.3 %all-to-all-start = ((bf16[32,4,16,128]{3,2,1,0:T(8,128)(2,1)}), bf16[32,4,16,128]{3,2,1,0:T(8,128)(2,1)S(1)}, u32[]{:S(2)}, u32[]{:S(2)}) async-start(bf16[32,4,16,128]{3,2,1,0:T(8,128)(2,1)} %bitcast.23), calls=%async_computation | async-start | bytes 1048576 | tf_op jit(solution)/shard_map/all_to_all | solution.py:678
  10.0 5.5 %weights.1 = (bf16[1,768,384]{2,1,0:T(8,128)(2,1)}, bf16[1,768,384]{2,1,0:T(8,128)(2,1)}, bf16[3,288,480]{2,1,0:T(8,128)(2,1)}, bf16[3,288,480]{2,1,0:T(8,128)(2...) custom-call(bf16[27,2,24]{2,1,0:T(2,128)(2,1)} %bitcast.29, ...), custom_call_target="tpu_custom_call" | custom-call | flops 1048576 | bytes 4194304 | tf_op jit(solution)/shard_map/weights/pallas_call | solution.py:665
  15.5 13.1 %normal_one.1 = (f32[2,2,2,128,128]{4,3,2,1,0:T(8,128)}, f32[2,8,2,128,128]{4,3,2,1,0:T(8,128)}, bf16[128,8,128]{2,1,0:T(8,128)(2,1)}) custom-call(f32[2,2,2,128,128]{4,3,2,1,0:T(8,128)} %get-tuple-element.24.cotangent, f32[2,8,2,128,128]{4,3,2,1,0:T(8,128)} %sens.1, s32[2,8,128,128]{3,2,1,0:T(8,128)} %mask.3, ...), custom_call_target="tpu_custom_call" | custom-call | flops 6442450944 | bytes 20971520 | tf_op jit(solution)/shard_map/normal_one/pallas_call | solution.py:643
  28.5 0.0 all-to-all-done
  28.5 0.0 copy-start.5
  28.5 6.0 %all-to-all-start.2 = ((bf16[32,4,8,128]{3,2,1,0:T(8,128)(2,1)}), bf16[32,4,8,128]{3,2,1,0:T(8,128)(2,1)S(1)}, u32[]{:S(2)}, u32[]{:S(2)}) async-start(bf16[32,4,8,128]{3,2,1,0:T(8,128)(2,1)} %bitcast.26), calls=%async_computation.2 | async-start | bytes 524288 | tf_op jit(solution)/shard_map/all_to_all | solution.py:678
  34.6 0.0 copy-done.5
  34.6 25.1 %both.1 = (bf16[1,8,384,512]{3,2,1,0:T(8,128)(2,1)}, bf16[1,8,384,512]{3,2,1,0:T(8,128)(2,1)}, bf16[8,4,4,8,128]{4,3,2,1,0:T(8,128)(2,1)}) custom-call(bf16[8,4,4,16,128]{4,3,2,1,0:T(8,128)(2,1)} %bitcast.22, f32[96,512]{1,0:T(8,128)} %get-tuple-element.27.bias_one, f32[96,512]{1,0:T(8,128)} %get-tuple-element.28.bias_two, ...), custom_call_target="tpu_custom_call" | custom-call | flops 13589544960 | bytes 16777216 | tf_op jit(solution)/shard_map/both/pallas_call | solution.py:665
  59.7 0.0 all-to-all-done.2
  59.7 0.0 copy-start.6
  59.7 5.7 %all-to-all-start.1 = ((bf16[32,4,8,128]{3,2,1,0:T(8,128)(2,1)}), bf16[32,4,8,128]{3,2,1,0:T(8,128)(2,1)S(1)}, u32[]{:S(2)}, u32[]{:S(2)}) async-start(bf16[32,4,8,128]{3,2,1,0:T(8,128)(2,1)} %bitcast.27), calls=%async_computation.1 | async-start | bytes 524288 | tf_op jit(solution)/shard_map/all_to_all | solution.py:678
  65.4 0.0 copy-done.6
  65.4 0.0 copy-start
  65.4 0.0 copy-start.1
  65.4 0.0 copy-start.2
  65.4 14.4 %back.1 = bf16[8,4,4,8,128]{4,3,2,1,0:T(8,128)(2,1)} custom-call(bf16[8,4,4,8,128]{4,3,2,1,0:T(8,128)(2,1)} %bitcast.24, bf16[8,4,4,8,128]{4,3,2,1,0:T(8,128)(2,1)} %get-tuple-element.34.before, bf16[1,768,384]{2,1,0:T(8,128)(2,1)} %get-tuple-element.31.out_far.m_out, bf16[3,288,480]{2,1,0:T(8,128)(2,1)} %get-tuple-element.32.back_far, ...), custom_call_target="tpu_custom_call" | custom-call | flops 6794772480 | bytes 12582912 | tf_op jit(solution)/shard_map/back/pallas_call | solution.py:665
  79.8 0.0 all-to-all-done.1
  79.8 6.1 %all-to-all-start.3 = ((bf16[32,4,8,128]{3,2,1,0:T(8,128)(2,1)}), bf16[32,4,8,128]{3,2,1,0:T(8,128)(2,1)S(1)}, u32[]{:S(2)}, u32[]{:S(2)}) async-start(bf16[32,4,8,128]{3,2,1,0:T(8,128)(2,1)} %bitcast.25), calls=%async_computation.3 | async-start | bytes 524288 | tf_op jit(solution)/shard_map/all_to_all | solution.py:678
  85.9 0.0 copy-done
  85.9 0.0 copy-done.1
  85.9 0.0 copy-done.2
  85.9 0.0 copy-start.3
  85.9 1.0 copy-done.3
  86.9 1.0 copy-done.4
  87.9 10.3 %normal_two.1 = (f32[2,2,2,128,128]{4,3,2,1,0:T(8,128)S(1)}, f32[2,2,2,128,128]{4,3,2,1,0:T(8,128)S(1)}) custom-call(f32[2,2,2,128,128]{4,3,2,1,0:T(8,128)S(1)} %copy-done.4, bf16[128,8,128]{2,1,0:T(8,128)(2,1)S(1)} %bitcast.21, f32[2,2,2,128,128]{4,3,2,1,0:T(8,128)S(1)} %copy-done, f32[2,8,2,128,128]{4,3,2,1,0:T(8,128)} %get-tuple-element.35.sens, ...), custom_call_target="tpu_custom_call" | custom-call | flops 6442450944 | bytes 20971520 | tf_op jit(solution)/shard_map/normal_two/pallas_call | solution.py:643
  98.2 0.0 all-to-all-done.3
  98.2 1.0 gram.1
  99.2 5.6 %all-to-all-start.4 = ((f32[32,1,128]{2,1,0:T(1,128)}), f32[32,1,128]{2,1,0:T(1,128)S(1)}, u32[]{:S(2)}, u32[]{:S(2)}) async-start(f32[32,1,128]{2,1,0:T(1,128)} %gram.1), calls=%async_computation.4 | async-start | bytes 32768 | tf_op jit(solution)/shard_map/all_to_all | solution.py:678
  104.8 0.3 turn.1
  105.2 6.8 %all-to-all-done.4.gathered = f32[32,1,128]{2,1,0:T(1,128)S(1)} async-done(((f32[32,1,128]{2,1,0:T(1,128)}), f32[32,1,128]{2,1,0:T(1,128)S(1)}, u32[]{:S(2)}, u32[]{:S(2)}) %all-to-all-start.4) | async-done | bytes 16416 | tf_op jit(solution)/shard_map/all_to_all | solution.py:678
  112.0 1.3 %mix.1 = f32[2,2,2,128,128]{4,3,2,1,0:T(8,128)} custom-call(f32[32,1,128]{2,1,0:T(1,128)S(1)} %all-to-all-done.4.gathered, f32[2,2,2,128,128]{4,3,2,1,0:T(8,128)S(1)} %get-tuple-element.41.first, f32[2,2,2,128,128]{4,3,2,1,0:T(8,128)S(1)} %get-tuple-element.42.second), custom_call_target="tpu_custom_call" | custom-call | flops 1048576 | bytes 4194304 | tf_op jit(solution)/shard_map/mix/pallas_call | solution.py:665
  (1 shorter events, 0.0 us)
Async XLA Ops:
  2.6 25.9 %all-to-all-start = ((bf16[32,4,16,128]{3,2,1,0:T(8,128)(2,1)}), bf16[32,4,16,128]{3,2,1,0:T(8,128)(2,1)S(1)}, u32[]{:S(2)}, u32[]{:S(2)}) async-start(bf16[32,4,16,128]{3,2,1,0:T(8,128)(2,1)} %bitcast.23), calls=%async_computation | async-start | bytes 1048576 | tf_op jit(solution)/shard_map/all_to_all | solution.py:678
  28.5 6.0 %copy-start.5 = (bf16[32,4,16,128]{3,2,1,0:T(8,128)(2,1)}, bf16[32,4,16,128]{3,2,1,0:T(8,128)(2,1)S(1)}, u32[]{:S(2)}) copy-start(bf16[32,4,16,128]{3,2,1,0:T(8,128)(2,1)S(1)} %all-to-all-done) | copy-start | bytes 1572868
  28.5 31.1 %all-to-all-start.2 = ((bf16[32,4,8,128]{3,2,1,0:T(8,128)(2,1)}), bf16[32,4,8,128]{3,2,1,0:T(8,128)(2,1)S(1)}, u32[]{:S(2)}, u32[]{:S(2)}) async-start(bf16[32,4,8,128]{3,2,1,0:T(8,128)(2,1)} %bitcast.26), calls=%async_computation.2 | async-start | bytes 524288 | tf_op jit(solution)/shard_map/all_to_all | solution.py:678
  59.7 5.7 %copy-start.6 = (bf16[32,4,8,128]{3,2,1,0:T(8,128)(2,1)}, bf16[32,4,8,128]{3,2,1,0:T(8,128)(2,1)S(1)}, u32[]{:S(2)}) copy-start(bf16[32,4,8,128]{3,2,1,0:T(8,128)(2,1)S(1)} %all-to-all-done.2) | copy-start | bytes 786436
  59.7 20.1 %all-to-all-start.1 = ((bf16[32,4,8,128]{3,2,1,0:T(8,128)(2,1)}), bf16[32,4,8,128]{3,2,1,0:T(8,128)(2,1)S(1)}, u32[]{:S(2)}, u32[]{:S(2)}) async-start(bf16[32,4,8,128]{3,2,1,0:T(8,128)(2,1)} %bitcast.27), calls=%async_computation.1 | async-start | bytes 524288 | tf_op jit(solution)/shard_map/all_to_all | solution.py:678
  65.4 20.5 %copy-start = (f32[2,2,2,128,128]{4,3,2,1,0:T(8,128)S(1)}, f32[2,2,2,128,128]{4,3,2,1,0:T(8,128)}, u32[]{:S(2)}) copy-start(f32[2,2,2,128,128]{4,3,2,1,0:T(8,128)} %get-tuple-element.24.cotangent) | copy-start | bytes 1572868
  65.4 20.5 %copy-start.1 = (s32[2,8,128,128]{3,2,1,0:T(8,128)S(1)}, s32[2,8,128,128]{3,2,1,0:T(8,128)}, u32[]{:S(2)}) copy-start(s32[2,8,128,128]{3,2,1,0:T(8,128)} %mask.3) | copy-start | bytes 3145732
  65.4 20.5 %copy-start.2 = (bf16[768,256]{1,0:T(8,128)(2,1)S(1)}, bf16[768,256]{1,0:T(8,128)(2,1)}, u32[]{:S(2)}) copy-start(bf16[768,256]{1,0:T(8,128)(2,1)} %constant.14.clone.forward_y.forward_z) | copy-start | bytes 1179652
  79.8 18.4 %all-to-all-start.3 = ((bf16[32,4,8,128]{3,2,1,0:T(8,128)(2,1)}), bf16[32,4,8,128]{3,2,1,0:T(8,128)(2,1)S(1)}, u32[]{:S(2)}, u32[]{:S(2)}) async-start(bf16[32,4,8,128]{3,2,1,0:T(8,128)(2,1)} %bitcast.25), calls=%async_computation.3 | async-start | bytes 524288 | tf_op jit(solution)/shard_map/all_to_all | solution.py:678
  85.9 1.0 copy-start.3
  86.9 1.0 copy-start.4
  99.2 12.8 %all-to-all-start.4 = ((f32[32,1,128]{2,1,0:T(1,128)}), f32[32,1,128]{2,1,0:T(1,128)S(1)}, u32[]{:S(2)}, u32[]{:S(2)}) async-start(f32[32,1,128]{2,1,0:T(1,128)} %gram.1), calls=%async_computation.4 | async-start | bytes 32768 | tf_op jit(solution)/shard_map/all_to_all | solution.py:678
